TPU v7x, 32 devices: a whole 2x2x4 slice. The times are simulated.
32 devices in a mesh: shard: 4 (over y, x), replica: 8 (over z, core).
Axes of the slice: x: 2, y: 2, z: 4, core: 2. Of those that a mesh axis runs over, the one named last changes fastest.
Arguments:
- series: bfloat16 [128, 16384], P(('shard', 'replica')), may hold values from -6 to 6
- mask: int32 [128, 256], P(('shard', 'replica')), may hold values from 0 to 1, as said below
- qkv_w: float32 [2, 512, 1536], P(None, 'shard'), may hold values from -0.25 to 0.25
- out_w: float32 [2, 512, 512], P(None, 'shard'), may hold values from -1 to 1
- up_w: float32 [2, 512, 2048], P(None, 'shard'), may hold values from -0.25 to 0.25
- down_w: float32 [2, 2048, 512], P(None, 'shard'), may hold values from -0.125 to 0.125
- patch_maps: float32 [384, 512], P(None, 'shard')
- norm_params: float32 [10, 512], P(None, 'shard')
- qkv_m: float32 [2, 512, 1536], P(None, 'shard'), may hold values from -5.9604645e-07 to 5.9604645e-07
- out_m: float32 [2, 512, 512], P(None, 'shard'), may hold values from -5.9604645e-07 to 5.9604645e-07
- up_m: float32 [2, 512, 2048], P(None, 'shard'), may hold values from -5.9604645e-07 to 5.9604645e-07
- down_m: float32 [2, 2048, 512], P(None, 'shard'), may hold values from -5.9604645e-07 to 5.9604645e-07
- patch_m: float32 [384, 512], P(None, 'shard'), may hold values from -5.9604645e-07 to 5.9604645e-07
- norm_m: float32 [10, 512], P(None, 'shard'), may hold values from -3.33786e-06 to 3.33786e-06
- qkv_v: float32 [2, 512, 1536], P(None, 'shard'), may hold values from 7.7003825e-17 to 1.2320612e-15
- out_v: float32 [2, 512, 512], P(None, 'shard'), may hold values from 7.7003825e-17 to 1.2320612e-15
- up_v: float32 [2, 512, 2048], P(None, 'shard'), may hold values from 7.7003825e-17 to 1.2320612e-15
- down_v: float32 [2, 2048, 512], P(None, 'shard'), may hold values from 7.7003825e-17 to 1.2320612e-15
- patch_v: float32 [384, 512], P(None, 'shard'), may hold values from 7.7003825e-17 to 1.2320612e-15
- norm_v: float32 [10, 512], P(None, 'shard'), may hold values from 1.9250956e-15 to 3.080153e-14
Outputs:
- loss: float32 [], replicated
- grad_norm: float32 [], replicated
- qkv_new: float32 [2, 512, 1536], P(None, 'shard')
- out_new: float32 [2, 512, 512], P(None, 'shard')
- up_new: float32 [2, 512, 2048], P(None, 'shard')
- down_new: float32 [2, 2048, 512], P(None, 'shard')
- patch_new: float32 [384, 512], P(None, 'shard')
- norm_new: float32 [10, 512], P(None, 'shard')
- qkv_m_new: float32 [2, 512, 1536], P(None, 'shard')
- out_m_new: float32 [2, 512, 512], P(None, 'shard')
- up_m_new: float32 [2, 512, 2048], P(None, 'shard')
- down_m_new: float32 [2, 2048, 512], P(None, 'shard')
- patch_m_new: float32 [384, 512], P(None, 'shard')
- norm_m_new: float32 [10, 512], P(None, 'shard')
- qkv_v_new: float32 [2, 512, 1536], P(None, 'shard')
- out_v_new: float32 [2, 512, 512], P(None, 'shard')
- up_v_new: float32 [2, 512, 2048], P(None, 'shard')
- down_v_new: float32 [2, 2048, 512], P(None, 'shard')
- patch_v_new: float32 [384, 512], P(None, 'shard')
- norm_v_new: float32 [10, 512], P(None, 'shard')
Inputs may be any that keep to these rules, and one draw needn't show every extreme that they name: `mask`: each series has exactly 102 masked patches.
All inputs are finite; a program needn't handle non-finite values.
Results may differ from a plain program's by a relative error of at most 0.02.
Values may be sent and summed in bfloat16 or wider, within the bound.
No kernel may reach another device: no remote copies, remote signals or barrier semaphores. Data moves between devices by JAX's collectives and lax.ppermute only.
A program may use at most 256 MiB of HBM per device.

v0:
```python
import jax
import jax.numpy as jnp
from jax import lax
from jax.experimental import pallas as pl
from jax.experimental.pallas import tpu as pltpu
from jax.sharding import PartitionSpec as P

D = 512
H = 8
DH = 64
FF = 2048
P_SIZE = 64
LEN = 256
L = 2
MASKED = 102

EPS = 1e-05
CLIP = 0.001
RATE = 0.05
TABLE_RATE = 0.3
BETA_ONE = 0.9
BETA_TWO = 0.999
ADAM_EPS = 1e-08
DECAY = 0.1
STEP_COUNT = 10

W = 512
SMALL = 512
NORMS_LOW = 2 * P_SIZE + LEN + 16
F32 = jnp.float32
BF16 = jnp.bfloat16


def dense(left, right):
    return jnp.dot(left, right, preferred_element_type=F32)


def dense_tn(left, right):
    return lax.dot_general(left, right, (((0,), (0,)), ((), ())), preferred_element_type=F32)


def dense_nt(left, right):
    return lax.dot_general(left, right, (((1,), (1,)), ((), ())), preferred_element_type=F32)


def layer_norm(x, gain, bias):
    center = x - jnp.mean(x, -1, keepdims=True)
    spread = jnp.mean(center * center, -1, keepdims=True)
    return center * lax.rsqrt(spread + EPS) * gain + bias


def params(**more):
    return pltpu.CompilerParams(vmem_limit_bytes=30 * 2**20, **more)


def cost(flops, data, trans=0):
    return pl.CostEstimate(flops=int(flops), bytes_accessed=int(data), transcendentals=int(trans))


def whole(shape):
    return pl.BlockSpec(shape, lambda *_: (0,) * len(shape))


def in_hbm(x):
    return pltpu.with_memory_space_constraint(x, pltpu.HBM)


ANY = pl.BlockSpec(memory_space=pl.ANY)
SMEM = pl.BlockSpec(memory_space=pltpu.SMEM)


def permute(x, axis, mask, size):
    return lax.ppermute(x, axis, [(i, i ^ mask) for i in range(size)])


def pick(x, index):
    return lax.dynamic_index_in_dim(x, index, 0, keepdims=False)


class Place:
    def __init__(self):
        self.shards = lax.axis_size("shard")
        self.replicas = lax.axis_size("replica")
        self.chips = self.replicas // 2
        self.shard = lax.axis_index("shard")
        replica = lax.axis_index("replica")
        self.core = replica % 2
        self.chip = replica // 2

    def to_core(self, x):
        return permute(x, "replica", 1, self.replicas)

    def to_shard(self, x, mask):
        return permute(x, "shard", mask, self.shards)

    def to_chip(self, x, mask):
        return permute(x, "replica", 2 * mask, self.replicas)


def gate(x, *after):
    return lax.optimization_barrier((x,) + after)[0]


def gather_shards(place, mine):
    return [place.to_shard(mine, mask) for mask in range(1, place.shards)]


def gather_cores(place, ours, *after):
    return place.to_core(jnp.stack(gates(ours, *after)))


def gates(items, *after):
    return list(lax.optimization_barrier(tuple(items) + after)[: len(items)])


def bits_of(size):
    return list(range(size.bit_length() - 1))


def total_of(values):
    total = values[0].astype(F32)
    for value in values[1:]:
        total = total + value.astype(F32)
    return total


def combine(where, jobs, name):
    lanes = W // 2
    arrays, leads, plans, shapes = [], [], [], []

    def number(array, lead):
        for n, known in enumerate(arrays):
            if known is array:
                return n
        arrays.append(array)
        leads.append(lead)
        return len(arrays) - 1

    for segments, lead, cut, bit in jobs:
        plans.append([[(number(a, lead), f, b) for a, f, b in parts] for parts in segments])
        blocks = sum(parts[0][2] for parts in segments)
        rows = segments[0][0][0].shape[-2]
        if cut is None:
            shapes.append(lead + (blocks, rows, W))
        elif cut == "rows":
            shapes += [lead + (blocks, rows // 2, W)] * 2
        else:
            shapes += [lead[:cut] + lead[cut + 1 :] + (blocks, rows, W)] * 2
    arrays = [a.reshape(lead + a.shape[-3:]) for a, lead in zip(arrays, leads)]

    def block(shape):
        zeros = (0,) * (len(shape) - 1)
        return pl.BlockSpec(shape[:-1] + (lanes,), lambda i: zeros + (i,))

    def kernel(where_ref, *refs):
        ins, outs = refs[: len(arrays)], list(refs[len(arrays) :])
        for (segments, lead, cut, bit), plan in zip(jobs, plans):
            some = (slice(None),) * len(lead)
            fewer = (slice(None),) * (len(lead) - (cut is not None and cut != "rows"))
            if cut is None:
                targets = [(outs.pop(0), None)]
            else:
                value = where_ref[bit]
                targets = [(outs.pop(0), 1 - value), (outs.pop(0), value)]
            for out_ref, at in targets:
                start = 0
                for parts in plan:
                    got = []
                    for n, f, b in parts:
                        index = some
                        if cut is not None and cut != "rows":
                            index = some[:cut] + (at,) + some[cut + 1 :]
                        index += (slice(f, f + b),)
                        if cut == "rows":
                            few = ins[n].shape[-2] // 2
                            index += (pl.ds(pl.multiple_of(at * few, few), few),)
                        got.append(ins[n][index])
                    out_ref[fewer + (slice(start, start + parts[0][2]),)] = total_of(got).astype(BF16)
                    start += parts[0][2]

    size = sum(a.size for a in arrays) * 4
    return pl.pallas_call(
        kernel,
        grid=(2,),
        in_specs=[SMEM] + [block(a.shape) for a in arrays],
        out_specs=[block(s) for s in shapes],
        out_shape=[jax.ShapeDtypeStruct(s, BF16) for s in shapes],
        compiler_params=params(),
        cost_estimate=cost(size, size),
        name=name,
    )(where, *arrays)


class Flow:
    def __init__(self, place, spread):
        self.place, self.spread = place, spread
        self.bits = bits_of(place.shards)
        self.steps = len(self.bits) + len(bits_of(place.chips))
        self.step = 0
        self.inputs = []
        self.ranges = []

    def begin(self, send, keep, *ranges):
        other = self.place.to_core(send)
        for first, blocks, order in ranges:
            self.ranges.append((len(self.inputs), first, blocks, order))
        self.inputs += [keep, other]
        self.left = [list(reversed(self.bits)) for _ in self.ranges]
        return send

    def last(self):
        return self.step == self.steps

    def plan(self, flat):
        if self.step == 0:
            parts = [[(flat[n], f, b), (flat[n + 1], f, b)] for n, f, b, _ in self.ranges]
        else:
            parts = [
                [(x, 0, x.shape[-3]) for x in flat[2 * n : 2 * n + 2]]
                for n in range(len(flat) // 2)
            ]
        if self.step >= len(self.bits):
            cut = self.spread and self.step == len(self.bits)
            return [(parts, (), "rows", 2 + len(self.bits)) if cut else (parts, (), None, 0)]
        jobs, self.chosen = [], []
        for n, (_, _, _, order) in enumerate(self.ranges):
            bit = (self.bits if order == 0 else self.bits[::-1])[self.step]
            jobs.append(([parts[n]], (2,) * len(self.left[n]), self.left[n].index(bit), 2 + bit))
            self.left[n].remove(bit)
            self.chosen.append(bit)
        return jobs

    def take(self, out):
        if self.step < len(self.bits):
            self.sends, self.stays = out[0::2], out[1::2]
        else:
            self.sends, self.stays = out[:1], out[-1:]
        return self.sends[0]

    def launch(self):
        place = self.place
        if self.step < len(self.bits):
            got = [place.to_shard(x, 1 << bit) for x, bit in zip(self.sends, self.chosen)]
        else:
            got = [place.to_chip(x, 1 << (self.step - len(self.bits))) for x in self.sends]
        self.inputs = [x for pair in zip(self.stays, got) for x in pair]
        self.step += 1

    def to_neighbours(self):
        self.pieces = [self.sends[0], self.place.to_core(self.sends[0])]
        if self.spread:
            self.pieces.append(self.place.to_chip(self.sends[0], 1))

    def to_last(self):
        if self.spread:
            self.pieces.append(self.place.to_core(self.pieces[2]))


def sum_round(where, flows, *after):
    flat = gates([x for flow in flows for x in flow.inputs], *after)
    jobs, counts = [], []
    for flow in flows:
        few = len(flow.inputs)
        some = flow.plan(flat[:few])
        flat = flat[few:]
        jobs += some
        counts.append(sum(1 if cut is None else 2 for _, _, cut, _ in some))
    out = combine(where, jobs, "sum_round")
    for flow, count in zip(flows, counts):
        token = flow.take(out[:count])
        out = out[count:]
    return token


def square_sum(pieces):
    def kernel(*refs):
        total = jnp.zeros((1, W), F32)
        for ref in refs[:-1]:
            for b in range(ref.shape[0]):
                x = ref[b].astype(F32)
                total = total + jnp.sum(x * x, 0, keepdims=True)
        refs[-1][...] = jnp.sum(total, 1, keepdims=True)

    return pl.pallas_call(
        kernel,
        grid=(1,),
        in_specs=[whole(p.shape) for p in pieces],
        out_specs=whole((1, 1)),
        out_shape=jax.ShapeDtypeStruct((1, 1), F32),
        compiler_params=params(),
        name="square_sum",
    )(*pieces)


def fill_weights(step, where_ref, sources, targets, sem):
    shard, core = where_ref[0], where_ref[1]
    count = len(sources) - 2

    @pl.when(step == 0)
    def _():
        made = targets(sources[0], shard, None)
        for k in range(count):
            made += targets(sources[1 + k], shard ^ (k + 1), core)
            made += targets(sources[-1].at[k], shard ^ (k + 1), 1 - core)
        todo = [pltpu.make_async_copy(s, t, sem.at[n]) for n, (s, t) in enumerate(made)]
        for copy in todo:
            copy.start()
        for copy in todo:
            copy.wait()


def attn_targets(w_ref, rows):
    def targets(piece, at, half):
        if half is None:
            return [(piece.at[pl.ds(0, 4)], w_ref.at[:, pl.ds(pl.multiple_of(at * rows, rows), rows)])]
        start = pl.multiple_of(at * rows + half * (rows // 2), rows // 2)
        return [(piece.at[pl.ds(0, 4)], w_ref.at[:, pl.ds(start, rows // 2)])]

    return targets


def mlp_targets(up_ref, down_ref, rows):
    def targets(piece, at, half):
        few = rows if half is None else rows // 2
        skip = 0 if half is None else half * few
        start = pl.multiple_of(at * rows + skip, few)
        skip = pl.multiple_of(skip, few) if half is not None else 0
        return [
            (piece.at[pl.ds(0, 4)], up_ref.at[:, pl.ds(start, few)]),
            (piece.at[pl.ds(4, 4)], down_ref.at[pl.ds(at * 4, 4), pl.ds(skip, few)]),
        ]

    return targets


def pack(place, where, index, tall, wide, small):
    rows = D // place.shards
    half = rows // 2
    wide = [x.reshape(L, 4, rows, W) for x in wide]
    total = sum(x.shape[2] // W for x in tall) + 4 * len(wide) + bool(small)
    count = len(tall) + len(wide)

    def kernel(where_ref, *refs):
        full_ref, mine_ref = refs[count + len(small) : count + len(small) + 2]

        def run(core):
            own = slice(core * half, core * half + half)
            at = 0
            for ref in refs[: len(tall)]:
                for b in range(ref.shape[1] // W):
                    block = ref[:, W * b : W * b + W].astype(BF16)
                    full_ref[at] = block
                    mine_ref[at] = block[own]
                    at += 1
            for ref in refs[len(tall) : count]:
                for b in range(4):
                    block = ref[b].astype(BF16)
                    full_ref[at] = block
                    mine_ref[at] = block[own]
                    at += 1
            if small:
                table_ref = refs[-1]
                start = 0
                for ref in refs[count : count + len(small)]:
                    table_ref[start : start + ref.shape[0]] = ref[...]
                    start += ref.shape[0]
                table_ref[start:] = jnp.zeros((SMALL - start, rows), F32)
                norms = refs[count + 1][...]
                left = norms - norms.astype(BF16).astype(F32)
                table_ref[NORMS_LOW : NORMS_LOW + norms.shape[0]] = left
                for h in range(2):
                    for q in range(W // rows):
                        first = h * (SMALL // 2) + q * half
                        value = table_ref[first : first + half, :].astype(BF16)
                        spot = slice(q * rows, q * rows + rows)
                        full_ref[at, h * half : h * half + half, spot] = value
                        if h == core:
                            mine_ref[at, :, spot] = value

        for core in range(2):

            @pl.when(where_ref[1] == core)
            def _(core=core):
                run(core)

    return pl.pallas_call(
        kernel,
        grid=(1,),
        in_specs=[SMEM]
        + [pl.BlockSpec((None, rows, x.shape[2]), lambda i: (index, 0, 0)) for x in tall]
        + [pl.BlockSpec((None, 4, rows, W), lambda i: (index, 0, 0, 0)) for x in wide]
        + [whole(x.shape) for x in small],
        out_specs=[whole((total, rows, W)), whole((total, half, W))],
        out_shape=[
            pltpu.HBM((total, rows, W), BF16),
            pltpu.HBM((total, half, W), BF16),
        ],
        scratch_shapes=[pltpu.VMEM((SMALL, rows), F32)] * bool(small),
        compiler_params=params(),
        cost_estimate=cost(total * rows * W, total * rows * W * 7),
        name="pack",
    )(where, *map(in_hbm, tall), *map(in_hbm, wide), *map(in_hbm, small))


def embed_step(place, where, target, maskf, group):
    shards = place.shards
    rows = D // shards
    half = rows // 2
    n = target.shape[0]
    sources = len(group)

    def kernel(where_ref, target_ref, mask_ref, *refs):
        pieces, refs = refs[:sources], refs[sources:]
        x_ref, inputs_ref, head_ref, norm_ref, got_ref, table_ref, sem = refs

        def targets(piece, at, part):
            start = 0 if part is None else pl.multiple_of(part * half, half)
            few = rows if part is None else half
            return [(piece.at[4], got_ref.at[at, pl.ds(start, few)])]

        fill_weights(0, where_ref, pieces, targets, sem)
        for j in range(shards):
            for h in range(2):
                for q in range(W // rows):
                    spot = slice(q * rows, q * rows + rows)
                    part = slice(h * half, h * half + half)
                    value = got_ref[j, part, spot].astype(F32)
                    first = h * (SMALL // 2) + q * half
                    table_ref[first : first + half, j * rows : j * rows + rows] = value
        inputs = jnp.where(mask_ref[...] > 0, 0.0, target_ref[...].astype(F32)).astype(BF16)
        inputs_ref[...] = inputs
        embed = table_ref[:P_SIZE].astype(BF16)
        for s in range(n // LEN):
            part = slice(s * LEN, s * LEN + LEN)
            x_ref[part] = dense(inputs[part], embed) + table_ref[2 * P_SIZE : 2 * P_SIZE + LEN]
        head_ref[...] = table_ref[P_SIZE : 2 * P_SIZE].astype(BF16)
        low = table_ref[NORMS_LOW : NORMS_LOW + 16]
        norm_ref[...] = table_ref[NORMS_LOW - 16 : NORMS_LOW] + low

    return pl.pallas_call(
        kernel,
        grid=(1,),
        in_specs=[SMEM, whole((n, P_SIZE)), whole((n, 1))] + [ANY] * sources,
        out_specs=[whole((n, D)), whole((n, P_SIZE)), whole((P_SIZE, D)), whole((16, D))],
        out_shape=[
            jax.ShapeDtypeStruct((n, D), F32),
            jax.ShapeDtypeStruct((n, P_SIZE), BF16),
            jax.ShapeDtypeStruct((P_SIZE, D), BF16),
            jax.ShapeDtypeStruct((16, D), F32),
        ],
        scratch_shapes=[
            pltpu.VMEM((shards, rows, W), BF16),
            pltpu.VMEM((SMALL, D), F32),
            pltpu.SemaphoreType.DMA((copies_of(group),)),
        ],
        compiler_params=params(),
        cost_estimate=cost(2 * n * D * P_SIZE, n * D * 5),
        name="embed_step",
    )(where, target, maskf, *group)


def copies_of(group):
    return 2 * (2 * (len(group) - 2) + 1)


def norm_parts(x):
    center = x - jnp.mean(x, -1, keepdims=True)
    rstd = lax.rsqrt(jnp.mean(center * center, -1, keepdims=True) + EPS)
    return center * rstd, rstd


def norm_back(xhat, rstd, dy, gain):
    dxh = dy * gain
    return rstd * (
        dxh - jnp.mean(dxh, -1, keepdims=True) - xhat * jnp.mean(dxh * xhat, -1, keepdims=True)
    )


def head_lanes(x, h):
    lane = lax.broadcasted_iota(jnp.int32, (x.shape[0], 128), 1)
    own = (lane < DH) if h % 2 == 0 else (lane >= DH)
    return jnp.where(own, x[:, pair_of(h)], 0)


def pair_of(h):
    return slice(128 * (h // 2), 128 * (h // 2) + 128)


def head_of(h):
    return slice(DH * h, DH * h + DH)


SP = 1


def attn_fwd(place, where, x, norms, group):
    rows = D // place.shards
    n = x.shape[0]
    seqs = n // LEN
    sources = len(group)

    def kernel(where_ref, x_ref, norm_ref, *refs):
        pieces, refs = refs[:sources], refs[sources:]
        mid_ref, qkv_ref, pt_ref, ot_ref, w_ref, sem = refs
        fill_weights(pl.program_id(0), where_ref, pieces, attn_targets(w_ref, rows), sem)
        spans = [slice(LEN * s, LEN * s + LEN) for s in range(SP)]
        a, q, k, vt = [], [], [], []
        for s, span in enumerate(spans):
            xhat, _ = norm_parts(x_ref[span])
            a.append((xhat * norm_ref[0:1, :] + norm_ref[1:2, :]).astype(BF16))
            q.append((dense(a[s], w_ref[0]) * DH**-0.5).astype(BF16))
            k.append(dense(a[s], w_ref[1]).astype(BF16))
            qkv_ref[span, :D] = q[s]
            qkv_ref[span, D : 2 * D] = k[s]

        def scores(s, h):
            return dense_nt(k[s][:, pair_of(h)], head_lanes(q[s], h))

        def gather_values(s, h, p):
            ot_ref[s, head_of(h), :] = dense(vt[s][head_of(h), :], p).astype(BF16)

        items = [(s, h) for h in range(H) for s in range(SP)]
        ahead = scores(*items[0])
        for s, span in enumerate(spans):
            v = dense(a[s], w_ref[2]).astype(BF16)
            qkv_ref[span, 2 * D :] = v
            vt.append(v.T)
        last = None
        for at, (s, h) in enumerate(items):
            st = ahead
            if at + 1 < len(items):
                ahead = scores(*items[at + 1])
            if last is not None:
                gather_values(*last)
            e = jnp.exp(st - jnp.max(st, axis=0, keepdims=True))
            p = (e * (1.0 / jnp.sum(e, axis=0, keepdims=True))).astype(BF16)
            pt_ref[s, h] = p
            last = (s, h, p)
        gather_values(*last)
        for s, span in enumerate(spans):
            mid_ref[span] = x_ref[span] + dense_tn(ot_ref[s], w_ref[3])

    return pl.pallas_call(
        kernel,
        grid=(seqs // SP,),
        in_specs=[SMEM, pl.BlockSpec((SP * LEN, D), lambda i: (i, 0)), whole((4, D))]
        + [ANY] * sources,
        out_specs=[
            pl.BlockSpec((SP * LEN, D), lambda i: (i, 0)),
            pl.BlockSpec((SP * LEN, 3 * D), lambda i: (i, 0)),
            pl.BlockSpec((SP, H, LEN, LEN), lambda i: (i, 0, 0, 0)),
            pl.BlockSpec((SP, D, LEN), lambda i: (i, 0, 0)),
        ],
        out_shape=[
            jax.ShapeDtypeStruct((n, D), F32),
            pltpu.HBM((n, 3 * D), BF16),
            pltpu.HBM((seqs, H, LEN, LEN), BF16),
            pltpu.HBM((seqs, D, LEN), BF16),
        ],
        scratch_shapes=[
            pltpu.VMEM((4, D, W), BF16),
            pltpu.SemaphoreType.DMA((copies_of(group),)),
        ],
        compiler_params=params(),
        cost_estimate=cost(2 * n * D * (4 * D + 2 * LEN), n * D * 20, n * H * LEN),
        name="attn_fwd",
    )(where, x, norms, *group)


def gelu_pair(u):
    cdf = 0.5 * lax.erf(u * 0.7071067811865476) + 0.5
    density = jnp.exp(u * u * -0.5) * 0.3989422804014327
    return u * cdf, cdf + u * density


def mlp_fwd(place, where, mid, norms, group):
    rows = D // place.shards
    n = mid.shape[0]
    tall = LEN
    step = W // 2
    sources = len(group)
    per = W // rows

    def kernel(where_ref, mid_ref, norm_ref, *refs):
        pieces, refs = refs[:sources], refs[sources:]
        out_ref, act_ref, gp_ref, up_ref, down_ref, sem = refs
        fill_weights(pl.program_id(0), where_ref, pieces, mlp_targets(up_ref, down_ref, rows), sem)
        mid = mid_ref[...]
        xhat, _ = norm_parts(mid)
        c = (xhat * norm_ref[2:3, :] + norm_ref[3:4, :]).astype(BF16)
        total = mid

        def upper(b):
            cols = slice(step * (b % 2), step * (b % 2) + step)
            return dense(c, up_ref[b // 2, :, cols])

        def lower(act, b):
            few = per // 2
            return dense(act, down_ref[few * b : few * b + few].reshape(step, D))

        ahead = upper(0)
        for b in range(FF // step):
            cols = slice(step * b, step * b + step)
            u = ahead
            if b + 1 < FF // step:
                ahead = upper(b + 1)
            if b > 0:
                total = total + lower(last, b - 1)
            act, slope = gelu_pair(u)
            last = act.astype(BF16)
            act_ref[:, cols] = last
            gp_ref[:, cols] = slope.astype(BF16)
        out_ref[...] = total + lower(last, FF // step - 1)

    def row(width):
        return pl.BlockSpec((tall, width), lambda i: (i, 0))

    return pl.pallas_call(
        kernel,
        grid=(n // tall,),
        in_specs=[SMEM, row(D), whole((4, D))] + [ANY] * sources,
        out_specs=[row(D), row(FF), row(FF)],
        out_shape=[
            jax.ShapeDtypeStruct((n, D), F32),
            pltpu.HBM((n, FF), BF16),
            pltpu.HBM((n, FF), BF16),
        ],
        scratch_shapes=[
            pltpu.VMEM((4, D, W), BF16),
            pltpu.VMEM((FF // rows, rows, D), BF16),
            pltpu.SemaphoreType.DMA((copies_of(group),)),
        ],
        compiler_params=params(),
        cost_estimate=cost(4 * n * D * FF, n * D * 24, n * FF * 2),
        name="mlp_fwd",
    )(where, mid, norms, *group)


def mlp_bwd(place, where, dz, mid, gp, norms, group):
    rows = D // place.shards
    n = mid.shape[0]
    sources = len(group)
    per = W // rows

    def kernel(where_ref, dz_ref, mid_ref, gp_ref, norm_ref, *refs):
        pieces, refs = refs[:sources], refs[sources:]
        dmid_ref, dh_ref, du_ref, c_ref, dm_ref, dn_ref, up_ref, down_ref, sem = refs
        i = pl.program_id(0)
        fill_weights(i, where_ref, pieces, mlp_targets(up_ref, down_ref, rows), sem)
        dm = dz_ref[...].astype(BF16)
        dm_ref[...] = dm

        def upper(b):
            return dense_nt(dm, down_ref[per * b : per * b + per].reshape(W, D))

        dc = jnp.zeros((LEN, D), F32)
        ahead = upper(0)
        for b in range(FF // W):
            cols = slice(W * b, W * b + W)
            da = ahead
            if b + 1 < FF // W:
                ahead = upper(b + 1)
            if b > 0:
                dc = dc + dense_nt(last, up_ref[b - 1])
            last = (gp_ref[:, cols].astype(F32) * da).astype(BF16)
            du_ref[:, cols] = last
        dc = dc + dense_nt(last, up_ref[FF // W - 1])
        xhat, rstd = norm_parts(mid_ref[...])
        gain = norm_ref[2:3, :]
        c_ref[...] = (xhat * gain + norm_ref[3:4, :]).astype(BF16)
        dmid = dz_ref[...] + norm_back(xhat, rstd, dc, gain)
        dmid_ref[...] = dmid
        dh_ref[...] = dmid.astype(BF16)

        @pl.when(i == 0)
        def _():
            dn_ref[...] = jnp.zeros_like(dn_ref)

        dn_ref[0:1, :] += jnp.sum(dc * xhat, 0, keepdims=True)
        dn_ref[1:2, :] += jnp.sum(dc, 0, keepdims=True)

    def row(width):
        return pl.BlockSpec((LEN, width), lambda i: (i, 0))

    return pl.pallas_call(
        kernel,
        grid=(n // LEN,),
        in_specs=[SMEM, row(D), row(D), row(FF), whole((4, D))] + [ANY] * sources,
        out_specs=[row(D), row(D), row(FF), row(D), row(D), whole((8, D))],
        out_shape=[
            jax.ShapeDtypeStruct((n, D), F32),
            jax.ShapeDtypeStruct((n, D), BF16),
            jax.ShapeDtypeStruct((n, FF), BF16),
            jax.ShapeDtypeStruct((n, D), BF16),
            jax.ShapeDtypeStruct((n, D), BF16),
            jax.ShapeDtypeStruct((8, D), F32),
        ],
        scratch_shapes=[
            pltpu.VMEM((4, D, W), BF16),
            pltpu.VMEM((FF // rows, rows, D), BF16),
            pltpu.SemaphoreType.DMA((copies_of(group),)),
        ],
        compiler_params=params(),
        cost_estimate=cost(4 * n * D * FF, n * D * 32),
        name="mlp_bwd",
    )(where, dz, mid, in_hbm(gp), norms, *group)


def attn_bwd(place, where, dmid, dh, x, qkv, pt, ot, norms, group):
    rows = D // place.shards
    n = x.shape[0]
    seqs = n // LEN
    sources = len(group)

    def kernel(where_ref, dmid_ref, dh_ref, x_ref, qkv_ref, pt_ref, ot_ref, norm_ref, *refs):
        pieces, refs = refs[:sources], refs[sources:]
        dx_ref, dqkv_ref, a_ref, dn_ref, w_ref, dqt_ref, sem = refs
        i = pl.program_id(0)
        fill_weights(i, where_ref, pieces, attn_targets(w_ref, rows), sem)
        spans = [slice(None)]
        do, delta, kt = [], [], []
        for s, span in enumerate(spans):
            do.append(dense_nt(dh_ref[span], w_ref[3]).astype(BF16))
            along = do[s].T.astype(F32) * ot_ref[s].astype(F32)
            delta.append([jnp.sum(along[head_of(h), :], axis=0, keepdims=True) for h in range(H)])
            kt.append(qkv_ref[span, D : 2 * D].T)

        def first(s, h):
            doh = head_lanes(do[s], h)
            v = qkv_ref[spans[s], 2 * D + 128 * (h // 2) : 2 * D + 128 * (h // 2) + 128]
            return dense_nt(v, doh), dense(pt_ref[s, h], doh)

        halves = {}

        def second(s, h, dst, dv):
            q = qkv_ref[spans[s], pair_of(h)]
            lane = lax.broadcasted_iota(jnp.int32, (LEN, 128), 1)
            own = (lane < DH) if h % 2 == 0 else (lane >= DH)
            dk = dense(dst, jnp.where(own, q, 0))
            dqt_ref[s, head_of(h), :] = (dense(kt[s][head_of(h), :], dst) * DH**-0.5).astype(BF16)
            if h % 2 == 0:
                halves[s] = (dk, dv)
                return
            at = 128 * (h // 2)
            dk, dv = dk + halves[s][0], dv + halves[s][1]
            dqkv_ref[spans[s], D + at : D + at + 128] = dk.astype(BF16)
            dqkv_ref[spans[s], 2 * D + at : 2 * D + at + 128] = dv.astype(BF16)

        items = [(s, h) for h in range(H) for s in range(1)]
        ahead = first(*items[0])
        last = None
        for at, (s, h) in enumerate(items):
            dpt, dv = ahead
            if at + 1 < len(items):
                ahead = first(*items[at + 1])
            if last is not None:
                second(*last)
            dst = (pt_ref[s, h].astype(F32) * (dpt - delta[s][h])).astype(BF16)
            last = (s, h, dst, dv)
        second(*last)

        @pl.when(i == 0)
        def _():
            dn_ref[...] = jnp.zeros_like(dn_ref)

        gain = norm_ref[0:1, :]
        for s, span in enumerate(spans):
            da = dense_nt(dqkv_ref[span, D : 2 * D], w_ref[1])
            da = da + dense_nt(dqkv_ref[span, 2 * D :], w_ref[2])
            dq = dqt_ref[s].T
            dqkv_ref[span, :D] = dq
            da = da + dense_nt(dq, w_ref[0])
            xhat, rstd = norm_parts(x_ref[span])
            a_ref[span] = (xhat * gain + norm_ref[1:2, :]).astype(BF16)
            dx_ref[span] = dmid_ref[span] + norm_back(xhat, rstd, da, gain)
            dn_ref[0:1, :] += jnp.sum(da * xhat, 0, keepdims=True)
            dn_ref[1:2, :] += jnp.sum(da, 0, keepdims=True)

    def row(width):
        return pl.BlockSpec((LEN, width), lambda i: (i, 0))

    return pl.pallas_call(
        kernel,
        grid=(seqs,),
        in_specs=[
            SMEM,
            row(D),
            row(D),
            row(D),
            row(3 * D),
            pl.BlockSpec((1, H, LEN, LEN), lambda i: (i, 0, 0, 0)),
            pl.BlockSpec((1, D, LEN), lambda i: (i, 0, 0)),
            whole((4, D)),
        ]
        + [ANY] * sources,
        out_specs=[row(D), row(3 * D), row(D), whole((8, D))],
        out_shape=[
            jax.ShapeDtypeStruct((n, D), F32),
            jax.ShapeDtypeStruct((n, 3 * D), BF16),
            jax.ShapeDtypeStruct((n, D), BF16),
            jax.ShapeDtypeStruct((8, D), F32),
        ],
        scratch_shapes=[
            pltpu.VMEM((4, D, W), BF16),
            pltpu.VMEM((1, D, LEN), BF16),
            pltpu.SemaphoreType.DMA((copies_of(group),)),
        ],
        compiler_params=params(),
        cost_estimate=cost(2 * n * D * (4 * D + 5 * LEN), n * D * 32),
        name="attn_bwd",
    )(where, dmid, dh, x, in_hbm(qkv), in_hbm(pt), in_hbm(ot), norms, *group)


def head_step(place, x, target, maskf, head, norms, count):
    n = x.shape[0]

    def kernel(x_ref, target_ref, mask_ref, head_ref, norm_ref, dx_ref, loss_ref, gh_ref, dn_ref):
        i = pl.program_id(0)
        xhat, rstd = norm_parts(x_ref[...])
        gain = norm_ref[0:1, :]
        y = (xhat * gain + norm_ref[1:2, :]).astype(BF16)
        masked = mask_ref[...]
        err = (dense_nt(y, head_ref[...]) - target_ref[...].astype(F32)) * masked
        dpred = (err * (2.0 / (P_SIZE * count))).astype(BF16)
        dy = dense(dpred, head_ref[...])
        dx_ref[...] = norm_back(xhat, rstd, dy, gain)

        @pl.when(i == 0)
        def _():
            loss_ref[...] = jnp.zeros_like(loss_ref)
            gh_ref[...] = jnp.zeros_like(gh_ref)
            dn_ref[...] = jnp.zeros_like(dn_ref)

        loss_ref[...] += jnp.sum(err * err, 0, keepdims=True)
        gh_ref[...] += dense_tn(dpred, y)
        dn_ref[0:1, :] += jnp.sum(dy * xhat, 0, keepdims=True)
        dn_ref[1:2, :] += jnp.sum(dy, 0, keepdims=True)

    def row(width):
        return pl.BlockSpec((LEN, width), lambda i: (i, 0))

    return pl.pallas_call(
        kernel,
        grid=(n // LEN,),
        in_specs=[row(D), row(P_SIZE), row(1), whole((P_SIZE, D)), whole((2, D))],
        out_specs=[row(D), whole((1, P_SIZE)), whole((P_SIZE, D)), whole((8, D))],
        out_shape=[
            jax.ShapeDtypeStruct((n, D), F32),
            jax.ShapeDtypeStruct((1, P_SIZE), F32),
            jax.ShapeDtypeStruct((P_SIZE, D), F32),
            jax.ShapeDtypeStruct((8, D), F32),
        ],
        compiler_params=params(),
        cost_estimate=cost(6 * n * D * P_SIZE, n * D * 8),
        name="head_step",
    )(x, target, maskf, head, norms)


def put_block(core, block, lead, send_ref, keep_ref, at):
    rows = block.shape[0]
    halves = block.reshape(lead + (2, rows // (2 * lead_size(lead)), W))
    first, second = halves[..., 0, :, :], halves[..., 1, :, :]
    keep_ref[at] = jnp.where(core == 0, first, second)
    send_ref[at] = jnp.where(core == 0, second, first)


def lead_size(lead):
    size = 1
    for n in lead:
        size *= n
    return size


def grad_mlp(place, where, c, du, act, dm, ot, dh):
    shards = place.shards
    rows = D // shards
    n = c.shape[0]
    seqs = n // LEN
    wide = 2 * W
    steps = FF // wide
    per = shards // steps
    blocks = 9

    def kernel(where_ref, c_ref, du_ref, act_ref, dm_ref, ot_ref, dh_ref, send_ref, keep_ref, ct_ref):
        i = pl.program_id(0)
        core = where_ref[1]

        @pl.when(i == 0)
        def _():
            ct_ref[...] = c_ref[...].T

        @pl.when(i < steps)
        def _():
            block = dense(ct_ref[...], du_ref[...]).astype(BF16)
            for b in range(wide // W):
                at = (slice(None), i * (wide // W) + b)
                put_block(core, block[:, W * b : W * b + W], (shards,), send_ref, keep_ref, at)

        @pl.when((i >= steps) & (i < 2 * steps))
        def _():
            block = dense_tn(act_ref[...], dm_ref[...]).astype(BF16)
            at = (pl.ds((i - steps) * per, per), slice(4, 8))
            put_block(core, block, (per, 4), send_ref, keep_ref, at)

        @pl.when(i == 2 * steps)
        def _():
            total = dense(ot_ref[0], dh_ref[:LEN, :])
            for s in range(1, seqs):
                total = total + dense(ot_ref[s], dh_ref[LEN * s : LEN * s + LEN, :])
            put_block(core, total.astype(BF16), (shards,), send_ref, keep_ref, (slice(None), 8))

    shape = (shards, blocks, rows // 2, W)
    return pl.pallas_call(
        kernel,
        grid=(2 * steps + 1,),
        in_specs=[
            SMEM,
            whole((n, D)),
            pl.BlockSpec((n, wide), lambda i: (0, jnp.minimum(i, steps - 1))),
            pl.BlockSpec((n, wide), lambda i: (0, jnp.clip(i - steps, 0, steps - 1))),
            whole((n, D)),
            whole((seqs, D, LEN)),
            whole((n, D)),
        ],
        out_specs=[whole(shape), whole(shape)],
        scratch_shapes=[pltpu.VMEM((D, n), BF16)],
        out_shape=[jax.ShapeDtypeStruct(shape, BF16)] * 2,
        compiler_params=params(),
        cost_estimate=cost(4 * n * D * FF, n * (4 * D + 4 * FF) + 4 * D * FF),
        name="grad_mlp",
    )(where, c, du, in_hbm(act), dm, in_hbm(ot), dh)


def grad_qkv(place, where, a, dqkv, small=()):
    shards = place.shards
    rows = D // shards
    half = rows // 2
    n = a.shape[0]
    blocks = 3 + bool(small)
    extra = len(small)

    def kernel(where_ref, a_ref, dqkv_ref, *refs):
        small_refs, refs = refs[:extra], refs[extra:]
        send_ref, keep_ref, at_ref = refs[:3]
        i = pl.program_id(0)

        @pl.when(i == 0)
        def _():
            at_ref[...] = a_ref[...].T

        @pl.when(i < 3)
        def _():
            block = dense(at_ref[...], dqkv_ref[...]).astype(BF16)
            put_block(where_ref[1], block, (shards,), send_ref, keep_ref, (slice(None), i))

        if extra:
            table_ref = refs[3]
            inputs_ref, dx_ref, head_ref = small_refs[:3]

            @pl.when(i == 3)
            def _():
                dx = dx_ref[...]
                table_ref[:P_SIZE] = dense_tn(inputs_ref[...], dx.astype(BF16)).astype(BF16)
                table_ref[P_SIZE : 2 * P_SIZE] = head_ref[...].astype(BF16)
                total = dx[:LEN]
                for s in range(1, n // LEN):
                    total = total + dx[s * LEN : s * LEN + LEN]
                table_ref[2 * P_SIZE : 2 * P_SIZE + LEN] = total.astype(BF16)
                norms = jnp.concatenate(
                    [ref[0:2, :] for ref in small_refs[3:]]
                    + [jnp.zeros((16 - 2 * (extra - 3), D), F32)],
                    0,
                )
                start = 2 * P_SIZE + LEN
                table_ref[start : start + 16] = norms.astype(BF16)
                table_ref[start + 16 :] = jnp.zeros((SMALL - start - 16, D), BF16)
                for core in range(2):

                    @pl.when(where_ref[1] == core)
                    def _(core=core):
                        for h in range(2):
                            out_ref = keep_ref if h == core else send_ref
                            for j in range(shards):
                                for q in range(W // rows):
                                    first = h * (SMALL // 2) + q * half
                                    value = table_ref[first : first + half, j * rows : j * rows + rows]
                                    out_ref[j, 3, :, q * rows : q * rows + rows] = value

    shape = (shards, blocks, half, W)
    return pl.pallas_call(
        kernel,
        grid=(blocks,),
        in_specs=[SMEM, whole((n, D)), pl.BlockSpec((n, W), lambda i: (0, jnp.minimum(i, 2)))]
        + [whole(x.shape) for x in small],
        out_specs=[whole(shape), whole(shape)],
        scratch_shapes=[pltpu.VMEM((D, n), BF16)] + [pltpu.VMEM((SMALL, D), BF16)] * bool(small),
        out_shape=[jax.ShapeDtypeStruct(shape, BF16)] * 2,
        compiler_params=params(),
        cost_estimate=cost(6 * n * D * D, n * 8 * D + 6 * D * D),
        name="grad_qkv",
    )(where, a, dqkv, *small)


def adam(weight, first, second, grad, rate):
    first = BETA_ONE * first + (1 - BETA_ONE) * grad
    second = BETA_TWO * second + (1 - BETA_TWO) * grad * grad
    spread = second * (1 / (1 - BETA_TWO**STEP_COUNT))
    lower = 1.0 / (spread * lax.rsqrt(spread) + ADAM_EPS)
    weight = weight * (1 - rate * DECAY) - first * lower * (rate / (1 - BETA_ONE**STEP_COUNT))
    return (weight, first, second)


def adam_step(place, where, factor, state, small, grads, chip):
    rows = D // place.shards
    half = rows // 2
    few = half // 2
    flat = [x for group in state for x in group]
    tiny = [x for group in small for x in group]

    def spec(x):
        if x.ndim == 4:
            return pl.BlockSpec((None, 4, few, W), lambda i, h, q: (i, 0, 2 * h + q, 0))
        return pl.BlockSpec((None, few, x.shape[2]), lambda i, h, q: (i, 2 * h + q, 0))

    gflat, spots = [], []
    for layer in grads:
        spots.append([])
        for pieces, first in layer:
            known = [n for n, x in enumerate(gflat) if x is pieces[0]]
            spots[-1].append((known[0] if known else len(gflat), len(pieces), first))
            gflat += [] if known else list(pieces)
    total = len(flat) + len(tiny)

    def kernel(where_ref, factor_ref, *refs):
        grad_refs, refs = refs[: len(gflat)], refs[len(gflat) :]
        ins, outs, table_ref = refs[:total], refs[total : 2 * total], refs[-1]
        layer, h, q = pl.program_id(0), pl.program_id(1), pl.program_id(2)
        scale = factor_ref[0]
        own = where_ref[1] == h
        near = where_ref[chip] == q

        def update(n, at, grad, rate):
            got = adam(ins[3 * n][at], ins[3 * n + 1][at], ins[3 * n + 2][at], grad, rate)
            for k in range(3):
                outs[3 * n + k][at] = got[k]

        part = pl.ds(pl.multiple_of(q * few, few), few)

        def run(layer):
            def grad(group, b):
                base, count, first = spots[layer][group]
                refs = grad_refs[base : base + count]
                if count == 2:
                    got = jnp.where(own, refs[0][first + b, part], refs[1][first + b, part])
                else:
                    close = jnp.where(own, refs[0][first + b], refs[1][first + b])
                    away = jnp.where(own, refs[2][first + b], refs[3][first + b])
                    got = jnp.where(near, close, away)
                return got.astype(F32) * scale

            for b in range(3):
                update(0, (slice(None), slice(W * b, W * b + W)), grad(0, b), RATE)
            update(1, (slice(None), slice(None)), grad(1, 8), RATE)
            for b in range(4):
                update(2, (slice(None), slice(W * b, W * b + W)), grad(1, b), RATE)
                update(3, (b,), grad(1, 4 + b), RATE)

        for i in range(L):

            @pl.when(layer == i)
            def _(i=i):
                run(i)

        @pl.when((layer == 0) & (h == 0) & (q == 0))
        def _():
            base, _, at = spots[0][0]
            mine, other = grad_refs[base][at + 3], grad_refs[base + 1][at + 3]
            first = where_ref[1] == 0
            for n, block in enumerate((jnp.where(first, mine, other), jnp.where(first, other, mine))):
                for k in range(W // rows):
                    start = n * (SMALL // 2) + k * half
                    table_ref[start : start + half] = (
                        block[:, k * rows : k * rows + rows].astype(F32) * scale
                    )
            count = 2 * P_SIZE + LEN
            update(4, (slice(None), slice(None)), table_ref[:count], TABLE_RATE)
            norms = small[1][0].shape[0]
            update(5, (slice(None), slice(None)), table_ref[count : count + norms], TABLE_RATE)

    out = pl.pallas_call(
        kernel,
        grid=(L, 2, 2),
        in_specs=[SMEM, SMEM]
        + [whole(g.shape) for g in gflat]
        + [spec(x) for x in flat]
        + [whole(x.shape) for x in tiny],
        out_specs=[spec(x) for x in flat] + [whole(x.shape) for x in tiny],
        out_shape=[pltpu.HBM(x.shape, F32) for x in flat + tiny],
        scratch_shapes=[pltpu.VMEM((SMALL, rows), F32)],
        compiler_params=params(),
        cost_estimate=cost(20 * L * 12 * rows * W, 24 * L * 12 * rows * W),
        name="adam_step",
    )(where, factor, *gflat, *map(in_hbm, flat), *map(in_hbm, tiny))
    return [tuple(out[3 * n : 3 * n + 3]) for n in range(len(state) + len(small))]


def on_device(
    series,
    mask,
    qkv_w,
    out_w,
    up_w,
    down_w,
    patch_maps,
    norm_params,
    qkv_m,
    out_m,
    up_m,
    down_m,
    patch_m,
    norm_m,
    qkv_v,
    out_v,
    up_v,
    down_v,
    patch_v,
    norm_v,
):
    place = Place()
    shards = place.shards
    rows = D // shards
    half = rows // 2
    seqs = series.shape[0]
    count = MASKED * seqs * shards * place.replicas
    shard_bits = [(place.shard >> bit) & 1 for bit in bits_of(shards)]
    where = jnp.stack([place.shard, place.core] + shard_bits + [place.chip & 1]).astype(jnp.int32)
    chip = 2 + len(shard_bits)

    small_now = [patch_maps, norm_params]
    packs = [
        (
            pack(place, where, i, [qkv_w, out_w], [], small_now if i == 0 else []),
            pack(place, where, i, [up_w], [down_w], []),
        )
        for i in range(L)
    ]

    def group_of(packed, ours, theirs):
        return [packed[0]] + ours + [theirs]

    attn_groups = [None] * L
    mlp_groups = [None] * L
    target = series.reshape(seqs * LEN, P_SIZE)
    maskf = mask.reshape(seqs * LEN, 1).astype(F32)
    ours = gather_shards(place, packs[0][0][1])
    theirs = gather_cores(place, ours, *[p[1] for pair in packs for p in pair], target, maskf)
    attn_groups[0] = group_of(packs[0][0], ours, theirs)
    mine = gate(packs[0][1][1], *ours)
    ours_mlp = gather_shards(place, mine)

    x, inputs, head, norms_all = embed_step(place, where, target, gate(maskf, mine), attn_groups[0])
    saved = []
    for index in range(L):
        norms = norms_all[4 * index : 4 * index + 4]
        mid, qkv, pt, ot = attn_fwd(place, where, x, norms, attn_groups[index])
        held = mid
        if index + 1 < L:
            got = gates(ours_mlp, mid)
            mine = gate(packs[index + 1][0][1], *got)
            ours_attn = gather_shards(place, mine)
            held = gate(mid, mine)
        theirs = gather_cores(place, ours_mlp, mid)
        mlp_groups[index] = group_of(packs[index][1], ours_mlp, theirs)
        pieces = mlp_groups[index] if index == 0 else [in_hbm(x) for x in mlp_groups[index]]
        y, act, gp = mlp_fwd(place, where, held, norms, pieces)
        if index + 1 < L:
            got = gates(ours_attn, y)
            theirs = gather_cores(place, got)
            attn_groups[index + 1] = group_of(packs[index + 1][0], ours_attn, theirs)
            mine = gate(packs[index + 1][1][1], *got)
            ours_mlp = gather_shards(place, mine)
            y = gate(y, mine)
        saved.append((x, mid, qkv, pt, ot, act, gp, norms))
        x = y

    grad, loss, g_head, dn_final = head_step(
        place, x, target, maskf, head, norms_all[4 * L : 4 * L + 2], count
    )
    loss = (jnp.sum(loss) / P_SIZE).reshape(1, 1)

    norm_grads = {}

    def backward_mlp(index, grad):
        x, mid, qkv, pt, ot, act, gp, norms = saved[index]
        dmid, dh, du, c, dm, dn = mlp_bwd(
            place, where, grad, mid, gp, norms, mlp_groups[index]
        )
        norm_grads[index, 1] = dn
        return dmid, dh, du, c, dm

    def backward_attn(index, dmid, dh):
        x, mid, qkv, pt, ot, act, gp, norms = saved[index]
        grad, dqkv, a, dn = attn_bwd(
            place, where, dmid, dh, x, qkv, pt, ot, norms, attn_groups[index]
        )
        norm_grads[index, 0] = dn
        return grad, dqkv, a

    def grads_mlp(index, du, c, dm, dh):
        return grad_mlp(place, where, c, du, saved[index][5], dm, saved[index][4], dh)

    one, two, end = Flow(place, True), Flow(place, True), Flow(place, False)

    def advance(flows, *after):
        token = sum_round(where, flows, *after)
        for flow in flows:
            flow.launch()
        return token

    loss = loss + place.to_core(loss)
    dmid, dh, du, c, dm = backward_mlp(1, grad)
    token = one.begin(*grads_mlp(1, du, c, dm, dh), (0, 4, 0), (4, 5, 1))
    grad, dqkv_one, a_one = backward_attn(1, gate(dmid, token), dh)
    token = advance([one], grad)
    dmid, dh, du, c, dm = backward_mlp(0, gate(grad, token))
    token = advance([one], dmid)
    token = two.begin(*grads_mlp(0, du, gate(c, token), dm, dh), (0, 4, 0), (4, 5, 1))
    token = advance([one], token)
    token = end.begin(*grad_qkv(place, where, gate(a_one, token), dqkv_one), (0, 3, 0))
    token = advance([two], token)
    grad, dqkv, a = backward_attn(0, gate(dmid, token), dh)
    token = sum_round(where, [one, two], grad)
    small = [inputs, grad, g_head]
    small += [norm_grads[i, k] for i in range(L) for k in range(2)] + [dn_final]
    token = end.begin(*grad_qkv(place, where, gate(a, token), dqkv, small), (0, 4, 1))
    one.launch()
    two.launch()
    while not one.last():
        token = advance([one], token)
    token = sum_round(where, [one, two, end], token)
    end.launch()
    two.launch()
    one.to_neighbours()
    hops = bits_of(place.chips)

    def pass_loss(loss, token):
        if not hops:
            return loss
        return loss + place.to_chip(gate(loss, token), 1 << hops.pop(0))

    while end.step < end.steps - 2:
        loss = pass_loss(loss, token)
        token = sum_round(where, [end] + ([two] if not two.last() else []), token, *one.pieces, loss)
        end.launch()
        if two.step == two.steps - 1:
            break
        if not two.last():
            two.launch()
    one.to_last()
    behind = not two.last()
    while end.step < end.steps - 1:
        loss = pass_loss(loss, token)
        token = advance([end], token, *one.pieces, loss)
    if behind:
        two.launch()
    while hops:
        loss = pass_loss(loss, token)
    state = [(qkv_w, qkv_m, qkv_v), (out_w, out_m, out_v), (up_w, up_m, up_v)]
    state.append(tuple(x.reshape(L, 4, rows, W) for x in (down_w, down_m, down_v)))
    token = sum_round(where, [end, two], token, loss)
    end.launch()
    two.to_neighbours()
    token = sum_round(where, [end], token, *two.pieces)
    end.to_neighbours()
    two.to_last()
    grads = [
        [(end.pieces, 3), (two.pieces, 0)],
        [(end.pieces, 0), (one.pieces, 0)],
    ]
    done_one, done_two, done_last = one.pieces, two.pieces, end.pieces

    both = jnp.concatenate([loss, square_sum(done_one + done_two + done_last)], 1)
    both = sum([place.to_shard(both, k) for k in range(1, shards)], both)
    loss = both[0, 0] / count
    grad_norm = jnp.sqrt(both[0, 1])
    factor = CLIP / jnp.maximum(grad_norm, CLIP)

    small = [(patch_maps, patch_m, patch_v), (norm_params, norm_m, norm_v)]
    results = adam_step(place, where, factor.reshape(1), state, small, grads, chip)
    results[3] = tuple(x.reshape(down_w.shape) for x in results[3])
    news = tuple(r[0] for r in results)
    new_m = tuple(r[1] for r in results)
    new_v = tuple(r[2] for r in results)
    return (loss, grad_norm) + news + new_m + new_v


def solution(mesh):
    batch = P(("shard", "replica"), None)
    stack = P(None, "shard", None)
    flat = P(None, "shard")
    state = (stack, stack, stack, stack, flat, flat)
    return jax.shard_map(
        on_device,
        mesh=mesh,
        in_specs=(batch, batch) + state * 3,
        out_specs=(P(), P()) + state * 3,
        check_vma=False,
    )
```

profile of v0, /device:TPU:0, one launch (start us, length us, event | category | flops | bytes accessed | tf_op | source)
XLA Modules:
  0.0 330.7 jit_solution(8047202550175790757)
XLA Ops:
  0.8 2.3 pack.5
  3.1 3.9 %collective-permute-start.2 = (bf16[5,64,512]{2,1,0:T(8,128)(2,1)}, bf16[5,64,512]{2,1,0:T(8,128)(2,1)S(1)}, u32[]{:S(2)}, u32[]{:S(2)}) collective-permute-start(bf16[5,64,512]{2,1,0:T(8,128)(2,1)} %get-tuple-element.203), channel_id=1, source_target_pairs={{0,24},{8,16},{16,8},{24,0},{1,25},{9,17},{17,9},{25,1},{2,26},{10... | collective-permute-start | bytes 983048 | tf_op jit(solution)/shard_map/ppermute | solution.py:73
  7.6 2.1 pack.6
  10.0 2.8 pack.7
  12.8 2.8 pack.4
  15.8 6.1 %collective-permute-done.1.refs_2_ = bf16[5,64,512]{2,1,0:T(8,128)(2,1)S(1)} collective-permute-done((bf16[5,64,512]{2,1,0:T(8,128)(2,1)}, bf16[5,64,512]{2,1,0:T(8,128)(2,1)S(1)}, u32[]{:S(2)}, u32[]{:S(2)}) %collective-permute-start.1) | collective-permute-done | bytes 327712 | tf_op jit(solution)/shard_map/ppermute | solution.py:73
  23.3 1.5 collective-permute-start.6
  24.7 1.5 collective-permute-start.5
  27.0 1.9 embed_step.1
  28.9 9.8 %attn_fwd.2 = (f32[1024,512]{1,0:T(8,128)S(1)}, bf16[1024,1536]{1,0:T(8,128)(2,1)}, bf16[4,8,256,256]{3,2,1,0:T(8,128)(2,1)}, bf16[4,512,256]{2,1,0:T(8,128)(2,1)}) custom-call(s32[5]{0:T(128)S(1)} %stack.71.where_ref, f32[1024,512]{1,0:T(8,128)S(1)} %get-tuple-element.212.x_ref, f32[4,512]{1,0:T(4,128)S(1)} %get-tuple-element.385.norm_ref, ...), custom_call_target="tpu_custom_call" | custom-call | flops 2684354560 | bytes 10485760 | tf_op jit(solution)/shard_map/attn_fwd/pallas_call | solution.py:543
  39.3 10.8 %collective-permute-done.5.refs_2_ = bf16[8,64,512]{2,1,0:T(8,128)(2,1)} collective-permute-done((bf16[8,64,512]{2,1,0:T(8,128)(2,1)}, bf16[8,64,512]{2,1,0:T(8,128)(2,1)}, u32[]{:S(2)}, u32[]{:S(2)}) %collective-permute-start.5) | collective-permute-done | bytes 524320 | tf_op jit(solution)/shard_map/ppermute | solution.py:73
  50.1 1.5 pad_maximum_fusion
  51.7 1.6 collective-permute-start.10
  53.3 1.4 collective-permute-start.9
  55.3 10.3 %mlp_fwd.2 = (f32[1024,512]{1,0:T(8,128)S(1)}, bf16[1024,2048]{1,0:T(8,128)(2,1)}, bf16[1024,2048]{1,0:T(8,128)(2,1)}) custom-call(s32[5]{0:T(128)S(1)} %stack.71.where_ref, f32[1024,512]{1,0:T(8,128)S(1)} %get-tuple-element.219.mid_ref, f32[4,512]{1,0:T(4,128)S(1)} %get-tuple-element.385.norm_ref, bf16[8,128,512]{2,1,0:T(8,128)(2,1)S(1)} %copy-done.25, ...), custom_call_target="tpu_custom_call" | custom-call | flops 4294967296 | bytes 12582912 | tf_op jit(solution)/shard_map/mlp_fwd/pallas_call | solution.py:618
  67.1 1.6 collective-permute-start.14
  68.7 1.4 collective-permute-start.13
  70.7 9.8 %attn_fwd.3 = (f32[1024,512]{1,0:T(8,128)S(1)}, bf16[1024,1536]{1,0:T(8,128)(2,1)}, bf16[4,8,256,256]{3,2,1,0:T(8,128)(2,1)}, bf16[4,512,256]{2,1,0:T(8,128)(2,1)}) custom-call(s32[5]{0:T(128)S(1)} %stack.71.where_ref, f32[1024,512]{1,0:T(8,128)S(1)} %get-tuple-element.226.x_ref, f32[4,512]{1,0:T(4,128)S(1)} %get-tuple-element.384.norm_ref, ...), custom_call_target="tpu_custom_call" | custom-call | flops 2684354560 | bytes 10485760 | tf_op jit(solution)/shard_map/attn_fwd/pallas_call | solution.py:543
  82.9 10.7 %collective-permute-done.13.refs_2_ = bf16[8,64,512]{2,1,0:T(8,128)(2,1)S(1)} collective-permute-done((bf16[8,64,512]{2,1,0:T(8,128)(2,1)S(1)}, bf16[8,64,512]{2,1,0:T(8,128)(2,1)S(1)}, u32[]{:S(2)}, u32[]{:S(2)}) %collective-permute-start.13) | collective-permute-done | bytes 524320 | tf_op jit(solution)/shard_map/ppermute | solution.py:73
  93.6 1.4 pad_maximum_fusion.1
  95.4 3.5 %collective-permute-done.15.refs_4_ = bf16[3,8,64,512]{3,2,1,0:T(8,128)(2,1)} collective-permute-done((bf16[3,8,64,512]{3,2,1,0:T(8,128)(2,1)}, bf16[3,8,64,512]{3,2,1,0:T(8,128)(2,1)}, u32[]{:S(2)}, u32[]{:S(2)}) %collective-permute-start.15) | collective-permute-done | bytes 1572896 | tf_op jit(solution)/shard_map/ppermute | solution.py:73
  98.9 1.6 copy-done.35
  100.5 10.8 %mlp_fwd.3 = (f32[1024,512]{1,0:T(8,128)S(1)}, bf16[1024,2048]{1,0:T(8,128)(2,1)}, bf16[1024,2048]{1,0:T(8,128)(2,1)}) custom-call(s32[5]{0:T(128)S(1)} %stack.71.where_ref, f32[1024,512]{1,0:T(8,128)S(1)} %copy-done.35, f32[4,512]{1,0:T(4,128)S(1)} %get-tuple-element.384.norm_ref, bf16[8,128,512]{2,1,0:T(8,128)(2,1)} %get-tuple-element.232.refs_0_, ...), custom_call_target="tpu_custom_call" | custom-call | flops 4294967296 | bytes 12582912 | tf_op jit(solution)/shard_map/mlp_fwd/pallas_call | solution.py:618
  111.3 3.8 %head_step.1 = (f32[1024,512]{1,0:T(8,128)S(1)}, f32[1,64]{1,0:T(1,128)S(1)}, f32[64,512]{1,0:T(8,128)S(1)}, f32[8,512]{1,0:T(8,128)S(1)}) custom-call(f32[1024,512]{1,0:T(8,128)S(1)} %get-tuple-element.236.x_ref, bf16[1024,64]{1,0:T(8,128)(2,1)S(1)} %reshape.110.target_ref, f32[1024,1]{1,0:T(8,128)S(1)} %copy.41.mask_ref, ...), custom_call_target="tpu_custom_call" | custom-call | flops 201326592 | bytes 4194304 | tf_op jit(solution)/shard_map/head_step/pallas_call | solution.py:842
  115.2 9.3 %mlp_bwd.2 = (f32[1024,512]{1,0:T(8,128)S(1)}, bf16[1024,512]{1,0:T(8,128)(2,1)S(1)}, bf16[1024,2048]{1,0:T(8,128)(2,1)S(1)}, bf16[1024,512]{1,0:T(8,128)(2,1)S(...) custom-call(s32[5]{0:T(128)S(1)} %stack.71.where_ref, f32[1024,512]{1,0:T(8,128)S(1)} %get-tuple-element.239.dz_ref, ...), custom_call_target="tpu_custom_call" | custom-call | flops 4294967296 | bytes 16777216 | tf_op jit(solution)/shard_map/mlp_bwd/pallas_call | solution.py:685
  124.6 9.1 %grad_mlp.2 = (bf16[4,9,64,512]{3,2,1,0:T(8,128)(2,1)S(1)}, bf16[4,9,64,512]{3,2,1,0:T(8,128)(2,1)S(1)}) custom-call(s32[5]{0:T(128)S(1)} %stack.71.where_ref, bf16[1024,512]{1,0:T(8,128)(2,1)S(1)} %get-tuple-element.241.c_ref, bf16[1024,2048]{1,0:T(8,128)(2,1)S(1)} %get-tuple-element.242.du_ref, bf16[1024,2048]{1,0:T(8,128)(2,1)} %get-tuple-element.243.act_ref, ...), custom_call_target="tpu_custom_call" | custom-call | flops 4294967296 | bytes 14680064 | tf_op jit(solution)/shard_map/grad_mlp/pallas_call | solution.py:913
  133.9 11.1 %attn_bwd.2 = (f32[1024,512]{1,0:T(8,128)S(1)}, bf16[1024,1536]{1,0:T(8,128)(2,1)S(1)}, bf16[1024,512]{1,0:T(8,128)(2,1)S(1)}, f32[8,512]{1,0:T(8,128)S(1)}) custom-call(s32[5]{0:T(128)S(1)} %stack.71.where_ref, f32[1024,512]{1,0:T(8,128)S(1)} %get-tuple-element.250.dmid_ref, bf16[1024,512]{1,0:T(8,128)(2,1)S(1)} %get-tuple-element.246.dh_ref, ...), custom_call_target="tpu_custom_call" | custom-call | flops 3489660928 | bytes 16777216 | tf_op jit(solution)/shard_map/attn_bwd/pallas_call | solution.py:782
  146.0 1.5 sum_round.10
  147.5 1.5 collective-permute-start.19
  149.7 9.2 %mlp_bwd.3 = (f32[1024,512]{1,0:T(8,128)S(1)}, bf16[1024,512]{1,0:T(8,128)(2,1)S(1)}, bf16[1024,2048]{1,0:T(8,128)(2,1)S(1)}, bf16[1024,512]{1,0:T(8,128)(2,1)S(...) custom-call(s32[5]{0:T(128)S(1)} %stack.71.where_ref, f32[1024,512]{1,0:T(8,128)S(1)} %get-tuple-element.260.dz_ref, ...), custom_call_target="tpu_custom_call" | custom-call | flops 4294967296 | bytes 16777216 | tf_op jit(solution)/shard_map/mlp_bwd/pallas_call | solution.py:685
  158.9 2.1 copy-done.30
  161.0 1.9 collective-permute-done.18.refs_1_
  162.9 1.7 collective-permute-done.19.refs_3_
  165.6 2.2 copy-done.31
  167.8 8.7 %grad_mlp.3 = (bf16[4,9,64,512]{3,2,1,0:T(8,128)(2,1)S(1)}, bf16[4,9,64,512]{3,2,1,0:T(8,128)(2,1)S(1)}) custom-call(s32[5]{0:T(128)S(1)} %stack.71.where_ref, bf16[1024,512]{1,0:T(8,128)(2,1)S(1)} %get-tuple-element.272.c_ref, bf16[1024,2048]{1,0:T(8,128)(2,1)S(1)} %copy-done.31, bf16[1024,2048]{1,0:T(8,128)(2,1)} %get-tuple-element.274.act_ref, ...), custom_call_target="tpu_custom_call" | custom-call | flops 4294967296 | bytes 14680064 | tf_op jit(solution)/shard_map/grad_mlp/pallas_call | solution.py:913
  176.6 1.5 collective-permute-start.21
  178.8 7.8 %collective-permute-done.20.refs_1_ = bf16[4,64,512]{2,1,0:T(8,128)(2,1)S(1)} collective-permute-done((bf16[4,64,512]{2,1,0:T(8,128)(2,1)S(1)}, bf16[4,64,512]{2,1,0:T(8,128)(2,1)S(1)}, u32[]{:S(2)}, u32[]{:S(2)}) %collective-permute-start.20) | collective-permute-done | bytes 262176 | tf_op jit(solution)/shard_map/ppermute | solution.py:73
  187.6 3.3 grad_qkv.2
  190.9 1.7 sum_round.13
  192.6 1.5 collective-permute-start.25
  194.8 1.7 collective-permute-start.22
  196.4 11.1 %attn_bwd.3 = (f32[1024,512]{1,0:T(8,128)S(1)}, bf16[1024,1536]{1,0:T(8,128)(2,1)S(1)}, bf16[1024,512]{1,0:T(8,128)(2,1)S(1)}, f32[8,512]{1,0:T(8,128)S(1)}) custom-call(s32[5]{0:T(128)S(1)} %stack.71.where_ref, f32[1024,512]{1,0:T(8,128)S(1)} %get-tuple-element.296.dmid_ref, bf16[1024,512]{1,0:T(8,128)(2,1)S(1)} %get-tuple-element.277.dh_ref, ...), custom_call_target="tpu_custom_call" | custom-call | flops 3489660928 | bytes 16777216 | tf_op jit(solution)/shard_map/attn_bwd/pallas_call | solution.py:782
  207.6 1.4 collective-permute-done.25.refs_5_
  210.1 3.9 %grad_qkv.3 = (bf16[4,4,64,512]{3,2,1,0:T(8,128)(2,1)S(1)}, bf16[4,4,64,512]{3,2,1,0:T(8,128)(2,1)S(1)}) custom-call(s32[5]{0:T(128)S(1)} %stack.71.where_ref, bf16[1024,512]{1,0:T(8,128)(2,1)S(1)} %get-tuple-element.313.a_ref, bf16[1024,1536]{1,0:T(8,128)(2,1)S(1)} %get-tuple-element.314.dqkv_ref, bf16[1024,64]{1,0:T(8,128)(2,1)S(1)} %copy-done.22, ...), custom_call_target="tpu_custom_call" | custom-call | flops 1610612736 | bytes 5767168 | tf_op jit(solution)/shard_map/grad_qkv/pallas_call | solution.py:990
  214.6 1.5 collective-permute-start.28
  216.0 2.6 collective-permute-start.26
  219.3 7.0 %collective-permute-done.27.refs_3_ = bf16[4,64,512]{2,1,0:T(8,128)(2,1)S(1)} collective-permute-done((bf16[4,64,512]{2,1,0:T(8,128)(2,1)S(1)}, bf16[4,64,512]{2,1,0:T(8,128)(2,1)S(1)}, u32[]{:S(2)}, u32[]{:S(2)}) %collective-permute-start.27) | collective-permute-done | bytes 262176 | tf_op jit(solution)/shard_map/ppermute | solution.py:73
  226.4 5.6 %collective-permute-done.26.refs_1_ = bf16[9,32,512]{2,1,0:T(8,128)(2,1)S(1)} collective-permute-done((bf16[9,32,512]{2,1,0:T(8,128)(2,1)S(1)}, bf16[9,32,512]{2,1,0:T(8,128)(2,1)S(1)}, u32[]{:S(2)}, u32[]{:S(2)}) %collective-permute-start.26) | collective-permute-done | bytes 294944 | tf_op jit(solution)/shard_map/ppermute | solution.py:73
  232.0 2.3 sum_round.15
  240.1 2.7 collective-permute-start.31
  245.0 6.4 %collective-permute-done.34.refs_5_ = bf16[9,32,512]{2,1,0:T(8,128)(2,1)S(1)} collective-permute-done((bf16[9,32,512]{2,1,0:T(8,128)(2,1)}, bf16[9,32,512]{2,1,0:T(8,128)(2,1)S(1)}, u32[]{:S(2)}, u32[]{:S(2)}) %collective-permute-start.34) | collective-permute-done | bytes 294944 | tf_op jit(solution)/shard_map/ppermute | solution.py:73
  253.2 1.4 collective-permute-start.39
  254.6 3.9 %collective-permute-start.37 = (f32[1,1]{1,0:T(1,128)}, f32[1,1]{1,0:T(1,128)}, u32[]{:S(2)}, u32[]{:S(2)}) collective-permute-start(f32[1,1]{1,0:T(1,128)} %add.25), channel_id=1, source_target_pairs={{0,4},{1,5},{2,6},{3,7},{4,0},{5,1},{6,2},{7,3},{8,12},{9,13},{10,... | collective-permute-start | bytes 20 | tf_op jit(solution)/shard_map/ppermute | solution.py:73
  261.8 2.9 collective-permute-start.42
  264.7 10.2 %collective-permute-done.42.refs_3_ = bf16[9,32,512]{2,1,0:T(8,128)(2,1)S(1)} collective-permute-done((bf16[9,32,512]{2,1,0:T(8,128)(2,1)S(1)}, bf16[9,32,512]{2,1,0:T(8,128)(2,1)S(1)}, u32[]{:S(2)}, u32[]{:S(2)}) %collective-permute-start.42) | collective-permute-done | bytes 294944 | tf_op jit(solution)/shard_map/ppermute | solution.py:73
  274.9 1.3 collective-permute-done.41.refs_1_
  277.1 2.1 collective-permute-start.46
  279.2 2.0 collective-permute-start.44
  281.2 12.8 %collective-permute-done.44.refs_6_.refs_4_ = bf16[9,32,512]{2,1,0:T(8,128)(2,1)S(1)} collective-permute-done((bf16[9,32,512]{2,1,0:T(8,128)(2,1)S(1)}, bf16[9,32,512]{2,1,0:T(8,128)(2,1)S(1)}, u32[]{:S(2)}, u32[]{:S(2)}) %collective-permute-start.44) | collective-permute-done | bytes 294944 | tf_op jit(solution)/shard_map/ppermute | solution.py:73
  294.0 4.2 %collective-permute-done.46.refs_1_ = bf16[7,64,512]{2,1,0:T(8,128)(2,1)S(1)} collective-permute-done((bf16[7,64,512]{2,1,0:T(8,128)(2,1)S(1)}, bf16[7,64,512]{2,1,0:T(8,128)(2,1)S(1)}, u32[]{:S(2)}, u32[]{:S(2)}) %collective-permute-start.46) | collective-permute-done | bytes 458784 | tf_op jit(solution)/shard_map/ppermute | solution.py:73
  299.6 1.7 collective-permute-done.45.refs_7_.refs_5_
  304.1 1.4 collective-permute-start.50
  306.8 1.8 collective-permute-done.50
  311.8 16.7 %adam_step.1 = (f32[2,128,1536]{2,1,0:T(8,128)}, f32[2,128,1536]{2,1,0:T(8,128)}, f32[2,128,1536]{2,1,0:T(8,128)}, f32[2,128,512]{2,1,0:T(8,128)}, f32[2,128,512...) custom-call(s32[5]{0:T(128)S(1)} %stack.71.where_ref, ...), custom_call_target="tpu_custom_call" | custom-call | flops 31457280 | bytes 37748736 | tf_op jit(solution)/shard_map/adam_step/pallas_call | solution.py:1090
  (164 shorter events, 35.3 us)
Async XLA Ops:
  3.1 12.7 %collective-permute-start.2 = (bf16[5,64,512]{2,1,0:T(8,128)(2,1)}, bf16[5,64,512]{2,1,0:T(8,128)(2,1)S(1)}, u32[]{:S(2)}, u32[]{:S(2)}) collective-permute-start(bf16[5,64,512]{2,1,0:T(8,128)(2,1)} %get-tuple-element.203), channel_id=1, source_target_pairs={{0,24},{8,16},{16,8},{24,0},{1,25},{9,17},{17,9},{25,1},{2,26},{10... | collective-permute-start | bytes 983048 | tf_op jit(solution)/shard_map/ppermute | solution.py:73
  7.0 14.9 %collective-permute-start.1 = (bf16[5,64,512]{2,1,0:T(8,128)(2,1)}, bf16[5,64,512]{2,1,0:T(8,128)(2,1)S(1)}, u32[]{:S(2)}, u32[]{:S(2)}) collective-permute-start(bf16[5,64,512]{2,1,0:T(8,128)(2,1)} %get-tuple-element.203), channel_id=1, source_target_pairs={{0,16},{8,24},{16,0},{24,8},{1,17},{9,25},{17,1},{25,9},{2,18},{10... | collective-permute-start | bytes 983048 | tf_op jit(solution)/shard_map/ppermute | solution.py:73
  7.5 14.7 %collective-permute-start = (bf16[5,64,512]{2,1,0:T(8,128)(2,1)}, bf16[5,64,512]{2,1,0:T(8,128)(2,1)S(1)}, u32[]{:S(2)}, u32[]{:S(2)}) collective-permute-start(bf16[5,64,512]{2,1,0:T(8,128)(2,1)} %get-tuple-element.203), channel_id=1, source_target_pairs={{0,8},{8,0},{16,24},{24,16},{1,9},{9,1},{17,25},{25,17},{2,10},{10... | collective-permute-start | bytes 983048 | tf_op jit(solution)/shard_map/ppermute | solution.py:73
  15.6 11.4 %copy-start = (bf16[5,128,512]{2,1,0:T(8,128)(2,1)S(1)}, bf16[5,128,512]{2,1,0:T(8,128)(2,1)}, u32[]{:S(2)}) copy-start(bf16[5,128,512]{2,1,0:T(8,128)(2,1)} %get-tuple-element.206.refs_0_) | copy-start | bytes 1966084
  23.3 3.7 %collective-permute-start.3 = (bf16[3,5,64,512]{3,2,1,0:T(8,128)(2,1)}, bf16[3,5,64,512]{3,2,1,0:T(8,128)(2,1)S(1)}, u32[]{:S(2)}, u32[]{:S(2)}) collective-permute-start(bf16[3,5,64,512]{3,2,1,0:T(8,128)(2,1)} %pad_maximum_fusion.2), channel_id=1, source_target_pairs={{0,1},{1,0},{2,3},{3,2},{4,5},{5,4},{6,7},{7,6},{8,9},{9,8},{10,11... | collective-permute-start | bytes 2949128 | tf_op jit(solution)/shard_map/ppermute | solution.py:73
  23.3 16.0 %collective-permute-start.6 = (bf16[8,64,512]{2,1,0:T(8,128)(2,1)}, bf16[8,64,512]{2,1,0:T(8,128)(2,1)}, u32[]{:S(2)}, u32[]{:S(2)}) collective-permute-start(bf16[8,64,512]{2,1,0:T(8,128)(2,1)} %get-tuple-element.204), channel_id=1, source_target_pairs={{0,24},{8,16},{16,8},{24,0},{1,25},{9,17},{17,9},{25,1},{2,26},{10... | collective-permute-start | bytes 1572872 | tf_op jit(solution)/shard_map/ppermute | solution.py:73
  24.7 25.3 %collective-permute-start.5 = (bf16[8,64,512]{2,1,0:T(8,128)(2,1)}, bf16[8,64,512]{2,1,0:T(8,128)(2,1)}, u32[]{:S(2)}, u32[]{:S(2)}) collective-permute-start(bf16[8,64,512]{2,1,0:T(8,128)(2,1)} %get-tuple-element.204), channel_id=1, source_target_pairs={{0,16},{8,24},{16,0},{24,8},{1,17},{9,25},{17,1},{25,9},{2,18},{10... | collective-permute-start | bytes 1572872 | tf_op jit(solution)/shard_map/ppermute | solution.py:73
  26.2 23.8 %collective-permute-start.4 = (bf16[8,64,512]{2,1,0:T(8,128)(2,1)}, bf16[8,64,512]{2,1,0:T(8,128)(2,1)}, u32[]{:S(2)}, u32[]{:S(2)}) collective-permute-start(bf16[8,64,512]{2,1,0:T(8,128)(2,1)} %get-tuple-element.204), channel_id=1, source_target_pairs={{0,8},{8,0},{16,24},{24,16},{1,9},{9,1},{17,25},{25,17},{2,10},{10... | collective-permute-start | bytes 1572872 | tf_op jit(solution)/shard_map/ppermute | solution.py:73
  38.8 26.8 %copy-start.32 = (f32[1024,512]{1,0:T(8,128)}, f32[1024,512]{1,0:T(8,128)S(1)}, u32[]{:S(2)}) copy-start(f32[1024,512]{1,0:T(8,128)S(1)} %get-tuple-element.219.mid_ref) | copy-start | bytes 6291460
  38.8 12.9 %copy-start.39 = (bf16[4,64,512]{2,1,0:T(8,128)(2,1)S(1)}, bf16[4,64,512]{2,1,0:T(8,128)(2,1)}, u32[]{:S(2)}) copy-start(bf16[4,64,512]{2,1,0:T(8,128)(2,1)} %get-tuple-element.218) | copy-start | bytes 786436
  38.8 16.4 %copy-start.25 = (bf16[8,128,512]{2,1,0:T(8,128)(2,1)S(1)}, bf16[8,128,512]{2,1,0:T(8,128)(2,1)}, u32[]{:S(2)}) copy-start(bf16[8,128,512]{2,1,0:T(8,128)(2,1)} %get-tuple-element.220.refs_0_) | copy-start | bytes 3145732
  51.6 3.6 %collective-permute-start.7 = (bf16[3,8,64,512]{3,2,1,0:T(8,128)(2,1)S(1)}, bf16[3,8,64,512]{3,2,1,0:T(8,128)(2,1)S(1)}, u32[]{:S(2)}, u32[]{:S(2)}) collective-permute-start(bf16[3,8,64,512]{3,2,1,0:T(8,128)(2,1)S(1)} %pad_maximum_fusion), channel_id=1, source_target_pairs={{0,1},{1,0},{2,3},{3,2},{4,5},{5,4},{6,7},{7,6},{8,9},{9,8},{10,11... | collective-permute-start | bytes 4718600 | tf_op jit(solution)/shard_map/ppermute | solution.py:73
  51.7 13.9 %collective-permute-start.10 = (bf16[4,64,512]{2,1,0:T(8,128)(2,1)S(1)}, bf16[4,64,512]{2,1,0:T(8,128)(2,1)S(1)}, u32[]{:S(2)}, u32[]{:S(2)}) collective-permute-start(bf16[4,64,512]{2,1,0:T(8,128)(2,1)S(1)} %copy-done.39), channel_id=1, source_target_pairs={{0,24},{8,16},{16,8},{24,0},{1,25},{9,17},{17,9},{25,1},{2,26},{10... | collective-permute-start | bytes 786440 | tf_op jit(solution)/shard_map/ppermute | solution.py:73
  53.3 13.6 %collective-permute-start.9 = (bf16[4,64,512]{2,1,0:T(8,128)(2,1)S(1)}, bf16[4,64,512]{2,1,0:T(8,128)(2,1)S(1)}, u32[]{:S(2)}, u32[]{:S(2)}) collective-permute-start(bf16[4,64,512]{2,1,0:T(8,128)(2,1)S(1)} %copy-done.39), channel_id=1, source_target_pairs={{0,16},{8,24},{16,0},{24,8},{1,17},{9,25},{17,1},{25,9},{2,18},{10... | collective-permute-start | bytes 786440 | tf_op jit(solution)/shard_map/ppermute | solution.py:73
  54.7 12.2 %collective-permute-start.8 = (bf16[4,64,512]{2,1,0:T(8,128)(2,1)S(1)}, bf16[4,64,512]{2,1,0:T(8,128)(2,1)S(1)}, u32[]{:S(2)}, u32[]{:S(2)}) collective-permute-start(bf16[4,64,512]{2,1,0:T(8,128)(2,1)S(1)} %copy-done.39), channel_id=1, source_target_pairs={{0,8},{8,0},{16,24},{24,16},{1,9},{9,1},{17,25},{25,17},{2,10},{10... | collective-permute-start | bytes 786440 | tf_op jit(solution)/shard_map/ppermute | solution.py:73
  55.3 10.3 %copy-start.23 = (bf16[3,8,64,512]{3,2,1,0:T(8,128)(2,1)}, bf16[3,8,64,512]{3,2,1,0:T(8,128)(2,1)S(1)}, u32[]{:S(2)}) copy-start(bf16[3,8,64,512]{3,2,1,0:T(8,128)(2,1)S(1)} %collective-permute-done.7.refs_4_) | copy-start | bytes 4718596
  55.3 11.9 %copy-start.38 = (bf16[8,64,512]{2,1,0:T(8,128)(2,1)S(1)}, bf16[8,64,512]{2,1,0:T(8,128)(2,1)}, u32[]{:S(2)}) copy-start(bf16[8,64,512]{2,1,0:T(8,128)(2,1)} %get-tuple-element.225) | copy-start | bytes 1572868
  55.3 15.4 %copy-start.13 = (bf16[4,128,512]{2,1,0:T(8,128)(2,1)S(1)}, bf16[4,128,512]{2,1,0:T(8,128)(2,1)}, u32[]{:S(2)}) copy-start(bf16[4,128,512]{2,1,0:T(8,128)(2,1)} %get-tuple-element.227.refs_0_) | copy-start | bytes 1572868
  65.6 15.0 %copy-start.3 = (f32[1024,512]{1,0:T(8,128)}, f32[1024,512]{1,0:T(8,128)S(1)}, u32[]{:S(2)}) copy-start(f32[1024,512]{1,0:T(8,128)S(1)} %get-tuple-element.226.x_ref) | copy-start | bytes 6291460
  65.6 15.0 %copy-start.5 = (bf16[4,64,512]{2,1,0:T(8,128)(2,1)}, bf16[4,64,512]{2,1,0:T(8,128)(2,1)S(1)}, u32[]{:S(2)}) copy-start(bf16[4,64,512]{2,1,0:T(8,128)(2,1)S(1)} %collective-permute-done.10.refs_3_) | copy-start | bytes 786436
  66.9 13.6 %copy-start.7 = (bf16[4,64,512]{2,1,0:T(8,128)(2,1)}, bf16[4,64,512]{2,1,0:T(8,128)(2,1)S(1)}, u32[]{:S(2)}) copy-start(bf16[4,64,512]{2,1,0:T(8,128)(2,1)S(1)} %collective-permute-done.9.refs_2_) | copy-start | bytes 786436
  66.9 13.6 %copy-start.9 = (bf16[4,64,512]{2,1,0:T(8,128)(2,1)}, bf16[4,64,512]{2,1,0:T(8,128)(2,1)S(1)}, u32[]{:S(2)}) copy-start(bf16[4,64,512]{2,1,0:T(8,128)(2,1)S(1)} %collective-permute-done.8.refs_1_) | copy-start | bytes 786436
  67.0 3.6 %collective-permute-start.11 = (bf16[3,4,64,512]{3,2,1,0:T(8,128)(2,1)S(1)}, bf16[3,4,64,512]{3,2,1,0:T(8,128)(2,1)S(1)}, u32[]{:S(2)}, u32[]{:S(2)}) collective-permute-start(bf16[3,4,64,512]{3,2,1,0:T(8,128)(2,1)S(1)} %pad_maximum_fusion.3), channel_id=1, source_target_pairs={{0,1},{1,0},{2,3},{3,2},{4,5},{5,4},{6,7},{7,6},{8,9},{9,8},{10,11... | collective-permute-start | bytes 2359304 | tf_op jit(solution)/shard_map/ppermute | solution.py:73
  67.1 15.7 %collective-permute-start.14 = (bf16[8,64,512]{2,1,0:T(8,128)(2,1)S(1)}, bf16[8,64,512]{2,1,0:T(8,128)(2,1)S(1)}, u32[]{:S(2)}, u32[]{:S(2)}) collective-permute-start(bf16[8,64,512]{2,1,0:T(8,128)(2,1)S(1)} %copy-done.38), channel_id=1, source_target_pairs={{0,24},{8,16},{16,8},{24,0},{1,25},{9,17},{17,9},{25,1},{2,26},{10... | collective-permute-start | bytes 1572872 | tf_op jit(solution)/shard_map/ppermute | solution.py:73
  68.7 24.9 %collective-permute-start.13 = (bf16[8,64,512]{2,1,0:T(8,128)(2,1)S(1)}, bf16[8,64,512]{2,1,0:T(8,128)(2,1)S(1)}, u32[]{:S(2)}, u32[]{:S(2)}) collective-permute-start(bf16[8,64,512]{2,1,0:T(8,128)(2,1)S(1)} %copy-done.38), channel_id=1, source_target_pairs={{0,16},{8,24},{16,0},{24,8},{1,17},{9,25},{17,1},{25,9},{2,18},{10... | collective-permute-start | bytes 1572872 | tf_op jit(solution)/shard_map/ppermute | solution.py:73
  70.1 23.5 %collective-permute-start.12 = (bf16[8,64,512]{2,1,0:T(8,128)(2,1)S(1)}, bf16[8,64,512]{2,1,0:T(8,128)(2,1)S(1)}, u32[]{:S(2)}, u32[]{:S(2)}) collective-permute-start(bf16[8,64,512]{2,1,0:T(8,128)(2,1)S(1)} %copy-done.38), channel_id=1, source_target_pairs={{0,8},{8,0},{16,24},{24,16},{1,9},{9,1},{17,25},{25,17},{2,10},{10... | collective-permute-start | bytes 1572872 | tf_op jit(solution)/shard_map/ppermute | solution.py:73
  82.9 12.2 %copy-start.15 = (bf16[8,64,512]{2,1,0:T(8,128)(2,1)}, bf16[8,64,512]{2,1,0:T(8,128)(2,1)S(1)}, u32[]{:S(2)}) copy-start(bf16[8,64,512]{2,1,0:T(8,128)(2,1)S(1)} %collective-permute-done.14.refs_3_) | copy-start | bytes 1572868
  95.1 3.8 %collective-permute-start.15 = (bf16[3,8,64,512]{3,2,1,0:T(8,128)(2,1)}, bf16[3,8,64,512]{3,2,1,0:T(8,128)(2,1)}, u32[]{:S(2)}, u32[]{:S(2)}) collective-permute-start(bf16[3,8,64,512]{3,2,1,0:T(8,128)(2,1)} %pad_maximum_fusion.1), channel_id=1, source_target_pairs={{0,1},{1,0},{2,3},{3,2},{4,5},{5,4},{6,7},{7,6},{8,9},{9,8},{10,11... | collective-permute-start | bytes 4718600 | tf_op jit(solution)/shard_map/ppermute | solution.py:73
  133.6 12.3 %collective-permute-start.17 = (bf16[4,9,64,512]{3,2,1,0:T(8,128)(2,1)S(1)}, bf16[4,9,64,512]{3,2,1,0:T(8,128)(2,1)S(1)}, u32[]{:S(2)}, u32[]{:S(2)}) collective-permute-start(bf16[4,9,64,512]{3,2,1,0:T(8,128)(2,1)S(1)} %get-tuple-element.248), channel_id=1, source_target_pairs={{0,1},{1,0},{2,3},{3,2},{4,5},{5,4},{6,7},{7,6},{8,9},{9,8},{10,11... | collective-permute-start | bytes 7077896 | tf_op jit(solution)/shard_map/ppermute | solution.py:73
  147.5 17.1 %collective-permute-start.19 = (bf16[2,5,64,512]{3,2,1,0:T(8,128)(2,1)S(1)}, bf16[2,5,64,512]{3,2,1,0:T(8,128)(2,1)S(1)}, u32[]{:S(2)}, u32[]{:S(2)}) collective-permute-start(bf16[2,5,64,512]{3,2,1,0:T(8,128)(2,1)S(1)} %get-tuple-element.259), channel_id=1, source_target_pairs={{0,16},{8,24},{16,0},{24,8},{1,17},{9,25},{17,1},{25,9},{2,18},{10... | collective-permute-start | bytes 1966088 | tf_op jit(solution)/shard_map/ppermute | solution.py:73
  149.0 13.9 %collective-permute-start.18 = (bf16[2,4,64,512]{3,2,1,0:T(8,128)(2,1)S(1)}, bf16[2,4,64,512]{3,2,1,0:T(8,128)(2,1)S(1)}, u32[]{:S(2)}, u32[]{:S(2)}) collective-permute-start(bf16[2,4,64,512]{3,2,1,0:T(8,128)(2,1)S(1)} %get-tuple-element.257), channel_id=1, source_target_pairs={{0,8},{8,0},{16,24},{24,16},{1,9},{9,1},{17,25},{25,17},{2,10},{10... | collective-permute-start | bytes 1572872 | tf_op jit(solution)/shard_map/ppermute | solution.py:73
  167.8 19.8 %copy-start.29 = (bf16[1024,512]{1,0:T(8,128)(2,1)S(1)}, bf16[1024,512]{1,0:T(8,128)(2,1)}, u32[]{:S(2)}) copy-start(bf16[1024,512]{1,0:T(8,128)(2,1)} %copy-done.28) | copy-start | bytes 3145732
  176.6 14.3 %collective-permute-start.23 = (bf16[4,9,64,512]{3,2,1,0:T(8,128)(2,1)S(1)}, bf16[4,9,64,512]{3,2,1,0:T(8,128)(2,1)S(1)}, u32[]{:S(2)}, u32[]{:S(2)}) collective-permute-start(bf16[4,9,64,512]{3,2,1,0:T(8,128)(2,1)S(1)} %get-tuple-element.278), channel_id=1, source_target_pairs={{0,1},{1,0},{2,3},{3,2},{4,5},{5,4},{6,7},{7,6},{8,9},{9,8},{10,11... | collective-permute-start | bytes 7077896 | tf_op jit(solution)/shard_map/ppermute | solution.py:73
  176.6 10.1 %collective-permute-start.21 = (bf16[5,64,512]{2,1,0:T(8,128)(2,1)S(1)}, bf16[5,64,512]{2,1,0:T(8,128)(2,1)S(1)}, u32[]{:S(2)}, u32[]{:S(2)}) collective-permute-start(bf16[5,64,512]{2,1,0:T(8,128)(2,1)S(1)} %get-tuple-element.270), channel_id=1, source_target_pairs={{0,8},{8,0},{16,24},{24,16},{1,9},{9,1},{17,25},{25,17},{2,10},{10... | collective-permute-start | bytes 983048 | tf_op jit(solution)/shard_map/ppermute | solution.py:73
  178.2 8.4 %collective-permute-start.20 = (bf16[4,64,512]{2,1,0:T(8,128)(2,1)S(1)}, bf16[4,64,512]{2,1,0:T(8,128)(2,1)S(1)}, u32[]{:S(2)}, u32[]{:S(2)}) collective-permute-start(bf16[4,64,512]{2,1,0:T(8,128)(2,1)S(1)} %get-tuple-element.268), channel_id=1, source_target_pairs={{0,16},{8,24},{16,0},{24,8},{1,17},{9,25},{17,1},{25,9},{2,18},{10... | collective-permute-start | bytes 786440 | tf_op jit(solution)/shard_map/ppermute | solution.py:73
  192.6 16.4 %collective-permute-start.25 = (bf16[2,5,64,512]{3,2,1,0:T(8,128)(2,1)S(1)}, bf16[2,5,64,512]{3,2,1,0:T(8,128)(2,1)S(1)}, u32[]{:S(2)}, u32[]{:S(2)}) collective-permute-start(bf16[2,5,64,512]{3,2,1,0:T(8,128)(2,1)S(1)} %get-tuple-element.295), channel_id=1, source_target_pairs={{0,16},{8,24},{16,0},{24,8},{1,17},{9,25},{17,1},{25,9},{2,18},{10... | collective-permute-start | bytes 1966088 | tf_op jit(solution)/shard_map/ppermute | solution.py:73
  194.1 13.5 %collective-permute-start.24 = (bf16[2,4,64,512]{3,2,1,0:T(8,128)(2,1)S(1)}, bf16[2,4,64,512]{3,2,1,0:T(8,128)(2,1)S(1)}, u32[]{:S(2)}, u32[]{:S(2)}) collective-permute-start(bf16[2,4,64,512]{3,2,1,0:T(8,128)(2,1)S(1)} %get-tuple-element.293), channel_id=1, source_target_pairs={{0,8},{8,0},{16,24},{24,16},{1,9},{9,1},{17,25},{25,17},{2,10},{10... | collective-permute-start | bytes 1572872 | tf_op jit(solution)/shard_map/ppermute | solution.py:73
  194.8 12.8 %collective-permute-start.22 = (bf16[9,32,512]{2,1,0:T(8,128)(2,1)S(1)}, bf16[9,32,512]{2,1,0:T(8,128)(2,1)S(1)}, u32[]{:S(2)}, u32[]{:S(2)}) collective-permute-start(bf16[9,32,512]{2,1,0:T(8,128)(2,1)S(1)} %get-tuple-element.284), channel_id=1, source_target_pairs={{0,2},{1,3},{2,0},{3,1},{4,6},{5,7},{6,4},{7,5},{8,10},{9,11},{10,... | collective-permute-start | bytes 884744 | tf_op jit(solution)/shard_map/ppermute | solution.py:73
  214.0 18.0 %collective-permute-start.30 = (bf16[4,4,64,512]{3,2,1,0:T(8,128)(2,1)S(1)}, bf16[4,4,64,512]{3,2,1,0:T(8,128)(2,1)S(1)}, u32[]{:S(2)}, u32[]{:S(2)}) collective-permute-start(bf16[4,4,64,512]{3,2,1,0:T(8,128)(2,1)S(1)} %get-tuple-element.323), channel_id=1, source_target_pairs={{0,1},{1,0},{2,3},{3,2},{4,5},{5,4},{6,7},{7,6},{8,9},{9,8},{10,11... | collective-permute-start | bytes 3145736 | tf_op jit(solution)/shard_map/ppermute | solution.py:73
  214.1 5.3 %collective-permute-start.29 = (bf16[4,3,64,512]{3,2,1,0:T(8,128)(2,1)S(1)}, bf16[4,3,64,512]{3,2,1,0:T(8,128)(2,1)S(1)}, u32[]{:S(2)}, u32[]{:S(2)}) collective-permute-start(bf16[4,3,64,512]{3,2,1,0:T(8,128)(2,1)S(1)} %get-tuple-element.289), channel_id=1, source_target_pairs={{0,1},{1,0},{2,3},{3,2},{4,5},{5,4},{6,7},{7,6},{8,9},{9,8},{10,11... | collective-permute-start | bytes 2359304 | tf_op jit(solution)/shard_map/ppermute | solution.py:73
  214.6 17.4 %collective-permute-start.28 = (bf16[5,64,512]{2,1,0:T(8,128)(2,1)S(1)}, bf16[5,64,512]{2,1,0:T(8,128)(2,1)S(1)}, u32[]{:S(2)}, u32[]{:S(2)}) collective-permute-start(bf16[5,64,512]{2,1,0:T(8,128)(2,1)S(1)} %get-tuple-element.310), channel_id=1, source_target_pairs={{0,8},{8,0},{16,24},{24,16},{1,9},{9,1},{17,25},{25,17},{2,10},{10... | collective-permute-start | bytes 983048 | tf_op jit(solution)/shard_map/ppermute | solution.py:73
  216.0 15.9 %collective-permute-start.26 = (bf16[9,32,512]{2,1,0:T(8,128)(2,1)S(1)}, bf16[9,32,512]{2,1,0:T(8,128)(2,1)S(1)}, u32[]{:S(2)}, u32[]{:S(2)}) collective-permute-start(bf16[9,32,512]{2,1,0:T(8,128)(2,1)S(1)} %get-tuple-element.324.refs_0_), channel_id=1, source_target_pairs={{0,4},{1,5},{2,6},{3,7},{4,0},{5,1},{6,2},{7,3},{8,12},{9,13},{10,... | collective-permute-start | bytes 884744 | tf_op jit(solution)/shard_map/ppermute | solution.py:73
  218.6 7.7 %collective-permute-start.27 = (bf16[4,64,512]{2,1,0:T(8,128)(2,1)S(1)}, bf16[4,64,512]{2,1,0:T(8,128)(2,1)S(1)}, u32[]{:S(2)}, u32[]{:S(2)}) collective-permute-start(bf16[4,64,512]{2,1,0:T(8,128)(2,1)S(1)} %get-tuple-element.308), channel_id=1, source_target_pairs={{0,16},{8,24},{16,0},{24,8},{1,17},{9,25},{17,1},{25,9},{2,18},{10... | collective-permute-start | bytes 786440 | tf_op jit(solution)/shard_map/ppermute | solution.py:73
  234.3 17.0 %collective-permute-start.33 = (bf16[2,4,64,512]{3,2,1,0:T(8,128)(2,1)}, bf16[2,4,64,512]{3,2,1,0:T(8,128)(2,1)S(1)}, u32[]{:S(2)}, u32[]{:S(2)}) collective-permute-start(bf16[2,4,64,512]{3,2,1,0:T(8,128)(2,1)} %get-tuple-element.338), channel_id=1, source_target_pairs={{0,16},{8,24},{16,0},{24,8},{1,17},{9,25},{17,1},{25,9},{2,18},{10... | collective-permute-start | bytes 1572872 | tf_op jit(solution)/shard_map/ppermute | solution.py:73
  235.0 16.4 %collective-permute-start.32 = (bf16[2,3,64,512]{3,2,1,0:T(8,128)(2,1)}, bf16[2,3,64,512]{3,2,1,0:T(8,128)(2,1)S(1)}, u32[]{:S(2)}, u32[]{:S(2)}) collective-permute-start(bf16[2,3,64,512]{3,2,1,0:T(8,128)(2,1)} %get-tuple-element.334), channel_id=1, source_target_pairs={{0,8},{8,0},{16,24},{24,16},{1,9},{9,1},{17,25},{25,17},{2,10},{10... | collective-permute-start | bytes 1179656 | tf_op jit(solution)/shard_map/ppermute | solution.py:73
  236.3 7.6 %collective-permute-start.36 = (bf16[9,32,512]{2,1,0:T(8,128)(2,1)S(1)}, bf16[9,32,512]{2,1,0:T(8,128)(2,1)S(1)}, u32[]{:S(2)}, u32[]{:S(2)}) collective-permute-start(bf16[9,32,512]{2,1,0:T(8,128)(2,1)S(1)} %get-tuple-element.341.refs_0_.refs_6_), channel_id=1, source_target_pairs={{0,2},{1,3},{2,0},{3,1},{4,6},{5,7},{6,4},{7,5},{8,10},{9,11},{10,... | collective-permute-start | bytes 884744 | tf_op jit(solution)/shard_map/ppermute | solution.py:73
  238.2 1.3 collective-permute-start.16
  240.1 3.7 %collective-permute-start.31 = (f32[1,1]{1,0:T(1,128)}, f32[1,1]{1,0:T(1,128)}, u32[]{:S(2)}, u32[]{:S(2)}) collective-permute-start(f32[1,1]{1,0:T(1,128)} %add.24), channel_id=1, source_target_pairs={{0,2},{1,3},{2,0},{3,1},{4,6},{5,7},{6,4},{7,5},{8,10},{9,11},{10,... | collective-permute-start | bytes 20 | tf_op jit(solution)/shard_map/ppermute | solution.py:73
  242.9 8.5 %collective-permute-start.34 = (bf16[9,32,512]{2,1,0:T(8,128)(2,1)}, bf16[9,32,512]{2,1,0:T(8,128)(2,1)S(1)}, u32[]{:S(2)}, u32[]{:S(2)}) collective-permute-start(bf16[9,32,512]{2,1,0:T(8,128)(2,1)} %get-tuple-element.340), channel_id=1, source_target_pairs={{0,2},{1,3},{2,0},{3,1},{4,6},{5,7},{6,4},{7,5},{8,10},{9,11},{10,... | collective-permute-start | bytes 884744 | tf_op jit(solution)/shard_map/ppermute | solution.py:73
  243.8 7.5 %collective-permute-start.35 = (bf16[9,32,512]{2,1,0:T(8,128)(2,1)S(1)}, bf16[9,32,512]{2,1,0:T(8,128)(2,1)S(1)}, u32[]{:S(2)}, u32[]{:S(2)}) collective-permute-start(bf16[9,32,512]{2,1,0:T(8,128)(2,1)S(1)} %get-tuple-element.341.refs_0_.refs_6_), channel_id=1, source_target_pairs={{0,1},{1,0},{2,3},{3,2},{4,5},{5,4},{6,7},{7,6},{8,9},{9,8},{10,11... | collective-permute-start | bytes 884744 | tf_op jit(solution)/shard_map/ppermute | solution.py:73
  243.8 15.9 %collective-permute-start.38 = (bf16[9,32,512]{2,1,0:T(8,128)(2,1)S(1)}, bf16[9,32,512]{2,1,0:T(8,128)(2,1)S(1)}, u32[]{:S(2)}, u32[]{:S(2)}) collective-permute-start(bf16[9,32,512]{2,1,0:T(8,128)(2,1)S(1)} %collective-permute-done.36.refs_2_.refs_8_), channel_id=1, source_target_pairs={{0,1},{1,0},{2,3},{3,2},{4,5},{5,4},{6,7},{7,6},{8,9},{9,8},{10,11... | collective-permute-start | bytes 884744 | tf_op jit(solution)/shard_map/ppermute | solution.py:73
  252.4 7.3 %collective-permute-start.40 = (bf16[4,64,512]{2,1,0:T(8,128)(2,1)S(1)}, bf16[4,64,512]{2,1,0:T(8,128)(2,1)S(1)}, u32[]{:S(2)}, u32[]{:S(2)}) collective-permute-start(bf16[4,64,512]{2,1,0:T(8,128)(2,1)S(1)} %get-tuple-element.353), channel_id=1, source_target_pairs={{0,8},{8,0},{16,24},{24,16},{1,9},{9,1},{17,25},{25,17},{2,10},{10... | collective-permute-start | bytes 786440 | tf_op jit(solution)/shard_map/ppermute | solution.py:73
  253.2 6.5 %collective-permute-start.39 = (bf16[3,64,512]{2,1,0:T(8,128)(2,1)S(1)}, bf16[3,64,512]{2,1,0:T(8,128)(2,1)S(1)}, u32[]{:S(2)}, u32[]{:S(2)}) collective-permute-start(bf16[3,64,512]{2,1,0:T(8,128)(2,1)S(1)} %get-tuple-element.351), channel_id=1, source_target_pairs={{0,16},{8,24},{16,0},{24,8},{1,17},{9,25},{17,1},{25,9},{2,18},{10... | collective-permute-start | bytes 589832 | tf_op jit(solution)/shard_map/ppermute | solution.py:73
  254.6 4.5 %collective-permute-start.37 = (f32[1,1]{1,0:T(1,128)}, f32[1,1]{1,0:T(1,128)}, u32[]{:S(2)}, u32[]{:S(2)}) collective-permute-start(f32[1,1]{1,0:T(1,128)} %add.25), channel_id=1, source_target_pairs={{0,4},{1,5},{2,6},{3,7},{4,0},{5,1},{6,2},{7,3},{8,12},{9,13},{10,... | collective-permute-start | bytes 20 | tf_op jit(solution)/shard_map/ppermute | solution.py:73
  260.6 15.7 %collective-permute-start.41 = (bf16[7,64,512]{2,1,0:T(8,128)(2,1)S(1)}, bf16[7,64,512]{2,1,0:T(8,128)(2,1)S(1)}, u32[]{:S(2)}, u32[]{:S(2)}) collective-permute-start(bf16[7,64,512]{2,1,0:T(8,128)(2,1)S(1)} %sum_round.17.refs_0_), channel_id=1, source_target_pairs={{0,2},{1,3},{2,0},{3,1},{4,6},{5,7},{6,4},{7,5},{8,10},{9,11},{10,... | collective-permute-start | bytes 1376264 | tf_op jit(solution)/shard_map/ppermute | solution.py:73
  261.8 13.1 %collective-permute-start.42 = (bf16[9,32,512]{2,1,0:T(8,128)(2,1)S(1)}, bf16[9,32,512]{2,1,0:T(8,128)(2,1)S(1)}, u32[]{:S(2)}, u32[]{:S(2)}) collective-permute-start(bf16[9,32,512]{2,1,0:T(8,128)(2,1)S(1)} %get-tuple-element.360.refs_2_), channel_id=1, source_target_pairs={{0,4},{1,5},{2,6},{3,7},{4,0},{5,1},{6,2},{7,3},{8,12},{9,13},{10,... | collective-permute-start | bytes 884744 | tf_op jit(solution)/shard_map/ppermute | solution.py:73
  277.1 21.1 %collective-permute-start.46 = (bf16[7,64,512]{2,1,0:T(8,128)(2,1)S(1)}, bf16[7,64,512]{2,1,0:T(8,128)(2,1)S(1)}, u32[]{:S(2)}, u32[]{:S(2)}) collective-permute-start(bf16[7,64,512]{2,1,0:T(8,128)(2,1)S(1)} %get-tuple-element.364.refs_0_), channel_id=1, source_target_pairs={{0,4},{1,5},{2,6},{3,7},{4,0},{5,1},{6,2},{7,3},{8,12},{9,13},{10,... | collective-permute-start | bytes 1376264 | tf_op jit(solution)/shard_map/ppermute | solution.py:73
  279.2 14.8 %collective-permute-start.44 = (bf16[9,32,512]{2,1,0:T(8,128)(2,1)S(1)}, bf16[9,32,512]{2,1,0:T(8,128)(2,1)S(1)}, u32[]{:S(2)}, u32[]{:S(2)}) collective-permute-start(bf16[9,32,512]{2,1,0:T(8,128)(2,1)S(1)} %get-tuple-element.362.refs_4_.refs_2_), channel_id=1, source_target_pairs={{0,2},{1,3},{2,0},{3,1},{4,6},{5,7},{6,4},{7,5},{8,10},{9,11},{10,... | collective-permute-start | bytes 884744 | tf_op jit(solution)/shard_map/ppermute | solution.py:73
  281.2 12.8 %collective-permute-start.43 = (bf16[9,32,512]{2,1,0:T(8,128)(2,1)S(1)}, bf16[9,32,512]{2,1,0:T(8,128)(2,1)S(1)}, u32[]{:S(2)}, u32[]{:S(2)}) collective-permute-start(bf16[9,32,512]{2,1,0:T(8,128)(2,1)S(1)} %get-tuple-element.362.refs_4_.refs_2_), channel_id=1, source_target_pairs={{0,1},{1,0},{2,3},{3,2},{4,5},{5,4},{6,7},{7,6},{8,9},{9,8},{10,11... | collective-permute-start | bytes 884744 | tf_op jit(solution)/shard_map/ppermute | solution.py:73
  299.0 2.3 collective-permute-start.47
  299.1 2.2 collective-permute-start.45
  303.2 3.5 %collective-permute-start.49 = (f32[1,2]{1,0:T(1,128)S(1)}, f32[1,2]{1,0:T(1,128)S(1)}, u32[]{:S(2)}, u32[]{:S(2)}) collective-permute-start(f32[1,2]{1,0:T(1,128)S(1)} %pad_maximum_fusion.4), channel_id=1, source_target_pairs={{0,16},{8,24},{16,0},{24,8},{1,17},{9,25},{17,1},{25,9},{2,18},{10... | collective-permute-start | bytes 32 | tf_op jit(solution)/shard_map/ppermute | solution.py:73
  304.1 4.4 %collective-permute-start.50 = (f32[1,2]{1,0:T(1,128)S(1)}, f32[1,2]{1,0:T(1,128)S(1)}, u32[]{:S(2)}, u32[]{:S(2)}) collective-permute-start(f32[1,2]{1,0:T(1,128)S(1)} %pad_maximum_fusion.4), channel_id=1, source_target_pairs={{0,24},{8,16},{16,8},{24,0},{1,25},{9,17},{17,9},{25,1},{2,26},{10... | collective-permute-start | bytes 32 | tf_op jit(solution)/shard_map/ppermute | solution.py:73
  305.5 3.5 %collective-permute-start.48 = (f32[1,2]{1,0:T(1,128)S(1)}, f32[1,2]{1,0:T(1,128)S(1)}, u32[]{:S(2)}, u32[]{:S(2)}) collective-permute-start(f32[1,2]{1,0:T(1,128)S(1)} %pad_maximum_fusion.4), channel_id=1, source_target_pairs={{0,8},{8,0},{16,24},{24,16},{1,9},{9,1},{17,25},{25,17},{2,10},{10... | collective-permute-start | bytes 32 | tf_op jit(solution)/shard_map/ppermute | solution.py:73
  (27 other events, 149.3 us)
where the time goes:
time: 332 us; the launch traced here: 331 us
  Pallas kernels  152 us (46%)
  waiting for transfers between devices  100 us (30%)
  starting transfers between devices  55 us (17%)
  local copies, waits for them, and re-layouts  9.69 us (3%)
  between operations  7.58 us (2%)
  other arithmetic  6.15 us (2%)
    ppermute x51, waiting for transfers between devices, permute(): return lax.ppermute(x, axis, [(i, i ^ mask) for i in range(size)])  100 us
    ppermute x51, starting transfers between devices, permute(): return lax.ppermute(x, axis, [(i, i ^ mask) for i in range(size)])  55 us
    pallas_call x2, Pallas kernels, attn_bwd(): pl.pallas_call(kernel, grid=(seqs,), in_specs=[SMEM, row(D), row(D), row(...  22.2 us
    pallas_call x2, Pallas kernels, mlp_fwd(): pl.pallas_call(kernel, grid=(n // tall,), in_specs=[SMEM, row(D), whole((...  21.1 us
    pallas_call x2, Pallas kernels, attn_fwd(): pl.pallas_call(kernel, grid=(seqs // SP,), in_specs=[SMEM, pl.BlockSpec((...  19.7 us
    pallas_call x2, Pallas kernels, mlp_bwd(): pl.pallas_call(kernel, grid=(n // LEN,), in_specs=[SMEM, row(D), row(D),...  18.5 us
    pallas_call x2, Pallas kernels, grad_mlp(): pl.pallas_call(kernel, grid=(2 * steps + 1,), in_specs=[SMEM, whole((n, D...  17.8 us
    pallas_call x1, Pallas kernels, adam_step(): pl.pallas_call(kernel, grid=(L, 2, 2), in_specs=[SMEM, SMEM] + [whole(g.s...  16.7 us
  transfers between devices with their start and end apart: 51, of which 28 were waited for; matrix products, arithmetic and copies ran while one was open for 0% of the time, Pallas kernels for 23%

commit v1 on v0

--- a/solution.py
+++ b/solution.py
@@ -49,12 +49,14 @@
     return center * lax.rsqrt(spread + EPS) * gain + bias
 
 
-def params(**more):
-    return pltpu.CompilerParams(vmem_limit_bytes=30 * 2**20, **more)
+def params(mib=30):
+    return pltpu.CompilerParams(vmem_limit_bytes=mib * 2**20)
 
 
 def cost(flops, data, trans=0):
-    return pl.CostEstimate(flops=int(flops), bytes_accessed=int(data), transcendentals=int(trans))
+    return pl.CostEstimate(
+        flops=int(30 * flops), bytes_accessed=int(30 * data), transcendentals=int(30 * trans)
+    )
 
 
 def whole(shape):
@@ -111,6 +113,13 @@
 
 def gates(items, *after):
     return list(lax.optimization_barrier(tuple(items) + after)[: len(items)])
+
+
+def select_of(items, index):
+    out = items[0]
+    for k in range(1, len(items)):
+        out = jnp.where(index == k, items[k], out)
+    return out
 
 
 def bits_of(size):
@@ -185,15 +194,16 @@
         in_specs=[SMEM] + [block(a.shape) for a in arrays],
         out_specs=[block(s) for s in shapes],
         out_shape=[jax.ShapeDtypeStruct(s, BF16) for s in shapes],
-        compiler_params=params(),
+        compiler_params=params(12),
         cost_estimate=cost(size, size),
         name=name,
     )(where, *arrays)
 
 
 class Flow:
-    def __init__(self, place, spread):
+    def __init__(self, place, spread, far_first=False):
         self.place, self.spread = place, spread
+        self.chip_bits = bits_of(place.chips)[:: -1 if far_first else 1]
         self.bits = bits_of(place.shards)
         self.steps = len(self.bits) + len(bits_of(place.chips))
         self.step = 0
@@ -207,6 +217,11 @@
         self.inputs += [keep, other]
         self.left = [list(reversed(self.bits)) for _ in self.ranges]
         return send
+
+    def join(self, other):
+        self.inputs = other.inputs + self.inputs
+        self.ranges = other.ranges + self.ranges
+        self.left = other.left + self.left
 
     def last(self):
         return self.step == self.steps
@@ -221,7 +236,8 @@
             ]
         if self.step >= len(self.bits):
             cut = self.spread and self.step == len(self.bits)
-            return [(parts, (), "rows", 2 + len(self.bits)) if cut else (parts, (), None, 0)]
+            bit = 2 + len(self.bits) + self.chip_bits[0]
+            return [(parts, (), "rows", bit) if cut else (parts, (), None, 0)]
         jobs, self.chosen = [], []
         for n, (_, _, _, order) in enumerate(self.ranges):
             bit = (self.bits if order == 0 else self.bits[::-1])[self.step]
@@ -242,14 +258,15 @@
         if self.step < len(self.bits):
             got = [place.to_shard(x, 1 << bit) for x, bit in zip(self.sends, self.chosen)]
         else:
-            got = [place.to_chip(x, 1 << (self.step - len(self.bits))) for x in self.sends]
+            bit = self.chip_bits[self.step - len(self.bits)]
+            got = [place.to_chip(x, 1 << bit) for x in self.sends]
         self.inputs = [x for pair in zip(self.stays, got) for x in pair]
         self.step += 1
 
     def to_neighbours(self):
         self.pieces = [self.sends[0], self.place.to_core(self.sends[0])]
         if self.spread:
-            self.pieces.append(self.place.to_chip(self.sends[0], 1))
+            self.pieces.append(self.place.to_chip(self.sends[0], 1 << self.chip_bits[0]))
 
     def to_last(self):
         if self.spread:
@@ -272,24 +289,26 @@
     return token
 
 
-def square_sum(pieces):
-    def kernel(*refs):
+def square_sum(pieces, loss):
+    def kernel(loss_ref, *refs):
         total = jnp.zeros((1, W), F32)
         for ref in refs[:-1]:
             for b in range(ref.shape[0]):
                 x = ref[b].astype(F32)
                 total = total + jnp.sum(x * x, 0, keepdims=True)
-        refs[-1][...] = jnp.sum(total, 1, keepdims=True)
+        refs[-1][:, 0:1] = loss_ref[...]
+        refs[-1][:, 1:2] = jnp.sum(total, 1, keepdims=True)
 
     return pl.pallas_call(
         kernel,
         grid=(1,),
-        in_specs=[whole(p.shape) for p in pieces],
-        out_specs=whole((1, 1)),
-        out_shape=jax.ShapeDtypeStruct((1, 1), F32),
-        compiler_params=params(),
+        in_specs=[whole((1, 1))] + [whole(p.shape) for p in pieces],
+        out_specs=whole((1, 2)),
+        out_shape=jax.ShapeDtypeStruct((1, 2), F32),
+        compiler_params=params(8),
+        cost_estimate=cost(10**6, 10**6),
         name="square_sum",
-    )(*pieces)
+    )(loss, *pieces)
 
 
 def fill_weights(step, where_ref, sources, targets, sem):
@@ -552,7 +571,7 @@
             pl.BlockSpec((SP, D, LEN), lambda i: (i, 0, 0)),
         ],
         out_shape=[
-            jax.ShapeDtypeStruct((n, D), F32),
+            pltpu.HBM((n, D), F32),
             pltpu.HBM((n, 3 * D), BF16),
             pltpu.HBM((seqs, H, LEN, LEN), BF16),
             pltpu.HBM((seqs, D, LEN), BF16),
@@ -633,7 +652,7 @@
         compiler_params=params(),
         cost_estimate=cost(4 * n * D * FF, n * D * 24, n * FF * 2),
         name="mlp_fwd",
-    )(where, mid, norms, *group)
+    )(where, in_hbm(mid), norms, *group)
 
 
 def mlp_bwd(place, where, dz, mid, gp, norms, group):
@@ -690,7 +709,7 @@
         out_shape=[
             jax.ShapeDtypeStruct((n, D), F32),
             jax.ShapeDtypeStruct((n, D), BF16),
-            jax.ShapeDtypeStruct((n, FF), BF16),
+            pltpu.HBM((n, FF), BF16),
             jax.ShapeDtypeStruct((n, D), BF16),
             jax.ShapeDtypeStruct((n, D), BF16),
             jax.ShapeDtypeStruct((8, D), F32),
@@ -703,7 +722,7 @@
         compiler_params=params(),
         cost_estimate=cost(4 * n * D * FF, n * D * 32),
         name="mlp_bwd",
-    )(where, dz, mid, in_hbm(gp), norms, *group)
+    )(where, dz, in_hbm(mid), in_hbm(gp), norms, *group)
 
 
 def attn_bwd(place, where, dmid, dh, x, qkv, pt, ot, norms, group):
@@ -928,7 +947,7 @@
         compiler_params=params(),
         cost_estimate=cost(4 * n * D * FF, n * (4 * D + 4 * FF) + 4 * D * FF),
         name="grad_mlp",
-    )(where, c, du, in_hbm(act), dm, in_hbm(ot), dh)
+    )(where, c, in_hbm(du), in_hbm(act), dm, in_hbm(ot), dh)
 
 
 def grad_qkv(place, where, a, dqkv, small=()):
@@ -1010,7 +1029,30 @@
     return (weight, first, second)
 
 
-def adam_step(place, where, factor, state, small, grads, chip):
+def fetch(arrays, where):
+    def kernel(where_ref, *refs):
+        sem = refs[-1]
+        count = len(arrays)
+        copies = [
+            pltpu.make_async_copy(refs[n], refs[count + n], sem.at[n]) for n in range(count)
+        ]
+        for copy in copies:
+            copy.start()
+        for copy in copies:
+            copy.wait()
+
+    return pl.pallas_call(
+        kernel,
+        in_specs=[SMEM] + [pl.BlockSpec(memory_space=pltpu.HBM)] * len(arrays),
+        out_specs=[pl.BlockSpec(memory_space=pltpu.VMEM)] * len(arrays),
+        out_shape=[pltpu.VMEM(x.shape, x.dtype) for x in arrays],
+        scratch_shapes=[pltpu.SemaphoreType.DMA((len(arrays),))],
+        compiler_params=params(4),
+        name="fetch",
+    )(where, *map(in_hbm, arrays))
+
+
+def adam_step(place, where, both, count, state, small, grads):
     rows = D // place.shards
     half = rows // 2
     few = half // 2
@@ -1025,19 +1067,27 @@
     gflat, spots = [], []
     for layer in grads:
         spots.append([])
-        for pieces, first in layer:
+        for pieces, first, bit in layer:
             known = [n for n, x in enumerate(gflat) if x is pieces[0]]
-            spots[-1].append((known[0] if known else len(gflat), len(pieces), first))
+            spots[-1].append((known[0] if known else len(gflat), len(pieces), first, bit))
             gflat += [] if known else list(pieces)
     total = len(flat) + len(tiny)
 
-    def kernel(where_ref, factor_ref, *refs):
+    def kernel(where_ref, *refs):
+        both_refs, refs = refs[: len(both)], refs[len(both) :]
         grad_refs, refs = refs[: len(gflat)], refs[len(gflat) :]
         ins, outs, table_ref = refs[:total], refs[total : 2 * total], refs[-1]
+        loss_ref, norm_ref = refs[2 * total : 2 * total + 2]
         layer, h, q = pl.program_id(0), pl.program_id(1), pl.program_id(2)
-        scale = factor_ref[0]
+        values = [ref[...] for ref in both_refs]
+        sums = jnp.zeros((1, 2), F32)
+        for j in range(len(values)):
+            sums = sums + select_of(values, where_ref[0] ^ j)
+        norm = jnp.sqrt(sums[:, 1:2])
+        loss_ref[...] = sums[:, 0:1] / count
+        norm_ref[...] = norm
+        scale = CLIP / jnp.maximum(norm, CLIP)
         own = where_ref[1] == h
-        near = where_ref[chip] == q
 
         def update(n, at, grad, rate):
             got = adam(ins[3 * n][at], ins[3 * n + 1][at], ins[3 * n + 2][at], grad, rate)
@@ -1048,14 +1098,14 @@
 
         def run(layer):
             def grad(group, b):
-                base, count, first = spots[layer][group]
+                base, count, first, bit = spots[layer][group]
                 refs = grad_refs[base : base + count]
                 if count == 2:
                     got = jnp.where(own, refs[0][first + b, part], refs[1][first + b, part])
                 else:
                     close = jnp.where(own, refs[0][first + b], refs[1][first + b])
                     away = jnp.where(own, refs[2][first + b], refs[3][first + b])
-                    got = jnp.where(near, close, away)
+                    got = jnp.where(where_ref[bit] == q, close, away)
                 return got.astype(F32) * scale
 
             for b in range(3):
@@ -1073,7 +1123,7 @@
 
         @pl.when((layer == 0) & (h == 0) & (q == 0))
         def _():
-            base, _, at = spots[0][0]
+            base, _, at, _ = spots[0][0]
             mine, other = grad_refs[base][at + 3], grad_refs[base + 1][at + 3]
             first = where_ref[1] == 0
             for n, block in enumerate((jnp.where(first, mine, other), jnp.where(first, other, mine))):
@@ -1090,18 +1140,21 @@
     out = pl.pallas_call(
         kernel,
         grid=(L, 2, 2),
-        in_specs=[SMEM, SMEM]
+        in_specs=[SMEM]
+        + [whole((1, 2)) for _ in both]
         + [whole(g.shape) for g in gflat]
         + [spec(x) for x in flat]
         + [whole(x.shape) for x in tiny],
-        out_specs=[spec(x) for x in flat] + [whole(x.shape) for x in tiny],
-        out_shape=[pltpu.HBM(x.shape, F32) for x in flat + tiny],
+        out_specs=[spec(x) for x in flat] + [whole(x.shape) for x in tiny] + [whole((1, 1))] * 2,
+        out_shape=[pltpu.HBM(x.shape, F32) for x in flat + tiny]
+        + [jax.ShapeDtypeStruct((1, 1), F32)] * 2,
         scratch_shapes=[pltpu.VMEM((SMALL, rows), F32)],
-        compiler_params=params(),
+        compiler_params=params(20),
         cost_estimate=cost(20 * L * 12 * rows * W, 24 * L * 12 * rows * W),
         name="adam_step",
-    )(where, factor, *gflat, *map(in_hbm, flat), *map(in_hbm, tiny))
-    return [tuple(out[3 * n : 3 * n + 3]) for n in range(len(state) + len(small))]
+    )(where, *both, *gflat, *flat, *map(in_hbm, tiny))
+    news = [tuple(out[3 * n : 3 * n + 3]) for n in range(len(state) + len(small))]
+    return out[-2].reshape(()), out[-1].reshape(()), news
 
 
 def on_device(
@@ -1133,7 +1186,8 @@
     seqs = series.shape[0]
     count = MASKED * seqs * shards * place.replicas
     shard_bits = [(place.shard >> bit) & 1 for bit in bits_of(shards)]
-    where = jnp.stack([place.shard, place.core] + shard_bits + [place.chip & 1]).astype(jnp.int32)
+    chip_bits = [(place.chip >> bit) & 1 for bit in bits_of(place.chips)]
+    where = jnp.stack([place.shard, place.core] + shard_bits + chip_bits).astype(jnp.int32)
     chip = 2 + len(shard_bits)
 
     small_now = [patch_maps, norm_params]
@@ -1209,7 +1263,8 @@
     def grads_mlp(index, du, c, dm, dh):
         return grad_mlp(place, where, c, du, saved[index][5], dm, saved[index][4], dh)
 
-    one, two, end = Flow(place, True), Flow(place, True), Flow(place, False)
+    one, two = Flow(place, True, True), Flow(place, True)
+    ahead, end = Flow(place, False), Flow(place, False)
 
     def advance(flows, *after):
         token = sum_round(where, flows, *after)
@@ -1226,19 +1281,21 @@
     token = advance([one], dmid)
     token = two.begin(*grads_mlp(0, du, gate(c, token), dm, dh), (0, 4, 0), (4, 5, 1))
     token = advance([one], token)
-    token = end.begin(*grad_qkv(place, where, gate(a_one, token), dqkv_one), (0, 3, 0))
+    token = ahead.begin(*grad_qkv(place, where, gate(a_one, token), dqkv_one), (0, 3, 0))
     token = advance([two], token)
     grad, dqkv, a = backward_attn(0, gate(dmid, token), dh)
-    token = sum_round(where, [one, two], grad)
+    token = sum_round(where, [one, two, ahead], grad)
     small = [inputs, grad, g_head]
     small += [norm_grads[i, k] for i in range(L) for k in range(2)] + [dn_final]
     token = end.begin(*grad_qkv(place, where, gate(a, token), dqkv, small), (0, 4, 1))
     one.launch()
     two.launch()
+    ahead.launch()
     while not one.last():
         token = advance([one], token)
     token = sum_round(where, [one, two, end], token)
     end.launch()
+    end.join(ahead)
     two.launch()
     one.to_neighbours()
     hops = bits_of(place.chips)
@@ -1250,17 +1307,17 @@
 
     while end.step < end.steps - 2:
         loss = pass_loss(loss, token)
-        token = sum_round(where, [end] + ([two] if not two.last() else []), token, *one.pieces, loss)
+        token = sum_round(where, [end] + ([two] if not two.last() else []), token, loss)
         end.launch()
         if two.step == two.steps - 1:
             break
         if not two.last():
             two.launch()
-    one.to_last()
     behind = not two.last()
     while end.step < end.steps - 1:
         loss = pass_loss(loss, token)
         token = advance([end], token, *one.pieces, loss)
+    one.to_last()
     if behind:
         two.launch()
     while hops:
@@ -1270,23 +1327,22 @@
     token = sum_round(where, [end, two], token, loss)
     end.launch()
     two.to_neighbours()
-    token = sum_round(where, [end], token, *two.pieces)
+    near = fetch([x for group in state for x in group], gate(where, token))
+    state = [tuple(near[3 * n : 3 * n + 3]) for n in range(len(state))]
+    token = sum_round(where, [end], token, *two.pieces, near[0])
     end.to_neighbours()
     two.to_last()
     grads = [
-        [(end.pieces, 3), (two.pieces, 0)],
-        [(end.pieces, 0), (one.pieces, 0)],
+        [(end.pieces, 3, 0), (two.pieces, 0, chip + two.chip_bits[0])],
+        [(end.pieces, 0, 0), (one.pieces, 0, chip + one.chip_bits[0])],
     ]
     done_one, done_two, done_last = one.pieces, two.pieces, end.pieces
 
-    both = jnp.concatenate([loss, square_sum(done_one + done_two + done_last)], 1)
-    both = sum([place.to_shard(both, k) for k in range(1, shards)], both)
-    loss = both[0, 0] / count
-    grad_norm = jnp.sqrt(both[0, 1])
-    factor = CLIP / jnp.maximum(grad_norm, CLIP)
+    both = square_sum(done_one + done_two + done_last, loss)
+    both = [both] + [place.to_shard(both, k) for k in range(1, shards)]
 
     small = [(patch_maps, patch_m, patch_v), (norm_params, norm_m, norm_v)]
-    results = adam_step(place, where, factor.reshape(1), state, small, grads, chip)
+    loss, grad_norm, results = adam_step(place, where, both, count, state, small, grads)
     results[3] = tuple(x.reshape(down_w.shape) for x in results[3])
     news = tuple(r[0] for r in results)
     new_m = tuple(r[1] for r in results)

time: 332 us -> 310 us (0.934)
  starting transfers between devices: 55 us -> 45.5 us
  waiting for transfers between devices: 100 us -> 91.9 us
  Pallas kernels: 152 us -> 160 us
  local copies, waits for them, and re-layouts: 9.69 us -> 4.13 us
  between operations: 7.58 us -> 4.01 us
    ppermute x51, starting transfers between devices: 55 us -> 45.5 us  [permute(): return lax.ppermute(x, axis, [(i, i ^ mask) for i in range(size)])]
    ppermute x51, waiting for transfers between devices: 100 us -> 91.9 us  [permute(): return lax.ppermute(x, axis, [(i, i ^ mask) for i in range(size)])]
    unnamed x81 -> x95, local copies, waits for them, and re-layouts: 8.32 us -> 2.62 us
    pallas_call x2 -> x3, Pallas kernels: 17.9 us -> 19.2 us  [the longest x1 11.5 us: adam_step(): pl.pallas_call(kernel, grid=(L, 2, 2), in_specs=[SMEM] + [whole((1, 2)) f...]
  transfers between devices with their start and end apart: 51 -> 51, of which waited for: 28 -> 26; matrix products, arithmetic and copies ran while one was open for 0% -> 1% of each run, Pallas kernels for 23% -> 32%
where the time goes in v1:
time: 310 us; the launch traced here: 309 us
  Pallas kernels  160 us (52%)
  waiting for transfers between devices  91.9 us (30%)
  starting transfers between devices  45.5 us (15%)
  local copies, waits for them, and re-layouts  4.13 us (1%)
  between operations  4.01 us (1%)
  other arithmetic  3.43 us (1%)
    ppermute x51, waiting for transfers between devices, permute(): return lax.ppermute(x, axis, [(i, i ^ mask) for i in range(size)])  91.9 us
    ppermute x51, starting transfers between devices, permute(): return lax.ppermute(x, axis, [(i, i ^ mask) for i in range(size)])  45.5 us
    pallas_call x2, Pallas kernels, attn_bwd(): pl.pallas_call(kernel, grid=(seqs,), in_specs=[SMEM, row(D), row(D), row(...  23.4 us
    pallas_call x2, Pallas kernels, mlp_fwd(): pl.pallas_call(kernel, grid=(n // tall,), in_specs=[SMEM, row(D), whole((...  21.4 us
    pallas_call x2, Pallas kernels, attn_fwd(): pl.pallas_call(kernel, grid=(seqs // SP,), in_specs=[SMEM, pl.BlockSpec((...  21 us
    pallas_call x2, Pallas kernels, mlp_bwd(): pl.pallas_call(kernel, grid=(n // LEN,), in_specs=[SMEM, row(D), row(D),...  19.6 us
    pallas_call x2, Pallas kernels, grad_mlp(): pl.pallas_call(kernel, grid=(2 * steps + 1,), in_specs=[SMEM, whole((n, D...  18.7 us
    pallas_call x10, Pallas kernels, combine(): pl.pallas_call(kernel, grid=(2,), in_specs=[SMEM] + [block(a.shape) for a...  13.4 us
  transfers between devices with their start and end apart: 51, of which 26 were waited for; matrix products, arithmetic and copies ran while one was open for 1% of the time, Pallas kernels for 32%

profile of v1, /device:TPU:0, one launch (start us, length us, event | category | flops | bytes accessed | tf_op | source)
XLA Modules:
  0.0 309.2 jit_solution(15368633376991821756)
XLA Ops:
  0.8 2.3 pack.5
  3.1 3.9 %collective-permute-start.2 = (bf16[5,64,512]{2,1,0:T(8,128)(2,1)}, bf16[5,64,512]{2,1,0:T(8,128)(2,1)S(1)}, u32[]{:S(2)}, u32[]{:S(2)}) collective-permute-start(bf16[5,64,512]{2,1,0:T(8,128)(2,1)} %get-tuple-element.218), channel_id=1, source_target_pairs={{0,24},{8,16},{16,8},{24,0},{1,25},{9,17},{17,9},{25,1},{2,26},{10... | collective-permute-start | bytes 983048 | tf_op jit(solution)/shard_map/ppermute | solution.py:75
  7.9 2.2 pack.6
  10.1 2.8 pack.7
  12.9 2.8 pack.4
  15.8 6.1 %collective-permute-done.1.refs_2_ = bf16[5,64,512]{2,1,0:T(8,128)(2,1)S(1)} collective-permute-done((bf16[5,64,512]{2,1,0:T(8,128)(2,1)}, bf16[5,64,512]{2,1,0:T(8,128)(2,1)S(1)}, u32[]{:S(2)}, u32[]{:S(2)}) %collective-permute-start.1) | collective-permute-done | bytes 327712 | tf_op jit(solution)/shard_map/ppermute | solution.py:75
  23.3 1.5 collective-permute-start.6
  24.8 1.4 collective-permute-start.5
  28.1 2.5 embed_step.1
  30.7 11.0 %attn_fwd.2 = (f32[1024,512]{1,0:T(8,128)}, bf16[1024,1536]{1,0:T(8,128)(2,1)}, bf16[4,8,256,256]{3,2,1,0:T(8,128)(2,1)}, bf16[4,512,256]{2,1,0:T(8,128)(2,1)}) custom-call(s32[6]{0:T(128)S(1)} %stack.75.where_ref, f32[1024,512]{1,0:T(8,128)S(1)} %get-tuple-element.227.x_ref, f32[4,512]{1,0:T(4,128)S(1)} %get-tuple-element.415.norm_ref, ...), custom_call_target="tpu_custom_call" | custom-call | flops 80530636800 | bytes 314572800 | tf_op jit(solution)/shard_map/attn_fwd/pallas_call | solution.py:562
  41.7 1.3 copy-done.35
  43.1 6.9 %collective-permute-done.5.refs_2_ = bf16[8,64,512]{2,1,0:T(8,128)(2,1)S(1)} collective-permute-done((bf16[8,64,512]{2,1,0:T(8,128)(2,1)}, bf16[8,64,512]{2,1,0:T(8,128)(2,1)S(1)}, u32[]{:S(2)}, u32[]{:S(2)}) %collective-permute-start.5) | collective-permute-done | bytes 524320 | tf_op jit(solution)/shard_map/ppermute | solution.py:75
  50.3 1.5 collective-permute-start.10
  51.9 1.4 collective-permute-start.9
  53.9 10.1 %mlp_fwd.2 = (f32[1024,512]{1,0:T(8,128)S(1)}, bf16[1024,2048]{1,0:T(8,128)(2,1)}, bf16[1024,2048]{1,0:T(8,128)(2,1)}) custom-call(s32[6]{0:T(128)S(1)} %stack.75.where_ref, f32[1024,512]{1,0:T(8,128)} %get-tuple-element.234.mid_ref, f32[4,512]{1,0:T(4,128)S(1)} %get-tuple-element.415.norm_ref, bf16[8,128,512]{2,1,0:T(8,128)(2,1)S(1)} %copy-done.26, ...), custom_call_target="tpu_custom_call" | custom-call | flops 128849018880 | bytes 377487360 | tf_op jit(solution)/shard_map/mlp_fwd/pallas_call | solution.py:637
  64.0 1.5 collective-permute-done.9.refs_2_
  65.8 1.5 collective-permute-start.14
  67.3 1.4 collective-permute-start.13
  69.3 10.0 %attn_fwd.3 = (f32[1024,512]{1,0:T(8,128)}, bf16[1024,1536]{1,0:T(8,128)(2,1)}, bf16[4,8,256,256]{3,2,1,0:T(8,128)(2,1)}, bf16[4,512,256]{2,1,0:T(8,128)(2,1)}) custom-call(s32[6]{0:T(128)S(1)} %stack.75.where_ref, f32[1024,512]{1,0:T(8,128)S(1)} %get-tuple-element.241.x_ref, f32[4,512]{1,0:T(4,128)S(1)} %get-tuple-element.414.norm_ref, ...), custom_call_target="tpu_custom_call" | custom-call | flops 80530636800 | bytes 314572800 | tf_op jit(solution)/shard_map/attn_fwd/pallas_call | solution.py:562
  79.4 2.1 collective-permute-done.14.refs_3_
  81.5 10.7 %collective-permute-done.13.refs_2_ = bf16[8,64,512]{2,1,0:T(8,128)(2,1)S(1)} collective-permute-done((bf16[8,64,512]{2,1,0:T(8,128)(2,1)S(1)}, bf16[8,64,512]{2,1,0:T(8,128)(2,1)S(1)}, u32[]{:S(2)}, u32[]{:S(2)}) %collective-permute-start.13) | collective-permute-done | bytes 524320 | tf_op jit(solution)/shard_map/ppermute | solution.py:75
  92.2 1.5 pad_maximum_fusion.1
  94.7 2.8 collective-permute-done.15.refs_4_
  97.5 11.4 %mlp_fwd.3 = (f32[1024,512]{1,0:T(8,128)S(1)}, bf16[1024,2048]{1,0:T(8,128)(2,1)}, bf16[1024,2048]{1,0:T(8,128)(2,1)}) custom-call(s32[6]{0:T(128)S(1)} %stack.75.where_ref, f32[1024,512]{1,0:T(8,128)} %get-tuple-element.246.mid_ref, f32[4,512]{1,0:T(4,128)S(1)} %get-tuple-element.414.norm_ref, bf16[8,128,512]{2,1,0:T(8,128)(2,1)} %get-tuple-element.247.refs_0_, ...), custom_call_target="tpu_custom_call" | custom-call | flops 128849018880 | bytes 377487360 | tf_op jit(solution)/shard_map/mlp_fwd/pallas_call | solution.py:637
  108.9 3.8 %head_step.1 = (f32[1024,512]{1,0:T(8,128)S(1)}, f32[1,64]{1,0:T(1,128)S(1)}, f32[64,512]{1,0:T(8,128)S(1)}, f32[8,512]{1,0:T(8,128)S(1)}) custom-call(f32[1024,512]{1,0:T(8,128)S(1)} %get-tuple-element.251.x_ref, bf16[1024,64]{1,0:T(8,128)(2,1)S(1)} %copy-done.13, f32[1024,1]{1,0:T(8,128)S(1)} %copy.41.mask_ref, ...), custom_call_target="tpu_custom_call" | custom-call | flops 6039797760 | bytes 125829120 | tf_op jit(solution)/shard_map/head_step/pallas_call | solution.py:861
  112.8 10.4 %mlp_bwd.2 = (f32[1024,512]{1,0:T(8,128)S(1)}, bf16[1024,512]{1,0:T(8,128)(2,1)S(1)}, bf16[1024,2048]{1,0:T(8,128)(2,1)}, bf16[1024,512]{1,0:T(8,128)(2,1)S(1)},...) custom-call(s32[6]{0:T(128)S(1)} %stack.75.where_ref, f32[1024,512]{1,0:T(8,128)S(1)} %get-tuple-element.254.dz_ref, ...), custom_call_target="tpu_custom_call" | custom-call | flops 128849018880 | bytes 503316480 | tf_op jit(solution)/shard_map/mlp_bwd/pallas_call | solution.py:704
  123.2 9.5 %grad_mlp.2 = (bf16[4,9,64,512]{3,2,1,0:T(8,128)(2,1)S(1)}, bf16[4,9,64,512]{3,2,1,0:T(8,128)(2,1)S(1)}) custom-call(s32[6]{0:T(128)S(1)} %stack.75.where_ref, bf16[1024,512]{1,0:T(8,128)(2,1)S(1)} %get-tuple-element.256.c_ref, bf16[1024,2048]{1,0:T(8,128)(2,1)} %get-tuple-element.257.du_ref, bf16[1024,2048]{1,0:T(8,128)(2,1)} %get-tuple-element.258.act_ref, ...), custom_call_target="tpu_custom_call" | custom-call | flops 128849018880 | bytes 440401920 | tf_op jit(solution)/shard_map/grad_mlp/pallas_call | solution.py:932
  133.0 11.1 %attn_bwd.2 = (f32[1024,512]{1,0:T(8,128)S(1)}, bf16[1024,1536]{1,0:T(8,128)(2,1)S(1)}, bf16[1024,512]{1,0:T(8,128)(2,1)S(1)}, f32[8,512]{1,0:T(8,128)S(1)}) custom-call(s32[6]{0:T(128)S(1)} %stack.75.where_ref, f32[1024,512]{1,0:T(8,128)S(1)} %get-tuple-element.265.dmid_ref, bf16[1024,512]{1,0:T(8,128)(2,1)S(1)} %get-tuple-element.261.dh_ref, ...), custom_call_target="tpu_custom_call" | custom-call | flops 104689827840 | bytes 503316480 | tf_op jit(solution)/shard_map/attn_bwd/pallas_call | solution.py:801
  144.1 1.5 sum_round.10
  145.6 1.5 collective-permute-start.18
  147.7 9.2 %mlp_bwd.3 = (f32[1024,512]{1,0:T(8,128)S(1)}, bf16[1024,512]{1,0:T(8,128)(2,1)S(1)}, bf16[1024,2048]{1,0:T(8,128)(2,1)}, bf16[1024,512]{1,0:T(8,128)(2,1)S(1)},...) custom-call(s32[6]{0:T(128)S(1)} %stack.75.where_ref, f32[1024,512]{1,0:T(8,128)S(1)} %get-tuple-element.275.dz_ref, ...), custom_call_target="tpu_custom_call" | custom-call | flops 128849018880 | bytes 503316480 | tf_op jit(solution)/shard_map/mlp_bwd/pallas_call | solution.py:704
  157.0 2.9 collective-permute-done.18.refs_1_
  159.9 3.9 %collective-permute-done.19.refs_3_ = bf16[2,5,64,512]{3,2,1,0:T(8,128)(2,1)S(1)} collective-permute-done((bf16[2,5,64,512]{3,2,1,0:T(8,128)(2,1)S(1)}, bf16[2,5,64,512]{3,2,1,0:T(8,128)(2,1)S(1)}, u32[]{:S(2)}, u32[]{:S(2)}) %collective-permute-start.19) | collective-permute-done | bytes 655392 | tf_op jit(solution)/shard_map/ppermute | solution.py:75
  165.6 1.4 collective-permute-start.21
  167.0 9.2 %grad_mlp.3 = (bf16[4,9,64,512]{3,2,1,0:T(8,128)(2,1)S(1)}, bf16[4,9,64,512]{3,2,1,0:T(8,128)(2,1)S(1)}) custom-call(s32[6]{0:T(128)S(1)} %stack.75.where_ref, bf16[1024,512]{1,0:T(8,128)(2,1)S(1)} %get-tuple-element.287.c_ref, bf16[1024,2048]{1,0:T(8,128)(2,1)} %get-tuple-element.288.du_ref, bf16[1024,2048]{1,0:T(8,128)(2,1)} %get-tuple-element.289.act_ref, ...), custom_call_target="tpu_custom_call" | custom-call | flops 128849018880 | bytes 440401920 | tf_op jit(solution)/shard_map/grad_mlp/pallas_call | solution.py:932
  176.3 1.4 sum_round.12
  177.7 2.6 collective-permute-start.22
  180.3 3.2 %grad_qkv.2 = (bf16[4,3,64,512]{3,2,1,0:T(8,128)(2,1)S(1)}, bf16[4,3,64,512]{3,2,1,0:T(8,128)(2,1)S(1)}) custom-call(s32[6]{0:T(128)S(1)} %stack.75.where_ref, bf16[1024,512]{1,0:T(8,128)(2,1)S(1)} %get-tuple-element.302.a_ref, bf16[1024,1536]{1,0:T(8,128)(2,1)S(1)} %get-tuple-element.303.dqkv_ref), custom_call_target="tpu_custom_call" | custom-call | flops 48318382080 | bytes 173015040 | tf_op jit(solution)/shard_map/grad_qkv/pallas_call | solution.py:1009
  183.8 1.7 sum_round.13
  186.4 1.2 collective-permute-start.25
  187.6 12.3 %attn_bwd.3 = (f32[1024,512]{1,0:T(8,128)S(1)}, bf16[1024,1536]{1,0:T(8,128)(2,1)S(1)}, bf16[1024,512]{1,0:T(8,128)(2,1)S(1)}, f32[8,512]{1,0:T(8,128)S(1)}) custom-call(s32[6]{0:T(128)S(1)} %stack.75.where_ref, f32[1024,512]{1,0:T(8,128)S(1)} %get-tuple-element.312.dmid_ref, bf16[1024,512]{1,0:T(8,128)(2,1)S(1)} %get-tuple-element.292.dh_ref, ...), custom_call_target="tpu_custom_call" | custom-call | flops 104689827840 | bytes 503316480 | tf_op jit(solution)/shard_map/attn_bwd/pallas_call | solution.py:801
  199.9 3.2 %collective-permute-done.25.refs_5_ = bf16[2,5,64,512]{3,2,1,0:T(8,128)(2,1)S(1)} collective-permute-done((bf16[2,5,64,512]{3,2,1,0:T(8,128)(2,1)S(1)}, bf16[2,5,64,512]{3,2,1,0:T(8,128)(2,1)S(1)}, u32[]{:S(2)}, u32[]{:S(2)}) %collective-permute-start.25) | collective-permute-done | bytes 655392 | tf_op jit(solution)/shard_map/ppermute | solution.py:75
  203.1 2.3 sum_round.14
  205.4 3.8 %grad_qkv.3 = (bf16[4,4,64,512]{3,2,1,0:T(8,128)(2,1)S(1)}, bf16[4,4,64,512]{3,2,1,0:T(8,128)(2,1)S(1)}) custom-call(s32[6]{0:T(128)S(1)} %stack.75.where_ref, bf16[1024,512]{1,0:T(8,128)(2,1)S(1)} %get-tuple-element.331.a_ref, bf16[1024,1536]{1,0:T(8,128)(2,1)S(1)} %get-tuple-element.332.dqkv_ref, bf16[1024,64]{1,0:T(8,128)(2,1)S(1)} %copy-done.38, ...), custom_call_target="tpu_custom_call" | custom-call | flops 48318382080 | bytes 173015040 | tf_op jit(solution)/shard_map/grad_qkv/pallas_call | solution.py:1009
  209.4 1.3 collective-permute-start.29
  210.6 1.6 collective-permute-start.27
  212.8 7.5 %collective-permute-done.28.refs_3_ = bf16[4,64,512]{2,1,0:T(8,128)(2,1)S(1)} collective-permute-done((bf16[4,64,512]{2,1,0:T(8,128)(2,1)S(1)}, bf16[4,64,512]{2,1,0:T(8,128)(2,1)S(1)}, u32[]{:S(2)}, u32[]{:S(2)}) %collective-permute-start.28) | collective-permute-done | bytes 262176 | tf_op jit(solution)/shard_map/ppermute | solution.py:75
  220.3 1.9 sum_round.15
  222.9 1.4 collective-permute-start.32
  228.3 2.5 collective-permute-start.31
  233.2 1.9 collective-permute-done.33.refs_3_
  238.2 1.6 collective-permute-start.35
  239.9 6.6 %collective-permute-done.35 = f32[1,1]{1,0:T(1,128)} collective-permute-done((f32[1,1]{1,0:T(1,128)}, f32[1,1]{1,0:T(1,128)}, u32[]{:S(2)}, u32[]{:S(2)}) %collective-permute-start.35) | collective-permute-done | bytes 36 | tf_op jit(solution)/shard_map/ppermute | solution.py:75
  247.9 1.3 collective-permute-start.42
  249.2 14.6 %collective-permute-done.42.refs_3_ = bf16[9,32,512]{2,1,0:T(8,128)(2,1)S(1)} collective-permute-done((bf16[9,32,512]{2,1,0:T(8,128)(2,1)S(1)}, bf16[9,32,512]{2,1,0:T(8,128)(2,1)S(1)}, u32[]{:S(2)}, u32[]{:S(2)}) %collective-permute-start.42) | collective-permute-done | bytes 294944 | tf_op jit(solution)/shard_map/ppermute | solution.py:75
  263.8 2.2 collective-permute-done.41.refs_1_
  266.9 1.3 collective-permute-start.46
  268.2 7.1 %fetch.1 = (f32[2,128,1536]{2,1,0:T(8,128)S(1)}, f32[2,128,1536]{2,1,0:T(8,128)S(1)}, f32[2,128,1536]{2,1,0:T(8,128)S(1)}, f32[2,128,512]{2,1,0:T(8,128)S(1)}, f...) custom-call(s32[6]{0:T(128)S(1)} %stack.75.where_ref, ...), custom_call_target="tpu_custom_call" | custom-call | tf_op jit(solution)/shard_map/fetch/pallas_call | solution.py:1044
  275.3 7.9 %collective-permute-done.44.refs_6_.refs_8_ = bf16[9,32,512]{2,1,0:T(8,128)(2,1)S(1)} collective-permute-done((bf16[9,32,512]{2,1,0:T(8,128)(2,1)S(1)}, bf16[9,32,512]{2,1,0:T(8,128)(2,1)S(1)}, u32[]{:S(2)}, u32[]{:S(2)}) %collective-permute-start.44) | collective-permute-done | bytes 294944 | tf_op jit(solution)/shard_map/ppermute | solution.py:75
  283.2 4.8 %collective-permute-done.46.refs_1_ = bf16[7,64,512]{2,1,0:T(8,128)(2,1)S(1)} collective-permute-done((bf16[7,64,512]{2,1,0:T(8,128)(2,1)S(1)}, bf16[7,64,512]{2,1,0:T(8,128)(2,1)S(1)}, u32[]{:S(2)}, u32[]{:S(2)}) %collective-permute-start.46) | collective-permute-done | bytes 458784 | tf_op jit(solution)/shard_map/ppermute | solution.py:75
  289.5 1.6 collective-permute-done.38.refs_3_.refs_13_
  292.2 1.5 collective-permute-start.50
  294.0 1.7 collective-permute-start.48
  297.5 11.5 %adam_step.1 = (f32[2,128,1536]{2,1,0:T(8,128)}, f32[2,128,1536]{2,1,0:T(8,128)}, f32[2,128,1536]{2,1,0:T(8,128)}, f32[2,128,512]{2,1,0:T(8,128)}, f32[2,128,512...) custom-call(s32[6]{0:T(128)S(1)} %stack.75.where_ref, ...), custom_call_target="tpu_custom_call" | custom-call | flops 943718400 | bytes 1132462080 | tf_op jit(solution)/shard_map/adam_step/pallas_call | solution.py:1140
  (176 shorter events, 26.5 us)
Async XLA Ops:
  3.1 12.7 %collective-permute-start.2 = (bf16[5,64,512]{2,1,0:T(8,128)(2,1)}, bf16[5,64,512]{2,1,0:T(8,128)(2,1)S(1)}, u32[]{:S(2)}, u32[]{:S(2)}) collective-permute-start(bf16[5,64,512]{2,1,0:T(8,128)(2,1)} %get-tuple-element.218), channel_id=1, source_target_pairs={{0,24},{8,16},{16,8},{24,0},{1,25},{9,17},{17,9},{25,1},{2,26},{10... | collective-permute-start | bytes 983048 | tf_op jit(solution)/shard_map/ppermute | solution.py:75
  7.0 14.9 %collective-permute-start.1 = (bf16[5,64,512]{2,1,0:T(8,128)(2,1)}, bf16[5,64,512]{2,1,0:T(8,128)(2,1)S(1)}, u32[]{:S(2)}, u32[]{:S(2)}) collective-permute-start(bf16[5,64,512]{2,1,0:T(8,128)(2,1)} %get-tuple-element.218), channel_id=1, source_target_pairs={{0,16},{8,24},{16,0},{24,8},{1,17},{9,25},{17,1},{25,9},{2,18},{10... | collective-permute-start | bytes 983048 | tf_op jit(solution)/shard_map/ppermute | solution.py:75
  7.5 14.7 %collective-permute-start = (bf16[5,64,512]{2,1,0:T(8,128)(2,1)}, bf16[5,64,512]{2,1,0:T(8,128)(2,1)S(1)}, u32[]{:S(2)}, u32[]{:S(2)}) collective-permute-start(bf16[5,64,512]{2,1,0:T(8,128)(2,1)} %get-tuple-element.218), channel_id=1, source_target_pairs={{0,8},{8,0},{16,24},{24,16},{1,9},{9,1},{17,25},{25,17},{2,10},{10... | collective-permute-start | bytes 983048 | tf_op jit(solution)/shard_map/ppermute | solution.py:75
  7.6 19.2 %copy-start.42 = (f32[1,1,4,256]{3,1,2,0:T(1,128)}, f32[1,1,4,256]{3,1,2,0:T(1,128)S(1)}, u32[]{:S(2)}) copy-start(f32[1,1,4,256]{3,1,2,0:T(1,128)S(1)} %copy.42) | copy-start | bytes 12292
  7.8 19.2 %copy-start.12 = (bf16[1024,64]{1,0:T(8,128)(2,1)}, bf16[1024,64]{1,0:T(8,128)(2,1)S(1)}, u32[]{:S(2)}) copy-start(bf16[1024,64]{1,0:T(8,128)(2,1)S(1)} %reshape.110.target_ref) | copy-start | bytes 393220
  15.8 14.9 %copy-start.6 = (bf16[5,64,512]{2,1,0:T(8,128)(2,1)}, bf16[5,64,512]{2,1,0:T(8,128)(2,1)S(1)}, u32[]{:S(2)}) copy-start(bf16[5,64,512]{2,1,0:T(8,128)(2,1)S(1)} %collective-permute-done.2.refs_3_) | copy-start | bytes 983044
  23.3 3.7 %collective-permute-start.3 = (bf16[3,5,64,512]{3,2,1,0:T(8,128)(2,1)}, bf16[3,5,64,512]{3,2,1,0:T(8,128)(2,1)}, u32[]{:S(2)}, u32[]{:S(2)}) collective-permute-start(bf16[3,5,64,512]{3,2,1,0:T(8,128)(2,1)} %pad_maximum_fusion.2), channel_id=1, source_target_pairs={{0,1},{1,0},{2,3},{3,2},{4,5},{5,4},{6,7},{7,6},{8,9},{9,8},{10,11... | collective-permute-start | bytes 2949128 | tf_op jit(solution)/shard_map/ppermute | solution.py:75
  23.3 19.7 %collective-permute-start.6 = (bf16[8,64,512]{2,1,0:T(8,128)(2,1)}, bf16[8,64,512]{2,1,0:T(8,128)(2,1)S(1)}, u32[]{:S(2)}, u32[]{:S(2)}) collective-permute-start(bf16[8,64,512]{2,1,0:T(8,128)(2,1)} %get-tuple-element.219), channel_id=1, source_target_pairs={{0,24},{8,16},{16,8},{24,0},{1,25},{9,17},{17,9},{25,1},{2,26},{10... | collective-permute-start | bytes 1572872 | tf_op jit(solution)/shard_map/ppermute | solution.py:75
  24.8 25.2 %collective-permute-start.5 = (bf16[8,64,512]{2,1,0:T(8,128)(2,1)}, bf16[8,64,512]{2,1,0:T(8,128)(2,1)S(1)}, u32[]{:S(2)}, u32[]{:S(2)}) collective-permute-start(bf16[8,64,512]{2,1,0:T(8,128)(2,1)} %get-tuple-element.219), channel_id=1, source_target_pairs={{0,16},{8,24},{16,0},{24,8},{1,17},{9,25},{17,1},{25,9},{2,18},{10... | collective-permute-start | bytes 1572872 | tf_op jit(solution)/shard_map/ppermute | solution.py:75
  26.2 23.8 %collective-permute-start.4 = (bf16[8,64,512]{2,1,0:T(8,128)(2,1)}, bf16[8,64,512]{2,1,0:T(8,128)(2,1)S(1)}, u32[]{:S(2)}, u32[]{:S(2)}) collective-permute-start(bf16[8,64,512]{2,1,0:T(8,128)(2,1)} %get-tuple-element.219), channel_id=1, source_target_pairs={{0,8},{8,0},{16,24},{24,16},{1,9},{9,1},{17,25},{25,17},{2,10},{10... | collective-permute-start | bytes 1572872 | tf_op jit(solution)/shard_map/ppermute | solution.py:75
  30.6 23.3 %copy-start.21 = (f32[4,512]{1,0:T(4,128)}, f32[4,512]{1,0:T(4,128)S(1)}, u32[]{:S(2)}) copy-start(f32[4,512]{1,0:T(4,128)S(1)} %get-tuple-element.415.norm_ref) | copy-start | bytes 24580
  50.2 3.6 %collective-permute-start.7 = (bf16[3,8,64,512]{3,2,1,0:T(8,128)(2,1)S(1)}, bf16[3,8,64,512]{3,2,1,0:T(8,128)(2,1)S(1)}, u32[]{:S(2)}, u32[]{:S(2)}) collective-permute-start(bf16[3,8,64,512]{3,2,1,0:T(8,128)(2,1)S(1)} %pad_maximum_fusion), channel_id=1, source_target_pairs={{0,1},{1,0},{2,3},{3,2},{4,5},{5,4},{6,7},{7,6},{8,9},{9,8},{10,11... | collective-permute-start | bytes 4718600 | tf_op jit(solution)/shard_map/ppermute | solution.py:75
  50.3 13.7 %collective-permute-start.10 = (bf16[4,64,512]{2,1,0:T(8,128)(2,1)S(1)}, bf16[4,64,512]{2,1,0:T(8,128)(2,1)S(1)}, u32[]{:S(2)}, u32[]{:S(2)}) collective-permute-start(bf16[4,64,512]{2,1,0:T(8,128)(2,1)S(1)} %copy-done.46), channel_id=1, source_target_pairs={{0,24},{8,16},{16,8},{24,0},{1,25},{9,17},{17,9},{25,1},{2,26},{10... | collective-permute-start | bytes 786440 | tf_op jit(solution)/shard_map/ppermute | solution.py:75
  51.9 13.7 %collective-permute-start.9 = (bf16[4,64,512]{2,1,0:T(8,128)(2,1)S(1)}, bf16[4,64,512]{2,1,0:T(8,128)(2,1)S(1)}, u32[]{:S(2)}, u32[]{:S(2)}) collective-permute-start(bf16[4,64,512]{2,1,0:T(8,128)(2,1)S(1)} %copy-done.46), channel_id=1, source_target_pairs={{0,16},{8,24},{16,0},{24,8},{1,17},{9,25},{17,1},{25,9},{2,18},{10... | collective-permute-start | bytes 786440 | tf_op jit(solution)/shard_map/ppermute | solution.py:75
  53.2 12.3 %collective-permute-start.8 = (bf16[4,64,512]{2,1,0:T(8,128)(2,1)S(1)}, bf16[4,64,512]{2,1,0:T(8,128)(2,1)S(1)}, u32[]{:S(2)}, u32[]{:S(2)}) collective-permute-start(bf16[4,64,512]{2,1,0:T(8,128)(2,1)S(1)} %copy-done.46), channel_id=1, source_target_pairs={{0,8},{8,0},{16,24},{24,16},{1,9},{9,1},{17,25},{25,17},{2,10},{10... | collective-permute-start | bytes 786440 | tf_op jit(solution)/shard_map/ppermute | solution.py:75
  53.9 11.9 %copy-start.45 = (bf16[8,64,512]{2,1,0:T(8,128)(2,1)S(1)}, bf16[8,64,512]{2,1,0:T(8,128)(2,1)}, u32[]{:S(2)}) copy-start(bf16[8,64,512]{2,1,0:T(8,128)(2,1)} %get-tuple-element.240) | copy-start | bytes 1572868
  53.9 15.4 %copy-start.33 = (bf16[4,128,512]{2,1,0:T(8,128)(2,1)S(1)}, bf16[4,128,512]{2,1,0:T(8,128)(2,1)}, u32[]{:S(2)}) copy-start(bf16[4,128,512]{2,1,0:T(8,128)(2,1)} %get-tuple-element.242.refs_0_) | copy-start | bytes 1572868
  64.0 15.3 %copy-start.39 = (f32[1024,512]{1,0:T(8,128)}, f32[1024,512]{1,0:T(8,128)S(1)}, u32[]{:S(2)}) copy-start(f32[1024,512]{1,0:T(8,128)S(1)} %get-tuple-element.241.x_ref) | copy-start | bytes 6291460
  64.0 15.3 %copy-start.14 = (bf16[4,64,512]{2,1,0:T(8,128)(2,1)}, bf16[4,64,512]{2,1,0:T(8,128)(2,1)S(1)}, u32[]{:S(2)}) copy-start(bf16[4,64,512]{2,1,0:T(8,128)(2,1)S(1)} %collective-permute-done.10.refs_3_) | copy-start | bytes 786436
  65.6 13.8 %copy-start.16 = (bf16[4,64,512]{2,1,0:T(8,128)(2,1)}, bf16[4,64,512]{2,1,0:T(8,128)(2,1)S(1)}, u32[]{:S(2)}) copy-start(bf16[4,64,512]{2,1,0:T(8,128)(2,1)S(1)} %collective-permute-done.9.refs_2_) | copy-start | bytes 786436
  65.6 13.8 %copy-start.18 = (bf16[4,64,512]{2,1,0:T(8,128)(2,1)}, bf16[4,64,512]{2,1,0:T(8,128)(2,1)S(1)}, u32[]{:S(2)}) copy-start(bf16[4,64,512]{2,1,0:T(8,128)(2,1)S(1)} %collective-permute-done.8.refs_1_) | copy-start | bytes 786436
  65.7 3.6 %collective-permute-start.11 = (bf16[3,4,64,512]{3,2,1,0:T(8,128)(2,1)S(1)}, bf16[3,4,64,512]{3,2,1,0:T(8,128)(2,1)S(1)}, u32[]{:S(2)}, u32[]{:S(2)}) collective-permute-start(bf16[3,4,64,512]{3,2,1,0:T(8,128)(2,1)S(1)} %pad_maximum_fusion.3), channel_id=1, source_target_pairs={{0,1},{1,0},{2,3},{3,2},{4,5},{5,4},{6,7},{7,6},{8,9},{9,8},{10,11... | collective-permute-start | bytes 2359304 | tf_op jit(solution)/shard_map/ppermute | solution.py:75
  65.8 15.7 %collective-permute-start.14 = (bf16[8,64,512]{2,1,0:T(8,128)(2,1)S(1)}, bf16[8,64,512]{2,1,0:T(8,128)(2,1)S(1)}, u32[]{:S(2)}, u32[]{:S(2)}) collective-permute-start(bf16[8,64,512]{2,1,0:T(8,128)(2,1)S(1)} %copy-done.45), channel_id=1, source_target_pairs={{0,24},{8,16},{16,8},{24,0},{1,25},{9,17},{17,9},{25,1},{2,26},{10... | collective-permute-start | bytes 1572872 | tf_op jit(solution)/shard_map/ppermute | solution.py:75
  67.3 24.9 %collective-permute-start.13 = (bf16[8,64,512]{2,1,0:T(8,128)(2,1)S(1)}, bf16[8,64,512]{2,1,0:T(8,128)(2,1)S(1)}, u32[]{:S(2)}, u32[]{:S(2)}) collective-permute-start(bf16[8,64,512]{2,1,0:T(8,128)(2,1)S(1)} %copy-done.45), channel_id=1, source_target_pairs={{0,16},{8,24},{16,0},{24,8},{1,17},{9,25},{17,1},{25,9},{2,18},{10... | collective-permute-start | bytes 1572872 | tf_op jit(solution)/shard_map/ppermute | solution.py:75
  68.7 23.5 %collective-permute-start.12 = (bf16[8,64,512]{2,1,0:T(8,128)(2,1)S(1)}, bf16[8,64,512]{2,1,0:T(8,128)(2,1)S(1)}, u32[]{:S(2)}, u32[]{:S(2)}) collective-permute-start(bf16[8,64,512]{2,1,0:T(8,128)(2,1)S(1)} %copy-done.45), channel_id=1, source_target_pairs={{0,8},{8,0},{16,24},{24,16},{1,9},{9,1},{17,25},{25,17},{2,10},{10... | collective-permute-start | bytes 1572872 | tf_op jit(solution)/shard_map/ppermute | solution.py:75
  79.4 14.4 %copy-start.43 = (f32[1,1,4,256]{3,1,2,0:T(1,128)S(1)}, f32[1,1,4,256]{3,1,2,0:T(1,128)}, u32[]{:S(2)}) copy-start(f32[1,1,4,256]{3,1,2,0:T(1,128)} %copy-done.42) | copy-start | bytes 12292
  81.5 16.0 %copy-start = (bf16[8,64,512]{2,1,0:T(8,128)(2,1)}, bf16[8,64,512]{2,1,0:T(8,128)(2,1)S(1)}, u32[]{:S(2)}) copy-start(bf16[8,64,512]{2,1,0:T(8,128)(2,1)S(1)} %collective-permute-done.14.refs_3_) | copy-start | bytes 1572868
  93.7 3.8 %collective-permute-start.15 = (bf16[3,8,64,512]{3,2,1,0:T(8,128)(2,1)}, bf16[3,8,64,512]{3,2,1,0:T(8,128)(2,1)}, u32[]{:S(2)}, u32[]{:S(2)}) collective-permute-start(bf16[3,8,64,512]{3,2,1,0:T(8,128)(2,1)} %pad_maximum_fusion.1), channel_id=1, source_target_pairs={{0,1},{1,0},{2,3},{3,2},{4,5},{5,4},{6,7},{7,6},{8,9},{9,8},{10,11... | collective-permute-start | bytes 4718600 | tf_op jit(solution)/shard_map/ppermute | solution.py:75
  97.5 11.4 %copy-start.13 = (bf16[1024,64]{1,0:T(8,128)(2,1)S(1)}, bf16[1024,64]{1,0:T(8,128)(2,1)}, u32[]{:S(2)}) copy-start(bf16[1024,64]{1,0:T(8,128)(2,1)} %copy-done.12) | copy-start | bytes 393220
  132.7 11.4 %collective-permute-start.17 = (bf16[4,9,64,512]{3,2,1,0:T(8,128)(2,1)S(1)}, bf16[4,9,64,512]{3,2,1,0:T(8,128)(2,1)S(1)}, u32[]{:S(2)}, u32[]{:S(2)}) collective-permute-start(bf16[4,9,64,512]{3,2,1,0:T(8,128)(2,1)S(1)} %get-tuple-element.263), channel_id=1, source_target_pairs={{0,1},{1,0},{2,3},{3,2},{4,5},{5,4},{6,7},{7,6},{8,9},{9,8},{10,11... | collective-permute-start | bytes 7077896 | tf_op jit(solution)/shard_map/ppermute | solution.py:75
  145.6 14.3 %collective-permute-start.18 = (bf16[2,4,64,512]{3,2,1,0:T(8,128)(2,1)S(1)}, bf16[2,4,64,512]{3,2,1,0:T(8,128)(2,1)S(1)}, u32[]{:S(2)}, u32[]{:S(2)}) collective-permute-start(bf16[2,4,64,512]{3,2,1,0:T(8,128)(2,1)S(1)} %get-tuple-element.272), channel_id=1, source_target_pairs={{0,8},{8,0},{16,24},{24,16},{1,9},{9,1},{17,25},{25,17},{2,10},{10... | collective-permute-start | bytes 1572872 | tf_op jit(solution)/shard_map/ppermute | solution.py:75
  147.1 16.7 %collective-permute-start.19 = (bf16[2,5,64,512]{3,2,1,0:T(8,128)(2,1)S(1)}, bf16[2,5,64,512]{3,2,1,0:T(8,128)(2,1)S(1)}, u32[]{:S(2)}, u32[]{:S(2)}) collective-permute-start(bf16[2,5,64,512]{3,2,1,0:T(8,128)(2,1)S(1)} %get-tuple-element.274), channel_id=1, source_target_pairs={{0,16},{8,24},{16,0},{24,8},{1,17},{9,25},{17,1},{25,9},{2,18},{10... | collective-permute-start | bytes 1966088 | tf_op jit(solution)/shard_map/ppermute | solution.py:75
  164.9 11.4 %collective-permute-start.20 = (bf16[4,64,512]{2,1,0:T(8,128)(2,1)S(1)}, bf16[4,64,512]{2,1,0:T(8,128)(2,1)S(1)}, u32[]{:S(2)}, u32[]{:S(2)}) collective-permute-start(bf16[4,64,512]{2,1,0:T(8,128)(2,1)S(1)} %get-tuple-element.283), channel_id=1, source_target_pairs={{0,16},{8,24},{16,0},{24,8},{1,17},{9,25},{17,1},{25,9},{2,18},{10... | collective-permute-start | bytes 786440 | tf_op jit(solution)/shard_map/ppermute | solution.py:75
  165.6 10.7 %collective-permute-start.21 = (bf16[5,64,512]{2,1,0:T(8,128)(2,1)S(1)}, bf16[5,64,512]{2,1,0:T(8,128)(2,1)S(1)}, u32[]{:S(2)}, u32[]{:S(2)}) collective-permute-start(bf16[5,64,512]{2,1,0:T(8,128)(2,1)S(1)} %get-tuple-element.285), channel_id=1, source_target_pairs={{0,8},{8,0},{16,24},{24,16},{1,9},{9,1},{17,25},{25,17},{2,10},{10... | collective-permute-start | bytes 983048 | tf_op jit(solution)/shard_map/ppermute | solution.py:75
  176.2 7.6 %collective-permute-start.23 = (bf16[4,9,64,512]{3,2,1,0:T(8,128)(2,1)S(1)}, bf16[4,9,64,512]{3,2,1,0:T(8,128)(2,1)S(1)}, u32[]{:S(2)}, u32[]{:S(2)}) collective-permute-start(bf16[4,9,64,512]{3,2,1,0:T(8,128)(2,1)S(1)} %get-tuple-element.293), channel_id=1, source_target_pairs={{0,1},{1,0},{2,3},{3,2},{4,5},{5,4},{6,7},{7,6},{8,9},{9,8},{10,11... | collective-permute-start | bytes 7077896 | tf_op jit(solution)/shard_map/ppermute | solution.py:75
  177.7 22.2 %collective-permute-start.22 = (bf16[9,32,512]{2,1,0:T(8,128)(2,1)}, bf16[9,32,512]{2,1,0:T(8,128)(2,1)}, u32[]{:S(2)}, u32[]{:S(2)}) collective-permute-start(bf16[9,32,512]{2,1,0:T(8,128)(2,1)} %get-tuple-element.299), channel_id=1, source_target_pairs={{0,4},{1,5},{2,6},{3,7},{4,0},{5,1},{6,2},{7,3},{8,12},{9,13},{10,... | collective-permute-start | bytes 884744 | tf_op jit(solution)/shard_map/ppermute | solution.py:75
  183.5 16.4 %collective-permute-start.26 = (bf16[4,3,64,512]{3,2,1,0:T(8,128)(2,1)S(1)}, bf16[4,3,64,512]{3,2,1,0:T(8,128)(2,1)S(1)}, u32[]{:S(2)}, u32[]{:S(2)}) collective-permute-start(bf16[4,3,64,512]{3,2,1,0:T(8,128)(2,1)S(1)} %get-tuple-element.304), channel_id=1, source_target_pairs={{0,1},{1,0},{2,3},{3,2},{4,5},{5,4},{6,7},{7,6},{8,9},{9,8},{10,11... | collective-permute-start | bytes 2359304 | tf_op jit(solution)/shard_map/ppermute | solution.py:75
  185.5 14.4 %collective-permute-start.24 = (bf16[2,4,64,512]{3,2,1,0:T(8,128)(2,1)S(1)}, bf16[2,4,64,512]{3,2,1,0:T(8,128)(2,1)S(1)}, u32[]{:S(2)}, u32[]{:S(2)}) collective-permute-start(bf16[2,4,64,512]{3,2,1,0:T(8,128)(2,1)S(1)} %get-tuple-element.308), channel_id=1, source_target_pairs={{0,8},{8,0},{16,24},{24,16},{1,9},{9,1},{17,25},{25,17},{2,10},{10... | collective-permute-start | bytes 1572872 | tf_op jit(solution)/shard_map/ppermute | solution.py:75
  186.4 16.7 %collective-permute-start.25 = (bf16[2,5,64,512]{3,2,1,0:T(8,128)(2,1)S(1)}, bf16[2,5,64,512]{3,2,1,0:T(8,128)(2,1)S(1)}, u32[]{:S(2)}, u32[]{:S(2)}) collective-permute-start(bf16[2,5,64,512]{3,2,1,0:T(8,128)(2,1)S(1)} %get-tuple-element.310), channel_id=1, source_target_pairs={{0,16},{8,24},{16,0},{24,8},{1,17},{9,25},{17,1},{25,9},{2,18},{10... | collective-permute-start | bytes 1966088 | tf_op jit(solution)/shard_map/ppermute | solution.py:75
  209.3 11.0 %collective-permute-start.30 = (bf16[4,4,64,512]{3,2,1,0:T(8,128)(2,1)S(1)}, bf16[4,4,64,512]{3,2,1,0:T(8,128)(2,1)S(1)}, u32[]{:S(2)}, u32[]{:S(2)}) collective-permute-start(bf16[4,4,64,512]{3,2,1,0:T(8,128)(2,1)S(1)} %get-tuple-element.341), channel_id=1, source_target_pairs={{0,1},{1,0},{2,3},{3,2},{4,5},{5,4},{6,7},{7,6},{8,9},{9,8},{10,11... | collective-permute-start | bytes 3145736 | tf_op jit(solution)/shard_map/ppermute | solution.py:75
  209.4 10.9 %collective-permute-start.29 = (bf16[5,64,512]{2,1,0:T(8,128)(2,1)S(1)}, bf16[5,64,512]{2,1,0:T(8,128)(2,1)S(1)}, u32[]{:S(2)}, u32[]{:S(2)}) collective-permute-start(bf16[5,64,512]{2,1,0:T(8,128)(2,1)S(1)} %get-tuple-element.328), channel_id=1, source_target_pairs={{0,8},{8,0},{16,24},{24,16},{1,9},{9,1},{17,25},{25,17},{2,10},{10... | collective-permute-start | bytes 983048 | tf_op jit(solution)/shard_map/ppermute | solution.py:75
  210.6 9.7 %collective-permute-start.27 = (bf16[9,32,512]{2,1,0:T(8,128)(2,1)S(1)}, bf16[9,32,512]{2,1,0:T(8,128)(2,1)S(1)}, u32[]{:S(2)}, u32[]{:S(2)}) collective-permute-start(bf16[9,32,512]{2,1,0:T(8,128)(2,1)S(1)} %get-tuple-element.342.refs_0_), channel_id=1, source_target_pairs={{0,2},{1,3},{2,0},{3,1},{4,6},{5,7},{6,4},{7,5},{8,10},{9,11},{10,... | collective-permute-start | bytes 884744 | tf_op jit(solution)/shard_map/ppermute | solution.py:75
  212.2 8.1 %collective-permute-start.28 = (bf16[4,64,512]{2,1,0:T(8,128)(2,1)S(1)}, bf16[4,64,512]{2,1,0:T(8,128)(2,1)S(1)}, u32[]{:S(2)}, u32[]{:S(2)}) collective-permute-start(bf16[4,64,512]{2,1,0:T(8,128)(2,1)S(1)} %get-tuple-element.326), channel_id=1, source_target_pairs={{0,16},{8,24},{16,0},{24,8},{1,17},{9,25},{17,1},{25,9},{2,18},{10... | collective-permute-start | bytes 786440 | tf_op jit(solution)/shard_map/ppermute | solution.py:75
  222.2 12.8 %collective-permute-start.33 = (bf16[2,4,64,512]{3,2,1,0:T(8,128)(2,1)S(1)}, bf16[2,4,64,512]{3,2,1,0:T(8,128)(2,1)S(1)}, u32[]{:S(2)}, u32[]{:S(2)}) collective-permute-start(bf16[2,4,64,512]{3,2,1,0:T(8,128)(2,1)S(1)} %get-tuple-element.350), channel_id=1, source_target_pairs={{0,16},{8,24},{16,0},{24,8},{1,17},{9,25},{17,1},{25,9},{2,18},{10... | collective-permute-start | bytes 1572872 | tf_op jit(solution)/shard_map/ppermute | solution.py:75
  222.9 10.3 %collective-permute-start.32 = (bf16[2,3,64,512]{3,2,1,0:T(8,128)(2,1)}, bf16[2,3,64,512]{3,2,1,0:T(8,128)(2,1)S(1)}, u32[]{:S(2)}, u32[]{:S(2)}) collective-permute-start(bf16[2,3,64,512]{3,2,1,0:T(8,128)(2,1)} %get-tuple-element.330), channel_id=1, source_target_pairs={{0,8},{8,0},{16,24},{24,16},{1,9},{9,1},{17,25},{25,17},{2,10},{10... | collective-permute-start | bytes 1179656 | tf_op jit(solution)/shard_map/ppermute | solution.py:75
  224.3 8.9 %collective-permute-start.34 = (bf16[9,32,512]{2,1,0:T(8,128)(2,1)}, bf16[9,32,512]{2,1,0:T(8,128)(2,1)S(1)}, u32[]{:S(2)}, u32[]{:S(2)}) collective-permute-start(bf16[9,32,512]{2,1,0:T(8,128)(2,1)} %get-tuple-element.355), channel_id=1, source_target_pairs={{0,2},{1,3},{2,0},{3,1},{4,6},{5,7},{6,4},{7,5},{8,10},{9,11},{10,... | collective-permute-start | bytes 884744 | tf_op jit(solution)/shard_map/ppermute | solution.py:75
  226.5 1.3 collective-permute-start.16
  228.3 3.7 %collective-permute-start.31 = (f32[1,1]{1,0:T(1,128)}, f32[1,1]{1,0:T(1,128)}, u32[]{:S(2)}, u32[]{:S(2)}) collective-permute-start(f32[1,1]{1,0:T(1,128)} %add.15), channel_id=1, source_target_pairs={{0,2},{1,3},{2,0},{3,1},{4,6},{5,7},{6,4},{7,5},{8,10},{9,11},{10,... | collective-permute-start | bytes 20 | tf_op jit(solution)/shard_map/ppermute | solution.py:75
  230.8 16.2 %collective-permute-start.37 = (bf16[9,32,512]{2,1,0:T(8,128)(2,1)S(1)}, bf16[9,32,512]{2,1,0:T(8,128)(2,1)S(1)}, u32[]{:S(2)}, u32[]{:S(2)}) collective-permute-start(bf16[9,32,512]{2,1,0:T(8,128)(2,1)S(1)} %get-tuple-element.364.refs_0_.refs_10_), channel_id=1, source_target_pairs={{0,4},{1,5},{2,6},{3,7},{4,0},{5,1},{6,2},{7,3},{8,12},{9,13},{10,... | collective-permute-start | bytes 884744 | tf_op jit(solution)/shard_map/ppermute | solution.py:75
  232.1 15.0 %collective-permute-start.36 = (bf16[9,32,512]{2,1,0:T(8,128)(2,1)S(1)}, bf16[9,32,512]{2,1,0:T(8,128)(2,1)S(1)}, u32[]{:S(2)}, u32[]{:S(2)}) collective-permute-start(bf16[9,32,512]{2,1,0:T(8,128)(2,1)S(1)} %get-tuple-element.364.refs_0_.refs_10_), channel_id=1, source_target_pairs={{0,1},{1,0},{2,3},{3,2},{4,5},{5,4},{6,7},{7,6},{8,9},{9,8},{10,11... | collective-permute-start | bytes 884744 | tf_op jit(solution)/shard_map/ppermute | solution.py:75
  236.1 10.9 %collective-permute-start.40 = (bf16[4,64,512]{2,1,0:T(8,128)(2,1)S(1)}, bf16[4,64,512]{2,1,0:T(8,128)(2,1)S(1)}, u32[]{:S(2)}, u32[]{:S(2)}) collective-permute-start(bf16[4,64,512]{2,1,0:T(8,128)(2,1)S(1)} %get-tuple-element.368), channel_id=1, source_target_pairs={{0,8},{8,0},{16,24},{24,16},{1,9},{9,1},{17,25},{25,17},{2,10},{10... | collective-permute-start | bytes 786440 | tf_op jit(solution)/shard_map/ppermute | solution.py:75
  237.2 9.8 %collective-permute-start.39 = (bf16[3,64,512]{2,1,0:T(8,128)(2,1)S(1)}, bf16[3,64,512]{2,1,0:T(8,128)(2,1)S(1)}, u32[]{:S(2)}, u32[]{:S(2)}) collective-permute-start(bf16[3,64,512]{2,1,0:T(8,128)(2,1)S(1)} %get-tuple-element.366), channel_id=1, source_target_pairs={{0,16},{8,24},{16,0},{24,8},{1,17},{9,25},{17,1},{25,9},{2,18},{10... | collective-permute-start | bytes 589832 | tf_op jit(solution)/shard_map/ppermute | solution.py:75
  238.2 8.2 %collective-permute-start.35 = (f32[1,1]{1,0:T(1,128)}, f32[1,1]{1,0:T(1,128)}, u32[]{:S(2)}, u32[]{:S(2)}) collective-permute-start(f32[1,1]{1,0:T(1,128)} %add.16), channel_id=1, source_target_pairs={{0,4},{1,5},{2,6},{3,7},{4,0},{5,1},{6,2},{7,3},{8,12},{9,13},{10,... | collective-permute-start | bytes 20 | tf_op jit(solution)/shard_map/ppermute | solution.py:75
  247.8 18.2 %collective-permute-start.41 = (bf16[7,64,512]{2,1,0:T(8,128)(2,1)S(1)}, bf16[7,64,512]{2,1,0:T(8,128)(2,1)S(1)}, u32[]{:S(2)}, u32[]{:S(2)}) collective-permute-start(bf16[7,64,512]{2,1,0:T(8,128)(2,1)S(1)} %sum_round.17.refs_0_), channel_id=1, source_target_pairs={{0,2},{1,3},{2,0},{3,1},{4,6},{5,7},{6,4},{7,5},{8,10},{9,11},{10,... | collective-permute-start | bytes 1376264 | tf_op jit(solution)/shard_map/ppermute | solution.py:75
  247.9 15.9 %collective-permute-start.42 = (bf16[9,32,512]{2,1,0:T(8,128)(2,1)S(1)}, bf16[9,32,512]{2,1,0:T(8,128)(2,1)S(1)}, u32[]{:S(2)}, u32[]{:S(2)}) collective-permute-start(bf16[9,32,512]{2,1,0:T(8,128)(2,1)S(1)} %get-tuple-element.375.refs_2_), channel_id=1, source_target_pairs={{0,4},{1,5},{2,6},{3,7},{4,0},{5,1},{6,2},{7,3},{8,12},{9,13},{10,... | collective-permute-start | bytes 884744 | tf_op jit(solution)/shard_map/ppermute | solution.py:75
  266.9 21.2 %collective-permute-start.46 = (bf16[7,64,512]{2,1,0:T(8,128)(2,1)S(1)}, bf16[7,64,512]{2,1,0:T(8,128)(2,1)S(1)}, u32[]{:S(2)}, u32[]{:S(2)}) collective-permute-start(bf16[7,64,512]{2,1,0:T(8,128)(2,1)S(1)} %get-tuple-element.381.refs_0_), channel_id=1, source_target_pairs={{0,4},{1,5},{2,6},{3,7},{4,0},{5,1},{6,2},{7,3},{8,12},{9,13},{10,... | collective-permute-start | bytes 1376264 | tf_op jit(solution)/shard_map/ppermute | solution.py:75
  268.1 15.1 %collective-permute-start.44 = (bf16[9,32,512]{2,1,0:T(8,128)(2,1)S(1)}, bf16[9,32,512]{2,1,0:T(8,128)(2,1)S(1)}, u32[]{:S(2)}, u32[]{:S(2)}) collective-permute-start(bf16[9,32,512]{2,1,0:T(8,128)(2,1)S(1)} %get-tuple-element.377.refs_4_.refs_6_), channel_id=1, source_target_pairs={{0,2},{1,3},{2,0},{3,1},{4,6},{5,7},{6,4},{7,5},{8,10},{9,11},{10,... | collective-permute-start | bytes 884744 | tf_op jit(solution)/shard_map/ppermute | solution.py:75
  268.2 15.1 %collective-permute-start.43 = (bf16[9,32,512]{2,1,0:T(8,128)(2,1)S(1)}, bf16[9,32,512]{2,1,0:T(8,128)(2,1)S(1)}, u32[]{:S(2)}, u32[]{:S(2)}) collective-permute-start(bf16[9,32,512]{2,1,0:T(8,128)(2,1)S(1)} %get-tuple-element.377.refs_4_.refs_6_), channel_id=1, source_target_pairs={{0,1},{1,0},{2,3},{3,2},{4,5},{5,4},{6,7},{7,6},{8,9},{9,8},{10,11... | collective-permute-start | bytes 884744 | tf_op jit(solution)/shard_map/ppermute | solution.py:75
  288.8 2.7 collective-permute-start.47
  288.9 2.2 collective-permute-start.38
  289.4 2.1 collective-permute-start.45
  292.2 4.4 %collective-permute-start.50 = (f32[1,2]{1,0:T(1,128)S(1)}, f32[1,2]{1,0:T(1,128)S(1)}, u32[]{:S(2)}, u32[]{:S(2)}) collective-permute-start(f32[1,2]{1,0:T(1,128)S(1)} %square_sum.1.refs_0_), channel_id=1, source_target_pairs={{0,24},{8,16},{16,8},{24,0},{1,25},{9,17},{17,9},{25,1},{2,26},{10... | collective-permute-start | bytes 32 | tf_op jit(solution)/shard_map/ppermute | solution.py:75
  293.7 3.5 %collective-permute-start.49 = (f32[1,2]{1,0:T(1,128)S(1)}, f32[1,2]{1,0:T(1,128)S(1)}, u32[]{:S(2)}, u32[]{:S(2)}) collective-permute-start(f32[1,2]{1,0:T(1,128)S(1)} %square_sum.1.refs_0_), channel_id=1, source_target_pairs={{0,16},{8,24},{16,0},{24,8},{1,17},{9,25},{17,1},{25,9},{2,18},{10... | collective-permute-start | bytes 32 | tf_op jit(solution)/shard_map/ppermute | solution.py:75
  294.0 3.5 %collective-permute-start.48 = (f32[1,2]{1,0:T(1,128)S(1)}, f32[1,2]{1,0:T(1,128)S(1)}, u32[]{:S(2)}, u32[]{:S(2)}) collective-permute-start(f32[1,2]{1,0:T(1,128)S(1)} %square_sum.1.refs_0_), channel_id=1, source_target_pairs={{0,8},{8,0},{16,24},{24,16},{1,9},{9,1},{17,25},{25,17},{2,10},{10... | collective-permute-start | bytes 32 | tf_op jit(solution)/shard_map/ppermute | solution.py:75
  (34 other events, 210.7 us)

commit v2 on v1

--- a/solution.py
+++ b/solution.py
@@ -108,7 +108,27 @@
 
 
 def gather_cores(place, ours, *after):
-    return place.to_core(jnp.stack(gates(ours, *after)))
+    items = gates(ours, *after)
+    return place.to_core(stack(items) if items[0].shape[0] % 4 == 0 else jnp.stack(items))
+
+
+def stack(items):
+    def kernel(*refs):
+        for n, ref in enumerate(refs[:-1]):
+            refs[-1][n] = ref[...]
+
+    few, rows, width = items[0].shape
+    part = pl.BlockSpec((few // 2, rows, width), lambda i: (i, 0, 0))
+    return pl.pallas_call(
+        kernel,
+        grid=(2,),
+        in_specs=[part] * len(items),
+        out_specs=pl.BlockSpec((len(items), few // 2, rows, width), lambda i: (0, i, 0, 0)),
+        out_shape=jax.ShapeDtypeStruct((len(items), few, rows, width), items[0].dtype),
+        compiler_params=params(12),
+        cost_estimate=cost(10**5, 10**5),
+        name="stack",
+    )(*items)
 
 
 def gates(items, *after):
@@ -462,7 +482,7 @@
         in_specs=[SMEM, whole((n, P_SIZE)), whole((n, 1))] + [ANY] * sources,
         out_specs=[whole((n, D)), whole((n, P_SIZE)), whole((P_SIZE, D)), whole((16, D))],
         out_shape=[
-            jax.ShapeDtypeStruct((n, D), F32),
+            pltpu.HBM((n, D), F32),
             jax.ShapeDtypeStruct((n, P_SIZE), BF16),
             jax.ShapeDtypeStruct((P_SIZE, D), BF16),
             jax.ShapeDtypeStruct((16, D), F32),
@@ -475,7 +495,7 @@
         compiler_params=params(),
         cost_estimate=cost(2 * n * D * P_SIZE, n * D * 5),
         name="embed_step",
-    )(where, target, maskf, *group)
+    )(where, target, maskf, in_hbm(group[0]), *group[1:])
 
 
 def copies_of(group):
@@ -583,7 +603,7 @@
         compiler_params=params(),
         cost_estimate=cost(2 * n * D * (4 * D + 2 * LEN), n * D * 20, n * H * LEN),
         name="attn_fwd",
-    )(where, x, norms, *group)
+    )(where, x, norms, in_hbm(group[0]), *group[1:])
 
 
 def gelu_pair(u):
@@ -1020,13 +1040,13 @@
     )(where, a, dqkv, *small)
 
 
-def adam(weight, first, second, grad, rate):
-    first = BETA_ONE * first + (1 - BETA_ONE) * grad
-    second = BETA_TWO * second + (1 - BETA_TWO) * grad * grad
-    spread = second * (1 / (1 - BETA_TWO**STEP_COUNT))
-    lower = 1.0 / (spread * lax.rsqrt(spread) + ADAM_EPS)
-    weight = weight * (1 - rate * DECAY) - first * lower * (rate / (1 - BETA_ONE**STEP_COUNT))
-    return (weight, first, second)
+def adam(weight, first, second, tenth, rate):
+    scale = (1 - BETA_ONE**STEP_COUNT) / rate
+    first = BETA_ONE * first + tenth
+    second = BETA_TWO * second + tenth * ((1 - BETA_TWO) / (1 - BETA_ONE) ** 2) * tenth
+    spread = second * (scale * scale / (1 - BETA_TWO**STEP_COUNT))
+    step = first * (1.0 / (spread * lax.rsqrt(spread) + ADAM_EPS * scale))
+    return (weight * (1 - rate * DECAY) - step, first, second)
 
 
 def fetch(arrays, where):
@@ -1086,7 +1106,7 @@
         norm = jnp.sqrt(sums[:, 1:2])
         loss_ref[...] = sums[:, 0:1] / count
         norm_ref[...] = norm
-        scale = CLIP / jnp.maximum(norm, CLIP)
+        scale = (1 - BETA_ONE) * CLIP / jnp.maximum(norm, CLIP)
         own = where_ref[1] == h
 
         def update(n, at, grad, rate):
@@ -1216,7 +1236,8 @@
     saved = []
     for index in range(L):
         norms = norms_all[4 * index : 4 * index + 4]
-        mid, qkv, pt, ot = attn_fwd(place, where, x, norms, attn_groups[index])
+        held = in_hbm(x) if index == 0 else x
+        mid, qkv, pt, ot = attn_fwd(place, where, held, norms, attn_groups[index])
         held = mid
         if index + 1 < L:
             got = gates(ours_mlp, mid)
@@ -1281,13 +1302,13 @@
     token = advance([one], dmid)
     token = two.begin(*grads_mlp(0, du, gate(c, token), dm, dh), (0, 4, 0), (4, 5, 1))
     token = advance([one], token)
-    token = ahead.begin(*grad_qkv(place, where, gate(a_one, token), dqkv_one), (0, 3, 0))
+    token = ahead.begin(*grad_qkv(place, where, gate(a_one, token), dqkv_one), (0, 3, 1))
     token = advance([two], token)
     grad, dqkv, a = backward_attn(0, gate(dmid, token), dh)
     token = sum_round(where, [one, two, ahead], grad)
     small = [inputs, grad, g_head]
     small += [norm_grads[i, k] for i in range(L) for k in range(2)] + [dn_final]
-    token = end.begin(*grad_qkv(place, where, gate(a, token), dqkv, small), (0, 4, 1))
+    token = end.begin(*grad_qkv(place, where, gate(a, token), dqkv, small), (0, 4, 0))
     one.launch()
     two.launch()
     ahead.launch()

time: 310 us -> 309 us (level)
  transfers between devices with their start and end apart: 51 -> 51, of which waited for: 26 -> 26; matrix products, arithmetic and copies ran while one was open for 1% -> 1% of each run, Pallas kernels for 32% -> 33%
where the time goes in v2:
time: 309 us; the launch traced here: 308 us
  Pallas kernels  163 us (53%)
  waiting for transfers between devices  91.6 us (30%)
  starting transfers between devices  45.4 us (15%)
  between operations  4.31 us (1%)
    ppermute x51, waiting for transfers between devices, permute(): return lax.ppermute(x, axis, [(i, i ^ mask) for i in range(size)])  91.6 us
    ppermute x51, starting transfers between devices, permute(): return lax.ppermute(x, axis, [(i, i ^ mask) for i in range(size)])  45.4 us
    pallas_call x2, Pallas kernels, attn_bwd(): pl.pallas_call(kernel, grid=(seqs,), in_specs=[SMEM, row(D), row(D), row(...  23.4 us
    pallas_call x2, Pallas kernels, attn_fwd(): pl.pallas_call(kernel, grid=(seqs // SP,), in_specs=[SMEM, pl.BlockSpec((...  22.5 us
    pallas_call x2, Pallas kernels, mlp_fwd(): pl.pallas_call(kernel, grid=(n // tall,), in_specs=[SMEM, row(D), whole((...  21.4 us
    pallas_call x2, Pallas kernels, mlp_bwd(): pl.pallas_call(kernel, grid=(n // LEN,), in_specs=[SMEM, row(D), row(D),...  19.6 us
    pallas_call x2, Pallas kernels, grad_mlp(): pl.pallas_call(kernel, grid=(2 * steps + 1,), in_specs=[SMEM, whole((n, D...  18.7 us
    pallas_call x10, Pallas kernels, combine(): pl.pallas_call(kernel, grid=(2,), in_specs=[SMEM] + [block(a.shape) for a...  13.4 us
  transfers between devices with their start and end apart: 51, of which 26 were waited for; matrix products, arithmetic and copies ran while one was open for 1% of the time, Pallas kernels for 33%

profile of v2, /device:TPU:0, one launch (start us, length us, event | category | flops | bytes accessed | tf_op | source)
XLA Modules:
  0.0 308.4 jit_solution(16530294826901912489)
XLA Ops:
  0.8 2.3 pack.5
  3.1 3.9 %collective-permute-start.2 = (bf16[5,64,512]{2,1,0:T(8,128)(2,1)}, bf16[5,64,512]{2,1,0:T(8,128)(2,1)S(1)}, u32[]{:S(2)}, u32[]{:S(2)}) collective-permute-start(bf16[5,64,512]{2,1,0:T(8,128)(2,1)} %get-tuple-element.218), channel_id=1, source_target_pairs={{0,24},{8,16},{16,8},{24,0},{1,25},{9,17},{17,9},{25,1},{2,26},{10... | collective-permute-start | bytes 983048 | tf_op jit(solution)/shard_map/ppermute | solution.py:75
  7.9 2.2 pack.6
  10.1 2.8 pack.7
  12.9 2.8 pack.4
  15.8 6.1 %collective-permute-done.1.refs_2_ = bf16[5,64,512]{2,1,0:T(8,128)(2,1)S(1)} collective-permute-done((bf16[5,64,512]{2,1,0:T(8,128)(2,1)}, bf16[5,64,512]{2,1,0:T(8,128)(2,1)S(1)}, u32[]{:S(2)}, u32[]{:S(2)}) %collective-permute-start.1) | collective-permute-done | bytes 327712 | tf_op jit(solution)/shard_map/ppermute | solution.py:75
  23.3 1.6 collective-permute-start.6
  24.8 1.4 collective-permute-start.5
  27.0 3.6 %embed_step.1 = (f32[1024,512]{1,0:T(8,128)}, bf16[1024,64]{1,0:T(8,128)(2,1)S(1)}, bf16[64,512]{1,0:T(8,128)(2,1)S(1)}, f32[16,512]{1,0:T(8,128)S(1)}) custom-call(s32[6]{0:T(128)S(1)} %stack.42.where_ref, bf16[1024,64]{1,0:T(8,128)(2,1)S(1)} %reshape.110.target_ref, f32[1024,1]{1,0:T(8,128)S(1)} %copy.40.mask_ref, ...), custom_call_target="tpu_custom_call" | custom-call | flops 2013265920 | bytes 78643200 | tf_op jit(solution)/shard_map/embed_step/pallas_call | solution.py:479
  30.7 11.6 %attn_fwd.2 = (f32[1024,512]{1,0:T(8,128)}, bf16[1024,1536]{1,0:T(8,128)(2,1)}, bf16[4,8,256,256]{3,2,1,0:T(8,128)(2,1)}, bf16[4,512,256]{2,1,0:T(8,128)(2,1)}) custom-call(s32[6]{0:T(128)S(1)} %stack.42.where_ref, f32[1024,512]{1,0:T(8,128)} %get-tuple-element.227.x_ref, f32[4,512]{1,0:T(4,128)S(1)} %get-tuple-element.415.norm_ref, ...), custom_call_target="tpu_custom_call" | custom-call | flops 80530636800 | bytes 314572800 | tf_op jit(solution)/shard_map/attn_fwd/pallas_call | solution.py:582
  42.4 7.6 %collective-permute-done.5.refs_1_.refs_2_ = bf16[8,64,512]{2,1,0:T(8,128)(2,1)S(1)} collective-permute-done((bf16[8,64,512]{2,1,0:T(8,128)(2,1)}, bf16[8,64,512]{2,1,0:T(8,128)(2,1)S(1)}, u32[]{:S(2)}, u32[]{:S(2)}) %collective-permute-start.5) | collective-permute-done | bytes 524320 | tf_op jit(solution)/shard_map/ppermute | solution.py:75
  50.4 1.5 collective-permute-start.10
  51.9 1.4 collective-permute-start.9
  54.0 10.0 %mlp_fwd.2 = (f32[1024,512]{1,0:T(8,128)S(1)}, bf16[1024,2048]{1,0:T(8,128)(2,1)}, bf16[1024,2048]{1,0:T(8,128)(2,1)}) custom-call(s32[6]{0:T(128)S(1)} %stack.42.where_ref, f32[1024,512]{1,0:T(8,128)} %get-tuple-element.234.mid_ref, f32[4,512]{1,0:T(4,128)S(1)} %get-tuple-element.415.norm_ref, bf16[8,128,512]{2,1,0:T(8,128)(2,1)S(1)} %copy-done.32, ...), custom_call_target="tpu_custom_call" | custom-call | flops 128849018880 | bytes 377487360 | tf_op jit(solution)/shard_map/mlp_fwd/pallas_call | solution.py:657
  64.1 1.6 collective-permute-done.9.refs_1_.refs_2_
  65.9 1.5 collective-permute-start.14
  67.4 1.4 collective-permute-start.13
  69.4 10.8 %attn_fwd.3 = (f32[1024,512]{1,0:T(8,128)}, bf16[1024,1536]{1,0:T(8,128)(2,1)}, bf16[4,8,256,256]{3,2,1,0:T(8,128)(2,1)}, bf16[4,512,256]{2,1,0:T(8,128)(2,1)}) custom-call(s32[6]{0:T(128)S(1)} %stack.42.where_ref, f32[1024,512]{1,0:T(8,128)S(1)} %get-tuple-element.241.x_ref, f32[4,512]{1,0:T(4,128)S(1)} %get-tuple-element.414.norm_ref, ...), custom_call_target="tpu_custom_call" | custom-call | flops 80530636800 | bytes 314572800 | tf_op jit(solution)/shard_map/attn_fwd/pallas_call | solution.py:582
  80.4 1.3 collective-permute-done.14.refs_2_.refs_3_
  81.6 10.7 %collective-permute-done.13.refs_1_.refs_2_ = bf16[8,64,512]{2,1,0:T(8,128)(2,1)S(1)} collective-permute-done((bf16[8,64,512]{2,1,0:T(8,128)(2,1)S(1)}, bf16[8,64,512]{2,1,0:T(8,128)(2,1)S(1)}, u32[]{:S(2)}, u32[]{:S(2)}) %collective-permute-start.13) | collective-permute-done | bytes 524320 | tf_op jit(solution)/shard_map/ppermute | solution.py:75
  94.2 2.6 collective-permute-done.15.refs_4_
  96.8 11.4 %mlp_fwd.3 = (f32[1024,512]{1,0:T(8,128)S(1)}, bf16[1024,2048]{1,0:T(8,128)(2,1)}, bf16[1024,2048]{1,0:T(8,128)(2,1)}) custom-call(s32[6]{0:T(128)S(1)} %stack.42.where_ref, f32[1024,512]{1,0:T(8,128)} %get-tuple-element.246.mid_ref, f32[4,512]{1,0:T(4,128)S(1)} %get-tuple-element.414.norm_ref, bf16[8,128,512]{2,1,0:T(8,128)(2,1)} %get-tuple-element.247.refs_0_, ...), custom_call_target="tpu_custom_call" | custom-call | flops 128849018880 | bytes 377487360 | tf_op jit(solution)/shard_map/mlp_fwd/pallas_call | solution.py:657
  108.2 3.8 %head_step.1 = (f32[1024,512]{1,0:T(8,128)S(1)}, f32[1,64]{1,0:T(1,128)S(1)}, f32[64,512]{1,0:T(8,128)S(1)}, f32[8,512]{1,0:T(8,128)S(1)}) custom-call(f32[1024,512]{1,0:T(8,128)S(1)} %get-tuple-element.251.x_ref, bf16[1024,64]{1,0:T(8,128)(2,1)S(1)} %copy-done.19, f32[1024,1]{1,0:T(8,128)S(1)} %copy.41.mask_ref, ...), custom_call_target="tpu_custom_call" | custom-call | flops 6039797760 | bytes 125829120 | tf_op jit(solution)/shard_map/head_step/pallas_call | solution.py:881
  112.1 10.4 %mlp_bwd.2 = (f32[1024,512]{1,0:T(8,128)S(1)}, bf16[1024,512]{1,0:T(8,128)(2,1)S(1)}, bf16[1024,2048]{1,0:T(8,128)(2,1)}, bf16[1024,512]{1,0:T(8,128)(2,1)S(1)},...) custom-call(s32[6]{0:T(128)S(1)} %stack.42.where_ref, f32[1024,512]{1,0:T(8,128)S(1)} %get-tuple-element.254.dz_ref, ...), custom_call_target="tpu_custom_call" | custom-call | flops 128849018880 | bytes 503316480 | tf_op jit(solution)/shard_map/mlp_bwd/pallas_call | solution.py:724
  122.5 9.5 %grad_mlp.2 = (bf16[4,9,64,512]{3,2,1,0:T(8,128)(2,1)S(1)}, bf16[4,9,64,512]{3,2,1,0:T(8,128)(2,1)S(1)}) custom-call(s32[6]{0:T(128)S(1)} %stack.42.where_ref, bf16[1024,512]{1,0:T(8,128)(2,1)S(1)} %get-tuple-element.256.c_ref, bf16[1024,2048]{1,0:T(8,128)(2,1)} %get-tuple-element.257.du_ref, bf16[1024,2048]{1,0:T(8,128)(2,1)} %get-tuple-element.258.act_ref, ...), custom_call_target="tpu_custom_call" | custom-call | flops 128849018880 | bytes 440401920 | tf_op jit(solution)/shard_map/grad_mlp/pallas_call | solution.py:952
  132.3 11.1 %attn_bwd.2 = (f32[1024,512]{1,0:T(8,128)S(1)}, bf16[1024,1536]{1,0:T(8,128)(2,1)S(1)}, bf16[1024,512]{1,0:T(8,128)(2,1)S(1)}, f32[8,512]{1,0:T(8,128)S(1)}) custom-call(s32[6]{0:T(128)S(1)} %stack.42.where_ref, f32[1024,512]{1,0:T(8,128)S(1)} %get-tuple-element.265.dmid_ref, bf16[1024,512]{1,0:T(8,128)(2,1)S(1)} %get-tuple-element.261.dh_ref, ...), custom_call_target="tpu_custom_call" | custom-call | flops 104689827840 | bytes 503316480 | tf_op jit(solution)/shard_map/attn_bwd/pallas_call | solution.py:821
  143.5 1.5 sum_round.10
  145.0 1.4 collective-permute-start.18
  147.1 9.2 %mlp_bwd.3 = (f32[1024,512]{1,0:T(8,128)S(1)}, bf16[1024,512]{1,0:T(8,128)(2,1)S(1)}, bf16[1024,2048]{1,0:T(8,128)(2,1)}, bf16[1024,512]{1,0:T(8,128)(2,1)S(1)},...) custom-call(s32[6]{0:T(128)S(1)} %stack.42.where_ref, f32[1024,512]{1,0:T(8,128)S(1)} %get-tuple-element.275.dz_ref, ...), custom_call_target="tpu_custom_call" | custom-call | flops 128849018880 | bytes 503316480 | tf_op jit(solution)/shard_map/mlp_bwd/pallas_call | solution.py:724
  156.4 2.9 collective-permute-done.18.refs_1_
  159.2 3.9 %collective-permute-done.19.refs_3_ = bf16[2,5,64,512]{3,2,1,0:T(8,128)(2,1)S(1)} collective-permute-done((bf16[2,5,64,512]{3,2,1,0:T(8,128)(2,1)S(1)}, bf16[2,5,64,512]{3,2,1,0:T(8,128)(2,1)S(1)}, u32[]{:S(2)}, u32[]{:S(2)}) %collective-permute-start.19) | collective-permute-done | bytes 655392 | tf_op jit(solution)/shard_map/ppermute | solution.py:75
  164.9 1.4 collective-permute-start.21
  166.3 9.2 %grad_mlp.3 = (bf16[4,9,64,512]{3,2,1,0:T(8,128)(2,1)S(1)}, bf16[4,9,64,512]{3,2,1,0:T(8,128)(2,1)S(1)}) custom-call(s32[6]{0:T(128)S(1)} %stack.42.where_ref, bf16[1024,512]{1,0:T(8,128)(2,1)S(1)} %get-tuple-element.287.c_ref, bf16[1024,2048]{1,0:T(8,128)(2,1)} %get-tuple-element.288.du_ref, bf16[1024,2048]{1,0:T(8,128)(2,1)} %get-tuple-element.289.act_ref, ...), custom_call_target="tpu_custom_call" | custom-call | flops 128849018880 | bytes 440401920 | tf_op jit(solution)/shard_map/grad_mlp/pallas_call | solution.py:952
  175.6 1.4 sum_round.12
  177.0 2.6 collective-permute-start.22
  179.6 3.2 %grad_qkv.2 = (bf16[4,3,64,512]{3,2,1,0:T(8,128)(2,1)S(1)}, bf16[4,3,64,512]{3,2,1,0:T(8,128)(2,1)S(1)}) custom-call(s32[6]{0:T(128)S(1)} %stack.42.where_ref, bf16[1024,512]{1,0:T(8,128)(2,1)S(1)} %get-tuple-element.302.a_ref, bf16[1024,1536]{1,0:T(8,128)(2,1)S(1)} %get-tuple-element.303.dqkv_ref), custom_call_target="tpu_custom_call" | custom-call | flops 48318382080 | bytes 173015040 | tf_op jit(solution)/shard_map/grad_qkv/pallas_call | solution.py:1029
  183.2 1.7 sum_round.13
  185.7 1.2 collective-permute-start.25
  187.0 12.3 %attn_bwd.3 = (f32[1024,512]{1,0:T(8,128)S(1)}, bf16[1024,1536]{1,0:T(8,128)(2,1)S(1)}, bf16[1024,512]{1,0:T(8,128)(2,1)S(1)}, f32[8,512]{1,0:T(8,128)S(1)}) custom-call(s32[6]{0:T(128)S(1)} %stack.42.where_ref, f32[1024,512]{1,0:T(8,128)S(1)} %get-tuple-element.312.dmid_ref, bf16[1024,512]{1,0:T(8,128)(2,1)S(1)} %get-tuple-element.292.dh_ref, ...), custom_call_target="tpu_custom_call" | custom-call | flops 104689827840 | bytes 503316480 | tf_op jit(solution)/shard_map/attn_bwd/pallas_call | solution.py:821
  199.3 3.1 %collective-permute-done.25.refs_5_ = bf16[2,5,64,512]{3,2,1,0:T(8,128)(2,1)S(1)} collective-permute-done((bf16[2,5,64,512]{3,2,1,0:T(8,128)(2,1)S(1)}, bf16[2,5,64,512]{3,2,1,0:T(8,128)(2,1)S(1)}, u32[]{:S(2)}, u32[]{:S(2)}) %collective-permute-start.25) | collective-permute-done | bytes 655392 | tf_op jit(solution)/shard_map/ppermute | solution.py:75
  202.4 2.3 sum_round.14
  204.8 3.8 %grad_qkv.3 = (bf16[4,4,64,512]{3,2,1,0:T(8,128)(2,1)S(1)}, bf16[4,4,64,512]{3,2,1,0:T(8,128)(2,1)S(1)}) custom-call(s32[6]{0:T(128)S(1)} %stack.42.where_ref, bf16[1024,512]{1,0:T(8,128)(2,1)S(1)} %get-tuple-element.331.a_ref, bf16[1024,1536]{1,0:T(8,128)(2,1)S(1)} %get-tuple-element.332.dqkv_ref, bf16[1024,64]{1,0:T(8,128)(2,1)S(1)} %copy-done.41, ...), custom_call_target="tpu_custom_call" | custom-call | flops 48318382080 | bytes 173015040 | tf_op jit(solution)/shard_map/grad_qkv/pallas_call | solution.py:1029
  208.7 1.3 collective-permute-start.29
  210.0 1.5 collective-permute-start.27
  212.2 7.4 %collective-permute-done.28.refs_3_ = bf16[4,64,512]{2,1,0:T(8,128)(2,1)S(1)} collective-permute-done((bf16[4,64,512]{2,1,0:T(8,128)(2,1)S(1)}, bf16[4,64,512]{2,1,0:T(8,128)(2,1)S(1)}, u32[]{:S(2)}, u32[]{:S(2)}) %collective-permute-start.28) | collective-permute-done | bytes 262176 | tf_op jit(solution)/shard_map/ppermute | solution.py:75
  219.6 1.9 sum_round.15
  222.4 1.2 collective-permute-start.32
  227.8 2.4 collective-permute-start.31
  232.6 1.8 collective-permute-done.33.refs_3_
  234.4 1.1 sum_round.16
  235.5 1.1 collective-permute-start.40
  237.6 1.6 collective-permute-start.35
  239.2 6.7 %collective-permute-done.35 = f32[1,1]{1,0:T(1,128)} collective-permute-done((f32[1,1]{1,0:T(1,128)}, f32[1,1]{1,0:T(1,128)}, u32[]{:S(2)}, u32[]{:S(2)}) %collective-permute-start.35) | collective-permute-done | bytes 36 | tf_op jit(solution)/shard_map/ppermute | solution.py:75
  247.4 1.3 collective-permute-start.42
  248.6 14.7 %collective-permute-done.42.refs_3_ = bf16[9,32,512]{2,1,0:T(8,128)(2,1)S(1)} collective-permute-done((bf16[9,32,512]{2,1,0:T(8,128)(2,1)S(1)}, bf16[9,32,512]{2,1,0:T(8,128)(2,1)S(1)}, u32[]{:S(2)}, u32[]{:S(2)}) %collective-permute-start.42) | collective-permute-done | bytes 294944 | tf_op jit(solution)/shard_map/ppermute | solution.py:75
  263.3 2.2 collective-permute-done.41.refs_1_
  266.4 1.3 collective-permute-start.46
  267.6 7.1 %fetch.1 = (f32[2,128,1536]{2,1,0:T(8,128)S(1)}, f32[2,128,1536]{2,1,0:T(8,128)S(1)}, f32[2,128,1536]{2,1,0:T(8,128)S(1)}, f32[2,128,512]{2,1,0:T(8,128)S(1)}, f...) custom-call(s32[6]{0:T(128)S(1)} %stack.42.where_ref, ...), custom_call_target="tpu_custom_call" | custom-call | tf_op jit(solution)/shard_map/fetch/pallas_call | solution.py:1064
  274.8 7.9 %collective-permute-done.44.refs_6_.refs_8_ = bf16[9,32,512]{2,1,0:T(8,128)(2,1)S(1)} collective-permute-done((bf16[9,32,512]{2,1,0:T(8,128)(2,1)S(1)}, bf16[9,32,512]{2,1,0:T(8,128)(2,1)S(1)}, u32[]{:S(2)}, u32[]{:S(2)}) %collective-permute-start.44) | collective-permute-done | bytes 294944 | tf_op jit(solution)/shard_map/ppermute | solution.py:75
  282.7 4.9 %collective-permute-done.46.refs_1_ = bf16[7,64,512]{2,1,0:T(8,128)(2,1)S(1)} collective-permute-done((bf16[7,64,512]{2,1,0:T(8,128)(2,1)S(1)}, bf16[7,64,512]{2,1,0:T(8,128)(2,1)S(1)}, u32[]{:S(2)}, u32[]{:S(2)}) %collective-permute-start.46) | collective-permute-done | bytes 458784 | tf_op jit(solution)/shard_map/ppermute | solution.py:75
  289.0 1.6 collective-permute-done.38.refs_3_.refs_13_
  291.7 1.5 collective-permute-start.50
  293.5 1.7 collective-permute-start.48
  297.0 11.2 %adam_step.1 = (f32[2,128,1536]{2,1,0:T(8,128)}, f32[2,128,1536]{2,1,0:T(8,128)}, f32[2,128,1536]{2,1,0:T(8,128)}, f32[2,128,512]{2,1,0:T(8,128)}, f32[2,128,512...) custom-call(s32[6]{0:T(128)S(1)} %stack.42.where_ref, ...), custom_call_target="tpu_custom_call" | custom-call | flops 943718400 | bytes 1132462080 | tf_op jit(solution)/shard_map/adam_step/pallas_call | solution.py:1160
  (182 shorter events, 24.4 us)
Async XLA Ops:
  3.1 12.7 %collective-permute-start.2 = (bf16[5,64,512]{2,1,0:T(8,128)(2,1)}, bf16[5,64,512]{2,1,0:T(8,128)(2,1)S(1)}, u32[]{:S(2)}, u32[]{:S(2)}) collective-permute-start(bf16[5,64,512]{2,1,0:T(8,128)(2,1)} %get-tuple-element.218), channel_id=1, source_target_pairs={{0,24},{8,16},{16,8},{24,0},{1,25},{9,17},{17,9},{25,1},{2,26},{10... | collective-permute-start | bytes 983048 | tf_op jit(solution)/shard_map/ppermute | solution.py:75
  7.0 14.9 %collective-permute-start.1 = (bf16[5,64,512]{2,1,0:T(8,128)(2,1)}, bf16[5,64,512]{2,1,0:T(8,128)(2,1)S(1)}, u32[]{:S(2)}, u32[]{:S(2)}) collective-permute-start(bf16[5,64,512]{2,1,0:T(8,128)(2,1)} %get-tuple-element.218), channel_id=1, source_target_pairs={{0,16},{8,24},{16,0},{24,8},{1,17},{9,25},{17,1},{25,9},{2,18},{10... | collective-permute-start | bytes 983048 | tf_op jit(solution)/shard_map/ppermute | solution.py:75
  7.5 14.7 %collective-permute-start = (bf16[5,64,512]{2,1,0:T(8,128)(2,1)}, bf16[5,64,512]{2,1,0:T(8,128)(2,1)S(1)}, u32[]{:S(2)}, u32[]{:S(2)}) collective-permute-start(bf16[5,64,512]{2,1,0:T(8,128)(2,1)} %get-tuple-element.218), channel_id=1, source_target_pairs={{0,8},{8,0},{16,24},{24,16},{1,9},{9,1},{17,25},{25,17},{2,10},{10... | collective-permute-start | bytes 983048 | tf_op jit(solution)/shard_map/ppermute | solution.py:75
  7.6 19.2 %copy-start.45 = (f32[1,1,4,256]{3,1,2,0:T(1,128)}, f32[1,1,4,256]{3,1,2,0:T(1,128)S(1)}, u32[]{:S(2)}) copy-start(f32[1,1,4,256]{3,1,2,0:T(1,128)S(1)} %copy.42) | copy-start | bytes 12292
  7.8 19.2 %copy-start.18 = (bf16[1024,64]{1,0:T(8,128)(2,1)}, bf16[1024,64]{1,0:T(8,128)(2,1)S(1)}, u32[]{:S(2)}) copy-start(bf16[1024,64]{1,0:T(8,128)(2,1)S(1)} %reshape.110.target_ref) | copy-start | bytes 393220
  15.8 14.9 %copy-start.12 = (bf16[5,64,512]{2,1,0:T(8,128)(2,1)}, bf16[5,64,512]{2,1,0:T(8,128)(2,1)S(1)}, u32[]{:S(2)}) copy-start(bf16[5,64,512]{2,1,0:T(8,128)(2,1)S(1)} %collective-permute-done.2.refs_3_) | copy-start | bytes 983044
  23.3 3.7 %collective-permute-start.3 = (bf16[3,5,64,512]{3,2,1,0:T(8,128)(2,1)}, bf16[3,5,64,512]{3,2,1,0:T(8,128)(2,1)}, u32[]{:S(2)}, u32[]{:S(2)}) collective-permute-start(bf16[3,5,64,512]{3,2,1,0:T(8,128)(2,1)} %pad_maximum_fusion), channel_id=1, source_target_pairs={{0,1},{1,0},{2,3},{3,2},{4,5},{5,4},{6,7},{7,6},{8,9},{9,8},{10,11... | collective-permute-start | bytes 2949128 | tf_op jit(solution)/shard_map/ppermute | solution.py:75
  23.3 19.1 %collective-permute-start.6 = (bf16[8,64,512]{2,1,0:T(8,128)(2,1)}, bf16[8,64,512]{2,1,0:T(8,128)(2,1)S(1)}, u32[]{:S(2)}, u32[]{:S(2)}) collective-permute-start(bf16[8,64,512]{2,1,0:T(8,128)(2,1)} %get-tuple-element.219), channel_id=1, source_target_pairs={{0,24},{8,16},{16,8},{24,0},{1,25},{9,17},{17,9},{25,1},{2,26},{10... | collective-permute-start | bytes 1572872 | tf_op jit(solution)/shard_map/ppermute | solution.py:75
  24.8 25.1 %collective-permute-start.5 = (bf16[8,64,512]{2,1,0:T(8,128)(2,1)}, bf16[8,64,512]{2,1,0:T(8,128)(2,1)S(1)}, u32[]{:S(2)}, u32[]{:S(2)}) collective-permute-start(bf16[8,64,512]{2,1,0:T(8,128)(2,1)} %get-tuple-element.219), channel_id=1, source_target_pairs={{0,16},{8,24},{16,0},{24,8},{1,17},{9,25},{17,1},{25,9},{2,18},{10... | collective-permute-start | bytes 1572872 | tf_op jit(solution)/shard_map/ppermute | solution.py:75
  26.2 23.8 %collective-permute-start.4 = (bf16[8,64,512]{2,1,0:T(8,128)(2,1)}, bf16[8,64,512]{2,1,0:T(8,128)(2,1)S(1)}, u32[]{:S(2)}, u32[]{:S(2)}) collective-permute-start(bf16[8,64,512]{2,1,0:T(8,128)(2,1)} %get-tuple-element.219), channel_id=1, source_target_pairs={{0,8},{8,0},{16,24},{24,16},{1,9},{9,1},{17,25},{25,17},{2,10},{10... | collective-permute-start | bytes 1572872 | tf_op jit(solution)/shard_map/ppermute | solution.py:75
  30.7 23.3 %copy-start.27 = (f32[4,512]{1,0:T(4,128)}, f32[4,512]{1,0:T(4,128)S(1)}, u32[]{:S(2)}) copy-start(f32[4,512]{1,0:T(4,128)S(1)} %get-tuple-element.415.norm_ref) | copy-start | bytes 24580
  42.4 21.6 %copy-start = (bf16[8,64,512]{2,1,0:T(8,128)(2,1)}, bf16[8,64,512]{2,1,0:T(8,128)(2,1)S(1)}, u32[]{:S(2)}) copy-start(bf16[8,64,512]{2,1,0:T(8,128)(2,1)S(1)} %collective-permute-done.6.refs_2_.refs_3_) | copy-start | bytes 1572868
  50.0 14.0 %copy-start.2 = (bf16[8,64,512]{2,1,0:T(8,128)(2,1)}, bf16[8,64,512]{2,1,0:T(8,128)(2,1)S(1)}, u32[]{:S(2)}) copy-start(bf16[8,64,512]{2,1,0:T(8,128)(2,1)S(1)} %collective-permute-done.5.refs_1_.refs_2_) | copy-start | bytes 1572868
  50.1 13.9 %copy-start.4 = (bf16[8,64,512]{2,1,0:T(8,128)(2,1)}, bf16[8,64,512]{2,1,0:T(8,128)(2,1)S(1)}, u32[]{:S(2)}) copy-start(bf16[8,64,512]{2,1,0:T(8,128)(2,1)S(1)} %collective-permute-done.4.refs_0_.refs_1_) | copy-start | bytes 1572868
  50.3 3.6 %collective-permute-start.7 = (bf16[3,8,64,512]{3,2,1,0:T(8,128)(2,1)S(1)}, bf16[3,8,64,512]{3,2,1,0:T(8,128)(2,1)S(1)}, u32[]{:S(2)}, u32[]{:S(2)}) collective-permute-start(bf16[3,8,64,512]{3,2,1,0:T(8,128)(2,1)S(1)} %stack.47), channel_id=1, source_target_pairs={{0,1},{1,0},{2,3},{3,2},{4,5},{5,4},{6,7},{7,6},{8,9},{9,8},{10,11... | collective-permute-start | bytes 4718600 | tf_op jit(solution)/shard_map/ppermute | solution.py:75
  50.4 13.6 %collective-permute-start.10 = (bf16[4,64,512]{2,1,0:T(8,128)(2,1)S(1)}, bf16[4,64,512]{2,1,0:T(8,128)(2,1)S(1)}, u32[]{:S(2)}, u32[]{:S(2)}) collective-permute-start(bf16[4,64,512]{2,1,0:T(8,128)(2,1)S(1)} %copy-done.49), channel_id=1, source_target_pairs={{0,24},{8,16},{16,8},{24,0},{1,25},{9,17},{17,9},{25,1},{2,26},{10... | collective-permute-start | bytes 786440 | tf_op jit(solution)/shard_map/ppermute | solution.py:75
  51.9 13.7 %collective-permute-start.9 = (bf16[4,64,512]{2,1,0:T(8,128)(2,1)S(1)}, bf16[4,64,512]{2,1,0:T(8,128)(2,1)S(1)}, u32[]{:S(2)}, u32[]{:S(2)}) collective-permute-start(bf16[4,64,512]{2,1,0:T(8,128)(2,1)S(1)} %copy-done.49), channel_id=1, source_target_pairs={{0,16},{8,24},{16,0},{24,8},{1,17},{9,25},{17,1},{25,9},{2,18},{10... | collective-permute-start | bytes 786440 | tf_op jit(solution)/shard_map/ppermute | solution.py:75
  53.3 12.3 %collective-permute-start.8 = (bf16[4,64,512]{2,1,0:T(8,128)(2,1)S(1)}, bf16[4,64,512]{2,1,0:T(8,128)(2,1)S(1)}, u32[]{:S(2)}, u32[]{:S(2)}) collective-permute-start(bf16[4,64,512]{2,1,0:T(8,128)(2,1)S(1)} %copy-done.49), channel_id=1, source_target_pairs={{0,8},{8,0},{16,24},{24,16},{1,9},{9,1},{17,25},{25,17},{2,10},{10... | collective-permute-start | bytes 786440 | tf_op jit(solution)/shard_map/ppermute | solution.py:75
  64.0 16.3 %copy-start.42 = (f32[1024,512]{1,0:T(8,128)}, f32[1024,512]{1,0:T(8,128)S(1)}, u32[]{:S(2)}) copy-start(f32[1024,512]{1,0:T(8,128)S(1)} %get-tuple-element.241.x_ref) | copy-start | bytes 6291460
  64.0 16.3 %copy-start.20 = (bf16[4,64,512]{2,1,0:T(8,128)(2,1)}, bf16[4,64,512]{2,1,0:T(8,128)(2,1)S(1)}, u32[]{:S(2)}) copy-start(bf16[4,64,512]{2,1,0:T(8,128)(2,1)S(1)} %collective-permute-done.10.refs_2_.refs_3_) | copy-start | bytes 786436
  65.6 14.7 %copy-start.22 = (bf16[4,64,512]{2,1,0:T(8,128)(2,1)}, bf16[4,64,512]{2,1,0:T(8,128)(2,1)S(1)}, u32[]{:S(2)}) copy-start(bf16[4,64,512]{2,1,0:T(8,128)(2,1)S(1)} %collective-permute-done.9.refs_1_.refs_2_) | copy-start | bytes 786436
  65.7 14.7 %copy-start.24 = (bf16[4,64,512]{2,1,0:T(8,128)(2,1)}, bf16[4,64,512]{2,1,0:T(8,128)(2,1)S(1)}, u32[]{:S(2)}) copy-start(bf16[4,64,512]{2,1,0:T(8,128)(2,1)S(1)} %collective-permute-done.8.refs_0_.refs_1_) | copy-start | bytes 786436
  65.8 3.6 %collective-permute-start.11 = (bf16[3,4,64,512]{3,2,1,0:T(8,128)(2,1)S(1)}, bf16[3,4,64,512]{3,2,1,0:T(8,128)(2,1)S(1)}, u32[]{:S(2)}, u32[]{:S(2)}) collective-permute-start(bf16[3,4,64,512]{3,2,1,0:T(8,128)(2,1)S(1)} %stack.48), channel_id=1, source_target_pairs={{0,1},{1,0},{2,3},{3,2},{4,5},{5,4},{6,7},{7,6},{8,9},{9,8},{10,11... | collective-permute-start | bytes 2359304 | tf_op jit(solution)/shard_map/ppermute | solution.py:75
  65.9 15.7 %collective-permute-start.14 = (bf16[8,64,512]{2,1,0:T(8,128)(2,1)S(1)}, bf16[8,64,512]{2,1,0:T(8,128)(2,1)S(1)}, u32[]{:S(2)}, u32[]{:S(2)}) collective-permute-start(bf16[8,64,512]{2,1,0:T(8,128)(2,1)S(1)} %copy-done.48), channel_id=1, source_target_pairs={{0,24},{8,16},{16,8},{24,0},{1,25},{9,17},{17,9},{25,1},{2,26},{10... | collective-permute-start | bytes 1572872 | tf_op jit(solution)/shard_map/ppermute | solution.py:75
  67.4 24.9 %collective-permute-start.13 = (bf16[8,64,512]{2,1,0:T(8,128)(2,1)S(1)}, bf16[8,64,512]{2,1,0:T(8,128)(2,1)S(1)}, u32[]{:S(2)}, u32[]{:S(2)}) collective-permute-start(bf16[8,64,512]{2,1,0:T(8,128)(2,1)S(1)} %copy-done.48), channel_id=1, source_target_pairs={{0,16},{8,24},{16,0},{24,8},{1,17},{9,25},{17,1},{25,9},{2,18},{10... | collective-permute-start | bytes 1572872 | tf_op jit(solution)/shard_map/ppermute | solution.py:75
  68.8 23.5 %collective-permute-start.12 = (bf16[8,64,512]{2,1,0:T(8,128)(2,1)S(1)}, bf16[8,64,512]{2,1,0:T(8,128)(2,1)S(1)}, u32[]{:S(2)}, u32[]{:S(2)}) collective-permute-start(bf16[8,64,512]{2,1,0:T(8,128)(2,1)S(1)} %copy-done.48), channel_id=1, source_target_pairs={{0,8},{8,0},{16,24},{24,16},{1,9},{9,1},{17,25},{25,17},{2,10},{10... | collective-permute-start | bytes 1572872 | tf_op jit(solution)/shard_map/ppermute | solution.py:75
  80.3 12.9 %copy-start.46 = (f32[1,1,4,256]{3,1,2,0:T(1,128)S(1)}, f32[1,1,4,256]{3,1,2,0:T(1,128)}, u32[]{:S(2)}) copy-start(f32[1,1,4,256]{3,1,2,0:T(1,128)} %copy-done.45) | copy-start | bytes 12292
  81.6 15.2 %copy-start.6 = (bf16[8,64,512]{2,1,0:T(8,128)(2,1)}, bf16[8,64,512]{2,1,0:T(8,128)(2,1)S(1)}, u32[]{:S(2)}) copy-start(bf16[8,64,512]{2,1,0:T(8,128)(2,1)S(1)} %collective-permute-done.14.refs_2_.refs_3_) | copy-start | bytes 1572868
  93.2 3.5 %collective-permute-start.15 = (bf16[3,8,64,512]{3,2,1,0:T(8,128)(2,1)S(1)}, bf16[3,8,64,512]{3,2,1,0:T(8,128)(2,1)}, u32[]{:S(2)}, u32[]{:S(2)}) collective-permute-start(bf16[3,8,64,512]{3,2,1,0:T(8,128)(2,1)S(1)} %stack.49), channel_id=1, source_target_pairs={{0,1},{1,0},{2,3},{3,2},{4,5},{5,4},{6,7},{7,6},{8,9},{9,8},{10,11... | collective-permute-start | bytes 4718600 | tf_op jit(solution)/shard_map/ppermute | solution.py:75
  132.1 11.4 %collective-permute-start.17 = (bf16[4,9,64,512]{3,2,1,0:T(8,128)(2,1)S(1)}, bf16[4,9,64,512]{3,2,1,0:T(8,128)(2,1)S(1)}, u32[]{:S(2)}, u32[]{:S(2)}) collective-permute-start(bf16[4,9,64,512]{3,2,1,0:T(8,128)(2,1)S(1)} %get-tuple-element.263), channel_id=1, source_target_pairs={{0,1},{1,0},{2,3},{3,2},{4,5},{5,4},{6,7},{7,6},{8,9},{9,8},{10,11... | collective-permute-start | bytes 7077896 | tf_op jit(solution)/shard_map/ppermute | solution.py:75
  145.0 14.2 %collective-permute-start.18 = (bf16[2,4,64,512]{3,2,1,0:T(8,128)(2,1)S(1)}, bf16[2,4,64,512]{3,2,1,0:T(8,128)(2,1)S(1)}, u32[]{:S(2)}, u32[]{:S(2)}) collective-permute-start(bf16[2,4,64,512]{3,2,1,0:T(8,128)(2,1)S(1)} %get-tuple-element.272), channel_id=1, source_target_pairs={{0,8},{8,0},{16,24},{24,16},{1,9},{9,1},{17,25},{25,17},{2,10},{10... | collective-permute-start | bytes 1572872 | tf_op jit(solution)/shard_map/ppermute | solution.py:75
  146.4 16.7 %collective-permute-start.19 = (bf16[2,5,64,512]{3,2,1,0:T(8,128)(2,1)S(1)}, bf16[2,5,64,512]{3,2,1,0:T(8,128)(2,1)S(1)}, u32[]{:S(2)}, u32[]{:S(2)}) collective-permute-start(bf16[2,5,64,512]{3,2,1,0:T(8,128)(2,1)S(1)} %get-tuple-element.274), channel_id=1, source_target_pairs={{0,16},{8,24},{16,0},{24,8},{1,17},{9,25},{17,1},{25,9},{2,18},{10... | collective-permute-start | bytes 1966088 | tf_op jit(solution)/shard_map/ppermute | solution.py:75
  164.2 11.4 %collective-permute-start.20 = (bf16[4,64,512]{2,1,0:T(8,128)(2,1)S(1)}, bf16[4,64,512]{2,1,0:T(8,128)(2,1)S(1)}, u32[]{:S(2)}, u32[]{:S(2)}) collective-permute-start(bf16[4,64,512]{2,1,0:T(8,128)(2,1)S(1)} %get-tuple-element.283), channel_id=1, source_target_pairs={{0,16},{8,24},{16,0},{24,8},{1,17},{9,25},{17,1},{25,9},{2,18},{10... | collective-permute-start | bytes 786440 | tf_op jit(solution)/shard_map/ppermute | solution.py:75
  164.9 10.7 %collective-permute-start.21 = (bf16[5,64,512]{2,1,0:T(8,128)(2,1)S(1)}, bf16[5,64,512]{2,1,0:T(8,128)(2,1)S(1)}, u32[]{:S(2)}, u32[]{:S(2)}) collective-permute-start(bf16[5,64,512]{2,1,0:T(8,128)(2,1)S(1)} %get-tuple-element.285), channel_id=1, source_target_pairs={{0,8},{8,0},{16,24},{24,16},{1,9},{9,1},{17,25},{25,17},{2,10},{10... | collective-permute-start | bytes 983048 | tf_op jit(solution)/shard_map/ppermute | solution.py:75
  175.5 7.7 %collective-permute-start.23 = (bf16[4,9,64,512]{3,2,1,0:T(8,128)(2,1)S(1)}, bf16[4,9,64,512]{3,2,1,0:T(8,128)(2,1)S(1)}, u32[]{:S(2)}, u32[]{:S(2)}) collective-permute-start(bf16[4,9,64,512]{3,2,1,0:T(8,128)(2,1)S(1)} %get-tuple-element.293), channel_id=1, source_target_pairs={{0,1},{1,0},{2,3},{3,2},{4,5},{5,4},{6,7},{7,6},{8,9},{9,8},{10,11... | collective-permute-start | bytes 7077896 | tf_op jit(solution)/shard_map/ppermute | solution.py:75
  177.0 22.2 %collective-permute-start.22 = (bf16[9,32,512]{2,1,0:T(8,128)(2,1)}, bf16[9,32,512]{2,1,0:T(8,128)(2,1)}, u32[]{:S(2)}, u32[]{:S(2)}) collective-permute-start(bf16[9,32,512]{2,1,0:T(8,128)(2,1)} %get-tuple-element.299), channel_id=1, source_target_pairs={{0,4},{1,5},{2,6},{3,7},{4,0},{5,1},{6,2},{7,3},{8,12},{9,13},{10,... | collective-permute-start | bytes 884744 | tf_op jit(solution)/shard_map/ppermute | solution.py:75
  182.9 16.4 %collective-permute-start.26 = (bf16[4,3,64,512]{3,2,1,0:T(8,128)(2,1)S(1)}, bf16[4,3,64,512]{3,2,1,0:T(8,128)(2,1)S(1)}, u32[]{:S(2)}, u32[]{:S(2)}) collective-permute-start(bf16[4,3,64,512]{3,2,1,0:T(8,128)(2,1)S(1)} %get-tuple-element.304), channel_id=1, source_target_pairs={{0,1},{1,0},{2,3},{3,2},{4,5},{5,4},{6,7},{7,6},{8,9},{9,8},{10,11... | collective-permute-start | bytes 2359304 | tf_op jit(solution)/shard_map/ppermute | solution.py:75
  184.9 14.4 %collective-permute-start.24 = (bf16[2,4,64,512]{3,2,1,0:T(8,128)(2,1)S(1)}, bf16[2,4,64,512]{3,2,1,0:T(8,128)(2,1)S(1)}, u32[]{:S(2)}, u32[]{:S(2)}) collective-permute-start(bf16[2,4,64,512]{3,2,1,0:T(8,128)(2,1)S(1)} %get-tuple-element.308), channel_id=1, source_target_pairs={{0,8},{8,0},{16,24},{24,16},{1,9},{9,1},{17,25},{25,17},{2,10},{10... | collective-permute-start | bytes 1572872 | tf_op jit(solution)/shard_map/ppermute | solution.py:75
  185.7 16.7 %collective-permute-start.25 = (bf16[2,5,64,512]{3,2,1,0:T(8,128)(2,1)S(1)}, bf16[2,5,64,512]{3,2,1,0:T(8,128)(2,1)S(1)}, u32[]{:S(2)}, u32[]{:S(2)}) collective-permute-start(bf16[2,5,64,512]{3,2,1,0:T(8,128)(2,1)S(1)} %get-tuple-element.310), channel_id=1, source_target_pairs={{0,16},{8,24},{16,0},{24,8},{1,17},{9,25},{17,1},{25,9},{2,18},{10... | collective-permute-start | bytes 1966088 | tf_op jit(solution)/shard_map/ppermute | solution.py:75
  208.6 11.0 %collective-permute-start.30 = (bf16[4,4,64,512]{3,2,1,0:T(8,128)(2,1)S(1)}, bf16[4,4,64,512]{3,2,1,0:T(8,128)(2,1)S(1)}, u32[]{:S(2)}, u32[]{:S(2)}) collective-permute-start(bf16[4,4,64,512]{3,2,1,0:T(8,128)(2,1)S(1)} %get-tuple-element.341), channel_id=1, source_target_pairs={{0,1},{1,0},{2,3},{3,2},{4,5},{5,4},{6,7},{7,6},{8,9},{9,8},{10,11... | collective-permute-start | bytes 3145736 | tf_op jit(solution)/shard_map/ppermute | solution.py:75
  208.7 10.9 %collective-permute-start.29 = (bf16[5,64,512]{2,1,0:T(8,128)(2,1)S(1)}, bf16[5,64,512]{2,1,0:T(8,128)(2,1)S(1)}, u32[]{:S(2)}, u32[]{:S(2)}) collective-permute-start(bf16[5,64,512]{2,1,0:T(8,128)(2,1)S(1)} %get-tuple-element.328), channel_id=1, source_target_pairs={{0,8},{8,0},{16,24},{24,16},{1,9},{9,1},{17,25},{25,17},{2,10},{10... | collective-permute-start | bytes 983048 | tf_op jit(solution)/shard_map/ppermute | solution.py:75
  210.0 9.6 %collective-permute-start.27 = (bf16[9,32,512]{2,1,0:T(8,128)(2,1)S(1)}, bf16[9,32,512]{2,1,0:T(8,128)(2,1)S(1)}, u32[]{:S(2)}, u32[]{:S(2)}) collective-permute-start(bf16[9,32,512]{2,1,0:T(8,128)(2,1)S(1)} %get-tuple-element.342.refs_0_), channel_id=1, source_target_pairs={{0,2},{1,3},{2,0},{3,1},{4,6},{5,7},{6,4},{7,5},{8,10},{9,11},{10,... | collective-permute-start | bytes 884744 | tf_op jit(solution)/shard_map/ppermute | solution.py:75
  211.5 8.1 %collective-permute-start.28 = (bf16[4,64,512]{2,1,0:T(8,128)(2,1)S(1)}, bf16[4,64,512]{2,1,0:T(8,128)(2,1)S(1)}, u32[]{:S(2)}, u32[]{:S(2)}) collective-permute-start(bf16[4,64,512]{2,1,0:T(8,128)(2,1)S(1)} %get-tuple-element.326), channel_id=1, source_target_pairs={{0,16},{8,24},{16,0},{24,8},{1,17},{9,25},{17,1},{25,9},{2,18},{10... | collective-permute-start | bytes 786440 | tf_op jit(solution)/shard_map/ppermute | solution.py:75
  221.6 12.8 %collective-permute-start.33 = (bf16[2,4,64,512]{3,2,1,0:T(8,128)(2,1)S(1)}, bf16[2,4,64,512]{3,2,1,0:T(8,128)(2,1)S(1)}, u32[]{:S(2)}, u32[]{:S(2)}) collective-permute-start(bf16[2,4,64,512]{3,2,1,0:T(8,128)(2,1)S(1)} %get-tuple-element.350), channel_id=1, source_target_pairs={{0,8},{8,0},{16,24},{24,16},{1,9},{9,1},{17,25},{25,17},{2,10},{10... | collective-permute-start | bytes 1572872 | tf_op jit(solution)/shard_map/ppermute | solution.py:75
  222.4 10.2 %collective-permute-start.32 = (bf16[2,3,64,512]{3,2,1,0:T(8,128)(2,1)}, bf16[2,3,64,512]{3,2,1,0:T(8,128)(2,1)S(1)}, u32[]{:S(2)}, u32[]{:S(2)}) collective-permute-start(bf16[2,3,64,512]{3,2,1,0:T(8,128)(2,1)} %get-tuple-element.330), channel_id=1, source_target_pairs={{0,16},{8,24},{16,0},{24,8},{1,17},{9,25},{17,1},{25,9},{2,18},{10... | collective-permute-start | bytes 1179656 | tf_op jit(solution)/shard_map/ppermute | solution.py:75
  223.6 9.0 %collective-permute-start.34 = (bf16[9,32,512]{2,1,0:T(8,128)(2,1)}, bf16[9,32,512]{2,1,0:T(8,128)(2,1)S(1)}, u32[]{:S(2)}, u32[]{:S(2)}) collective-permute-start(bf16[9,32,512]{2,1,0:T(8,128)(2,1)} %get-tuple-element.355), channel_id=1, source_target_pairs={{0,2},{1,3},{2,0},{3,1},{4,6},{5,7},{6,4},{7,5},{8,10},{9,11},{10,... | collective-permute-start | bytes 884744 | tf_op jit(solution)/shard_map/ppermute | solution.py:75
  225.8 1.3 collective-permute-start.16
  227.8 3.7 %collective-permute-start.31 = (f32[1,1]{1,0:T(1,128)}, f32[1,1]{1,0:T(1,128)}, u32[]{:S(2)}, u32[]{:S(2)}) collective-permute-start(f32[1,1]{1,0:T(1,128)} %add.15), channel_id=1, source_target_pairs={{0,2},{1,3},{2,0},{3,1},{4,6},{5,7},{6,4},{7,5},{8,10},{9,11},{10,... | collective-permute-start | bytes 20 | tf_op jit(solution)/shard_map/ppermute | solution.py:75
  230.2 16.3 %collective-permute-start.37 = (bf16[9,32,512]{2,1,0:T(8,128)(2,1)S(1)}, bf16[9,32,512]{2,1,0:T(8,128)(2,1)S(1)}, u32[]{:S(2)}, u32[]{:S(2)}) collective-permute-start(bf16[9,32,512]{2,1,0:T(8,128)(2,1)S(1)} %get-tuple-element.364.refs_0_.refs_10_), channel_id=1, source_target_pairs={{0,4},{1,5},{2,6},{3,7},{4,0},{5,1},{6,2},{7,3},{8,12},{9,13},{10,... | collective-permute-start | bytes 884744 | tf_op jit(solution)/shard_map/ppermute | solution.py:75
  231.5 15.0 %collective-permute-start.36 = (bf16[9,32,512]{2,1,0:T(8,128)(2,1)S(1)}, bf16[9,32,512]{2,1,0:T(8,128)(2,1)S(1)}, u32[]{:S(2)}, u32[]{:S(2)}) collective-permute-start(bf16[9,32,512]{2,1,0:T(8,128)(2,1)S(1)} %get-tuple-element.364.refs_0_.refs_10_), channel_id=1, source_target_pairs={{0,1},{1,0},{2,3},{3,2},{4,5},{5,4},{6,7},{7,6},{8,9},{9,8},{10,11... | collective-permute-start | bytes 884744 | tf_op jit(solution)/shard_map/ppermute | solution.py:75
  235.5 11.0 %collective-permute-start.40 = (bf16[4,64,512]{2,1,0:T(8,128)(2,1)S(1)}, bf16[4,64,512]{2,1,0:T(8,128)(2,1)S(1)}, u32[]{:S(2)}, u32[]{:S(2)}) collective-permute-start(bf16[4,64,512]{2,1,0:T(8,128)(2,1)S(1)} %get-tuple-element.368), channel_id=1, source_target_pairs={{0,16},{8,24},{16,0},{24,8},{1,17},{9,25},{17,1},{25,9},{2,18},{10... | collective-permute-start | bytes 786440 | tf_op jit(solution)/shard_map/ppermute | solution.py:75
  236.5 10.0 %collective-permute-start.39 = (bf16[3,64,512]{2,1,0:T(8,128)(2,1)S(1)}, bf16[3,64,512]{2,1,0:T(8,128)(2,1)S(1)}, u32[]{:S(2)}, u32[]{:S(2)}) collective-permute-start(bf16[3,64,512]{2,1,0:T(8,128)(2,1)S(1)} %get-tuple-element.366), channel_id=1, source_target_pairs={{0,8},{8,0},{16,24},{24,16},{1,9},{9,1},{17,25},{25,17},{2,10},{10... | collective-permute-start | bytes 589832 | tf_op jit(solution)/shard_map/ppermute | solution.py:75
  237.6 8.3 %collective-permute-start.35 = (f32[1,1]{1,0:T(1,128)}, f32[1,1]{1,0:T(1,128)}, u32[]{:S(2)}, u32[]{:S(2)}) collective-permute-start(f32[1,1]{1,0:T(1,128)} %add.16), channel_id=1, source_target_pairs={{0,4},{1,5},{2,6},{3,7},{4,0},{5,1},{6,2},{7,3},{8,12},{9,13},{10,... | collective-permute-start | bytes 20 | tf_op jit(solution)/shard_map/ppermute | solution.py:75
  247.3 18.2 %collective-permute-start.41 = (bf16[7,64,512]{2,1,0:T(8,128)(2,1)S(1)}, bf16[7,64,512]{2,1,0:T(8,128)(2,1)S(1)}, u32[]{:S(2)}, u32[]{:S(2)}) collective-permute-start(bf16[7,64,512]{2,1,0:T(8,128)(2,1)S(1)} %sum_round.17.refs_0_), channel_id=1, source_target_pairs={{0,2},{1,3},{2,0},{3,1},{4,6},{5,7},{6,4},{7,5},{8,10},{9,11},{10,... | collective-permute-start | bytes 1376264 | tf_op jit(solution)/shard_map/ppermute | solution.py:75
  247.4 15.9 %collective-permute-start.42 = (bf16[9,32,512]{2,1,0:T(8,128)(2,1)S(1)}, bf16[9,32,512]{2,1,0:T(8,128)(2,1)S(1)}, u32[]{:S(2)}, u32[]{:S(2)}) collective-permute-start(bf16[9,32,512]{2,1,0:T(8,128)(2,1)S(1)} %get-tuple-element.375.refs_2_), channel_id=1, source_target_pairs={{0,4},{1,5},{2,6},{3,7},{4,0},{5,1},{6,2},{7,3},{8,12},{9,13},{10,... | collective-permute-start | bytes 884744 | tf_op jit(solution)/shard_map/ppermute | solution.py:75
  266.4 21.2 %collective-permute-start.46 = (bf16[7,64,512]{2,1,0:T(8,128)(2,1)S(1)}, bf16[7,64,512]{2,1,0:T(8,128)(2,1)S(1)}, u32[]{:S(2)}, u32[]{:S(2)}) collective-permute-start(bf16[7,64,512]{2,1,0:T(8,128)(2,1)S(1)} %get-tuple-element.381.refs_0_), channel_id=1, source_target_pairs={{0,4},{1,5},{2,6},{3,7},{4,0},{5,1},{6,2},{7,3},{8,12},{9,13},{10,... | collective-permute-start | bytes 1376264 | tf_op jit(solution)/shard_map/ppermute | solution.py:75
  267.6 15.1 %collective-permute-start.44 = (bf16[9,32,512]{2,1,0:T(8,128)(2,1)S(1)}, bf16[9,32,512]{2,1,0:T(8,128)(2,1)S(1)}, u32[]{:S(2)}, u32[]{:S(2)}) collective-permute-start(bf16[9,32,512]{2,1,0:T(8,128)(2,1)S(1)} %get-tuple-element.377.refs_4_.refs_6_), channel_id=1, source_target_pairs={{0,2},{1,3},{2,0},{3,1},{4,6},{5,7},{6,4},{7,5},{8,10},{9,11},{10,... | collective-permute-start | bytes 884744 | tf_op jit(solution)/shard_map/ppermute | solution.py:75
  267.6 15.1 %collective-permute-start.43 = (bf16[9,32,512]{2,1,0:T(8,128)(2,1)S(1)}, bf16[9,32,512]{2,1,0:T(8,128)(2,1)S(1)}, u32[]{:S(2)}, u32[]{:S(2)}) collective-permute-start(bf16[9,32,512]{2,1,0:T(8,128)(2,1)S(1)} %get-tuple-element.377.refs_4_.refs_6_), channel_id=1, source_target_pairs={{0,1},{1,0},{2,3},{3,2},{4,5},{5,4},{6,7},{7,6},{8,9},{9,8},{10,11... | collective-permute-start | bytes 884744 | tf_op jit(solution)/shard_map/ppermute | solution.py:75
  288.3 2.7 collective-permute-start.47
  288.4 2.2 collective-permute-start.38
  288.9 2.1 collective-permute-start.45
  291.7 4.4 %collective-permute-start.50 = (f32[1,2]{1,0:T(1,128)S(1)}, f32[1,2]{1,0:T(1,128)S(1)}, u32[]{:S(2)}, u32[]{:S(2)}) collective-permute-start(f32[1,2]{1,0:T(1,128)S(1)} %square_sum.1.refs_0_), channel_id=1, source_target_pairs={{0,24},{8,16},{16,8},{24,0},{1,25},{9,17},{17,9},{25,1},{2,26},{10... | collective-permute-start | bytes 32 | tf_op jit(solution)/shard_map/ppermute | solution.py:75
  293.1 3.5 %collective-permute-start.49 = (f32[1,2]{1,0:T(1,128)S(1)}, f32[1,2]{1,0:T(1,128)S(1)}, u32[]{:S(2)}, u32[]{:S(2)}) collective-permute-start(f32[1,2]{1,0:T(1,128)S(1)} %square_sum.1.refs_0_), channel_id=1, source_target_pairs={{0,16},{8,24},{16,0},{24,8},{1,17},{9,25},{17,1},{25,9},{2,18},{10... | collective-permute-start | bytes 32 | tf_op jit(solution)/shard_map/ppermute | solution.py:75
  293.5 3.5 %collective-permute-start.48 = (f32[1,2]{1,0:T(1,128)S(1)}, f32[1,2]{1,0:T(1,128)S(1)}, u32[]{:S(2)}, u32[]{:S(2)}) collective-permute-start(f32[1,2]{1,0:T(1,128)S(1)} %square_sum.1.refs_0_), channel_id=1, source_target_pairs={{0,8},{8,0},{16,24},{24,16},{1,9},{9,1},{17,25},{25,17},{2,10},{10... | collective-permute-start | bytes 32 | tf_op jit(solution)/shard_map/ppermute | solution.py:75
  (37 other events, 244.8 us)

commit v3 on v2

--- a/solution.py
+++ b/solution.py
@@ -1295,12 +1295,12 @@
 
     loss = loss + place.to_core(loss)
     dmid, dh, du, c, dm = backward_mlp(1, grad)
-    token = one.begin(*grads_mlp(1, du, c, dm, dh), (0, 4, 0), (4, 5, 1))
+    token = one.begin(*grads_mlp(1, du, c, dm, dh), (0, 5, 0), (5, 4, 1))
     grad, dqkv_one, a_one = backward_attn(1, gate(dmid, token), dh)
     token = advance([one], grad)
     dmid, dh, du, c, dm = backward_mlp(0, gate(grad, token))
     token = advance([one], dmid)
-    token = two.begin(*grads_mlp(0, du, gate(c, token), dm, dh), (0, 4, 0), (4, 5, 1))
+    token = two.begin(*grads_mlp(0, du, gate(c, token), dm, dh), (0, 5, 0), (5, 4, 1))
     token = advance([one], token)
     token = ahead.begin(*grad_qkv(place, where, gate(a_one, token), dqkv_one), (0, 3, 1))
     token = advance([two], token)

time: 309 us -> 308 us (level)
  transfers between devices with their start and end apart: 51 -> 51, of which waited for: 26 -> 27; matrix products, arithmetic and copies ran while one was open for 1% -> 1% of each run, Pallas kernels for 33% -> 33%
where the time goes in v3:
time: 308 us; the launch traced here: 307 us
  Pallas kernels  163 us (53%)
  waiting for transfers between devices  90.2 us (29%)
  starting transfers between devices  45.6 us (15%)
  between operations  4.3 us (1%)
    ppermute x51, waiting for transfers between devices, permute(): return lax.ppermute(x, axis, [(i, i ^ mask) for i in range(size)])  90.2 us
    ppermute x51, starting transfers between devices, permute(): return lax.ppermute(x, axis, [(i, i ^ mask) for i in range(size)])  45.6 us
    pallas_call x2, Pallas kernels, attn_bwd(): pl.pallas_call(kernel, grid=(seqs,), in_specs=[SMEM, row(D), row(D), row(...  23.4 us
    pallas_call x2, Pallas kernels, attn_fwd(): pl.pallas_call(kernel, grid=(seqs // SP,), in_specs=[SMEM, pl.BlockSpec((...  22.5 us
    pallas_call x2, Pallas kernels, mlp_fwd(): pl.pallas_call(kernel, grid=(n // tall,), in_specs=[SMEM, row(D), whole((...  21.4 us
    pallas_call x2, Pallas kernels, mlp_bwd(): pl.pallas_call(kernel, grid=(n // LEN,), in_specs=[SMEM, row(D), row(D),...  19.6 us
    pallas_call x2, Pallas kernels, grad_mlp(): pl.pallas_call(kernel, grid=(2 * steps + 1,), in_specs=[SMEM, whole((n, D...  18.7 us
    pallas_call x10, Pallas kernels, combine(): pl.pallas_call(kernel, grid=(2,), in_specs=[SMEM] + [block(a.shape) for a...  13.4 us
  transfers between devices with their start and end apart: 51, of which 27 were waited for; matrix products, arithmetic and copies ran while one was open for 1% of the time, Pallas kernels for 33%

profile of v3, /device:TPU:0, one launch (start us, length us, event | category | flops | bytes accessed | tf_op | source)
XLA Modules:
  0.0 307.2 jit_solution(12218121352110105448)
XLA Ops:
  0.8 2.3 pack.5
  3.1 3.9 %collective-permute-start.2 = (bf16[5,64,512]{2,1,0:T(8,128)(2,1)}, bf16[5,64,512]{2,1,0:T(8,128)(2,1)S(1)}, u32[]{:S(2)}, u32[]{:S(2)}) collective-permute-start(bf16[5,64,512]{2,1,0:T(8,128)(2,1)} %get-tuple-element.218), channel_id=1, source_target_pairs={{0,24},{8,16},{16,8},{24,0},{1,25},{9,17},{17,9},{25,1},{2,26},{10... | collective-permute-start | bytes 983048 | tf_op jit(solution)/shard_map/ppermute | solution.py:75
  7.9 2.2 pack.6
  10.1 2.8 pack.7
  12.9 2.8 pack.4
  15.8 6.1 %collective-permute-done.1.refs_2_ = bf16[5,64,512]{2,1,0:T(8,128)(2,1)S(1)} collective-permute-done((bf16[5,64,512]{2,1,0:T(8,128)(2,1)}, bf16[5,64,512]{2,1,0:T(8,128)(2,1)S(1)}, u32[]{:S(2)}, u32[]{:S(2)}) %collective-permute-start.1) | collective-permute-done | bytes 327712 | tf_op jit(solution)/shard_map/ppermute | solution.py:75
  23.3 1.6 collective-permute-start.6
  24.8 1.4 collective-permute-start.5
  27.0 3.6 %embed_step.1 = (f32[1024,512]{1,0:T(8,128)}, bf16[1024,64]{1,0:T(8,128)(2,1)S(1)}, bf16[64,512]{1,0:T(8,128)(2,1)S(1)}, f32[16,512]{1,0:T(8,128)S(1)}) custom-call(s32[6]{0:T(128)S(1)} %stack.42.where_ref, bf16[1024,64]{1,0:T(8,128)(2,1)S(1)} %reshape.110.target_ref, f32[1024,1]{1,0:T(8,128)S(1)} %copy.40.mask_ref, ...), custom_call_target="tpu_custom_call" | custom-call | flops 2013265920 | bytes 78643200 | tf_op jit(solution)/shard_map/embed_step/pallas_call | solution.py:479
  30.7 11.6 %attn_fwd.2 = (f32[1024,512]{1,0:T(8,128)}, bf16[1024,1536]{1,0:T(8,128)(2,1)}, bf16[4,8,256,256]{3,2,1,0:T(8,128)(2,1)}, bf16[4,512,256]{2,1,0:T(8,128)(2,1)}) custom-call(s32[6]{0:T(128)S(1)} %stack.42.where_ref, f32[1024,512]{1,0:T(8,128)} %get-tuple-element.227.x_ref, f32[4,512]{1,0:T(4,128)S(1)} %get-tuple-element.415.norm_ref, ...), custom_call_target="tpu_custom_call" | custom-call | flops 80530636800 | bytes 314572800 | tf_op jit(solution)/shard_map/attn_fwd/pallas_call | solution.py:582
  42.4 7.6 %collective-permute-done.5.refs_1_.refs_2_ = bf16[8,64,512]{2,1,0:T(8,128)(2,1)S(1)} collective-permute-done((bf16[8,64,512]{2,1,0:T(8,128)(2,1)}, bf16[8,64,512]{2,1,0:T(8,128)(2,1)S(1)}, u32[]{:S(2)}, u32[]{:S(2)}) %collective-permute-start.5) | collective-permute-done | bytes 524320 | tf_op jit(solution)/shard_map/ppermute | solution.py:75
  50.4 1.5 collective-permute-start.10
  51.9 1.4 collective-permute-start.9
  54.0 10.0 %mlp_fwd.2 = (f32[1024,512]{1,0:T(8,128)S(1)}, bf16[1024,2048]{1,0:T(8,128)(2,1)}, bf16[1024,2048]{1,0:T(8,128)(2,1)}) custom-call(s32[6]{0:T(128)S(1)} %stack.42.where_ref, f32[1024,512]{1,0:T(8,128)} %get-tuple-element.234.mid_ref, f32[4,512]{1,0:T(4,128)S(1)} %get-tuple-element.415.norm_ref, bf16[8,128,512]{2,1,0:T(8,128)(2,1)S(1)} %copy-done.32, ...), custom_call_target="tpu_custom_call" | custom-call | flops 128849018880 | bytes 377487360 | tf_op jit(solution)/shard_map/mlp_fwd/pallas_call | solution.py:657
  64.1 1.6 collective-permute-done.9.refs_1_.refs_2_
  65.9 1.5 collective-permute-start.14
  67.4 1.4 collective-permute-start.13
  69.4 10.8 %attn_fwd.3 = (f32[1024,512]{1,0:T(8,128)}, bf16[1024,1536]{1,0:T(8,128)(2,1)}, bf16[4,8,256,256]{3,2,1,0:T(8,128)(2,1)}, bf16[4,512,256]{2,1,0:T(8,128)(2,1)}) custom-call(s32[6]{0:T(128)S(1)} %stack.42.where_ref, f32[1024,512]{1,0:T(8,128)S(1)} %get-tuple-element.241.x_ref, f32[4,512]{1,0:T(4,128)S(1)} %get-tuple-element.414.norm_ref, ...), custom_call_target="tpu_custom_call" | custom-call | flops 80530636800 | bytes 314572800 | tf_op jit(solution)/shard_map/attn_fwd/pallas_call | solution.py:582
  80.4 1.3 collective-permute-done.14.refs_2_.refs_3_
  81.6 10.7 %collective-permute-done.13.refs_1_.refs_2_ = bf16[8,64,512]{2,1,0:T(8,128)(2,1)S(1)} collective-permute-done((bf16[8,64,512]{2,1,0:T(8,128)(2,1)S(1)}, bf16[8,64,512]{2,1,0:T(8,128)(2,1)S(1)}, u32[]{:S(2)}, u32[]{:S(2)}) %collective-permute-start.13) | collective-permute-done | bytes 524320 | tf_op jit(solution)/shard_map/ppermute | solution.py:75
  94.2 2.6 collective-permute-done.15.refs_4_
  96.8 11.4 %mlp_fwd.3 = (f32[1024,512]{1,0:T(8,128)S(1)}, bf16[1024,2048]{1,0:T(8,128)(2,1)}, bf16[1024,2048]{1,0:T(8,128)(2,1)}) custom-call(s32[6]{0:T(128)S(1)} %stack.42.where_ref, f32[1024,512]{1,0:T(8,128)} %get-tuple-element.246.mid_ref, f32[4,512]{1,0:T(4,128)S(1)} %get-tuple-element.414.norm_ref, bf16[8,128,512]{2,1,0:T(8,128)(2,1)} %get-tuple-element.247.refs_0_, ...), custom_call_target="tpu_custom_call" | custom-call | flops 128849018880 | bytes 377487360 | tf_op jit(solution)/shard_map/mlp_fwd/pallas_call | solution.py:657
  108.2 3.8 %head_step.1 = (f32[1024,512]{1,0:T(8,128)S(1)}, f32[1,64]{1,0:T(1,128)S(1)}, f32[64,512]{1,0:T(8,128)S(1)}, f32[8,512]{1,0:T(8,128)S(1)}) custom-call(f32[1024,512]{1,0:T(8,128)S(1)} %get-tuple-element.251.x_ref, bf16[1024,64]{1,0:T(8,128)(2,1)S(1)} %copy-done.19, f32[1024,1]{1,0:T(8,128)S(1)} %copy.41.mask_ref, ...), custom_call_target="tpu_custom_call" | custom-call | flops 6039797760 | bytes 125829120 | tf_op jit(solution)/shard_map/head_step/pallas_call | solution.py:881
  112.1 10.4 %mlp_bwd.2 = (f32[1024,512]{1,0:T(8,128)S(1)}, bf16[1024,512]{1,0:T(8,128)(2,1)S(1)}, bf16[1024,2048]{1,0:T(8,128)(2,1)}, bf16[1024,512]{1,0:T(8,128)(2,1)S(1)},...) custom-call(s32[6]{0:T(128)S(1)} %stack.42.where_ref, f32[1024,512]{1,0:T(8,128)S(1)} %get-tuple-element.254.dz_ref, ...), custom_call_target="tpu_custom_call" | custom-call | flops 128849018880 | bytes 503316480 | tf_op jit(solution)/shard_map/mlp_bwd/pallas_call | solution.py:724
  122.5 9.5 %grad_mlp.2 = (bf16[4,9,64,512]{3,2,1,0:T(8,128)(2,1)S(1)}, bf16[4,9,64,512]{3,2,1,0:T(8,128)(2,1)S(1)}) custom-call(s32[6]{0:T(128)S(1)} %stack.42.where_ref, bf16[1024,512]{1,0:T(8,128)(2,1)S(1)} %get-tuple-element.256.c_ref, bf16[1024,2048]{1,0:T(8,128)(2,1)} %get-tuple-element.257.du_ref, bf16[1024,2048]{1,0:T(8,128)(2,1)} %get-tuple-element.258.act_ref, ...), custom_call_target="tpu_custom_call" | custom-call | flops 128849018880 | bytes 440401920 | tf_op jit(solution)/shard_map/grad_mlp/pallas_call | solution.py:952
  132.3 11.1 %attn_bwd.2 = (f32[1024,512]{1,0:T(8,128)S(1)}, bf16[1024,1536]{1,0:T(8,128)(2,1)S(1)}, bf16[1024,512]{1,0:T(8,128)(2,1)S(1)}, f32[8,512]{1,0:T(8,128)S(1)}) custom-call(s32[6]{0:T(128)S(1)} %stack.42.where_ref, f32[1024,512]{1,0:T(8,128)S(1)} %get-tuple-element.265.dmid_ref, bf16[1024,512]{1,0:T(8,128)(2,1)S(1)} %get-tuple-element.261.dh_ref, ...), custom_call_target="tpu_custom_call" | custom-call | flops 104689827840 | bytes 503316480 | tf_op jit(solution)/shard_map/attn_bwd/pallas_call | solution.py:821
  143.5 1.5 sum_round.10
  145.0 1.4 collective-permute-start.18
  147.1 9.2 %mlp_bwd.3 = (f32[1024,512]{1,0:T(8,128)S(1)}, bf16[1024,512]{1,0:T(8,128)(2,1)S(1)}, bf16[1024,2048]{1,0:T(8,128)(2,1)}, bf16[1024,512]{1,0:T(8,128)(2,1)S(1)},...) custom-call(s32[6]{0:T(128)S(1)} %stack.42.where_ref, f32[1024,512]{1,0:T(8,128)S(1)} %get-tuple-element.275.dz_ref, ...), custom_call_target="tpu_custom_call" | custom-call | flops 128849018880 | bytes 503316480 | tf_op jit(solution)/shard_map/mlp_bwd/pallas_call | solution.py:724
  156.3 4.0 %collective-permute-done.19.refs_3_ = bf16[2,4,64,512]{3,2,1,0:T(8,128)(2,1)S(1)} collective-permute-done((bf16[2,4,64,512]{3,2,1,0:T(8,128)(2,1)S(1)}, bf16[2,4,64,512]{3,2,1,0:T(8,128)(2,1)S(1)}, u32[]{:S(2)}, u32[]{:S(2)}) %collective-permute-start.19) | collective-permute-done | bytes 524320 | tf_op jit(solution)/shard_map/ppermute | solution.py:75
  160.3 1.7 collective-permute-done.18.refs_1_
  163.1 1.5 collective-permute-start.20
  165.2 9.2 %grad_mlp.3 = (bf16[4,9,64,512]{3,2,1,0:T(8,128)(2,1)S(1)}, bf16[4,9,64,512]{3,2,1,0:T(8,128)(2,1)S(1)}) custom-call(s32[6]{0:T(128)S(1)} %stack.42.where_ref, bf16[1024,512]{1,0:T(8,128)(2,1)S(1)} %get-tuple-element.287.c_ref, bf16[1024,2048]{1,0:T(8,128)(2,1)} %get-tuple-element.288.du_ref, bf16[1024,2048]{1,0:T(8,128)(2,1)} %get-tuple-element.289.act_ref, ...), custom_call_target="tpu_custom_call" | custom-call | flops 128849018880 | bytes 440401920 | tf_op jit(solution)/shard_map/grad_mlp/pallas_call | solution.py:952
  174.5 1.4 sum_round.12
  175.9 2.8 collective-permute-start.22
  178.7 3.2 %grad_qkv.2 = (bf16[4,3,64,512]{3,2,1,0:T(8,128)(2,1)S(1)}, bf16[4,3,64,512]{3,2,1,0:T(8,128)(2,1)S(1)}) custom-call(s32[6]{0:T(128)S(1)} %stack.42.where_ref, bf16[1024,512]{1,0:T(8,128)(2,1)S(1)} %get-tuple-element.302.a_ref, bf16[1024,1536]{1,0:T(8,128)(2,1)S(1)} %get-tuple-element.303.dqkv_ref), custom_call_target="tpu_custom_call" | custom-call | flops 48318382080 | bytes 173015040 | tf_op jit(solution)/shard_map/grad_qkv/pallas_call | solution.py:1029
  182.2 1.7 sum_round.13
  183.9 1.3 collective-permute-start.24
  185.9 12.3 %attn_bwd.3 = (f32[1024,512]{1,0:T(8,128)S(1)}, bf16[1024,1536]{1,0:T(8,128)(2,1)S(1)}, bf16[1024,512]{1,0:T(8,128)(2,1)S(1)}, f32[8,512]{1,0:T(8,128)S(1)}) custom-call(s32[6]{0:T(128)S(1)} %stack.42.where_ref, f32[1024,512]{1,0:T(8,128)S(1)} %get-tuple-element.312.dmid_ref, bf16[1024,512]{1,0:T(8,128)(2,1)S(1)} %get-tuple-element.292.dh_ref, ...), custom_call_target="tpu_custom_call" | custom-call | flops 104689827840 | bytes 503316480 | tf_op jit(solution)/shard_map/attn_bwd/pallas_call | solution.py:821
  199.1 1.9 collective-permute-done.24.refs_3_
  201.0 2.3 sum_round.14
  203.3 3.8 %grad_qkv.3 = (bf16[4,4,64,512]{3,2,1,0:T(8,128)(2,1)S(1)}, bf16[4,4,64,512]{3,2,1,0:T(8,128)(2,1)S(1)}) custom-call(s32[6]{0:T(128)S(1)} %stack.42.where_ref, bf16[1024,512]{1,0:T(8,128)(2,1)S(1)} %get-tuple-element.331.a_ref, bf16[1024,1536]{1,0:T(8,128)(2,1)S(1)} %get-tuple-element.332.dqkv_ref, bf16[1024,64]{1,0:T(8,128)(2,1)S(1)} %copy-done.41, ...), custom_call_target="tpu_custom_call" | custom-call | flops 48318382080 | bytes 173015040 | tf_op jit(solution)/shard_map/grad_qkv/pallas_call | solution.py:1029
  207.2 1.3 collective-permute-start.28
  208.5 1.6 collective-permute-start.27
  210.7 7.4 %collective-permute-done.29.refs_5_ = bf16[4,64,512]{2,1,0:T(8,128)(2,1)S(1)} collective-permute-done((bf16[4,64,512]{2,1,0:T(8,128)(2,1)S(1)}, bf16[4,64,512]{2,1,0:T(8,128)(2,1)S(1)}, u32[]{:S(2)}, u32[]{:S(2)}) %collective-permute-start.29) | collective-permute-done | bytes 262176 | tf_op jit(solution)/shard_map/ppermute | solution.py:75
  218.2 1.9 sum_round.15
  220.8 1.4 collective-permute-start.32
  226.3 2.4 collective-permute-start.31
  231.1 1.9 collective-permute-done.33.refs_3_
  233.0 1.1 sum_round.16
  234.0 1.1 collective-permute-start.40
  236.1 1.7 collective-permute-start.35
  237.8 6.6 %collective-permute-done.35 = f32[1,1]{1,0:T(1,128)} collective-permute-done((f32[1,1]{1,0:T(1,128)}, f32[1,1]{1,0:T(1,128)}, u32[]{:S(2)}, u32[]{:S(2)}) %collective-permute-start.35) | collective-permute-done | bytes 36 | tf_op jit(solution)/shard_map/ppermute | solution.py:75
  245.9 1.3 collective-permute-start.42
  247.2 14.6 %collective-permute-done.42.refs_3_ = bf16[9,32,512]{2,1,0:T(8,128)(2,1)S(1)} collective-permute-done((bf16[9,32,512]{2,1,0:T(8,128)(2,1)S(1)}, bf16[9,32,512]{2,1,0:T(8,128)(2,1)S(1)}, u32[]{:S(2)}, u32[]{:S(2)}) %collective-permute-start.42) | collective-permute-done | bytes 294944 | tf_op jit(solution)/shard_map/ppermute | solution.py:75
  261.8 2.2 collective-permute-done.41.refs_1_
  264.9 1.3 collective-permute-start.46
  266.2 7.1 %fetch.1 = (f32[2,128,1536]{2,1,0:T(8,128)S(1)}, f32[2,128,1536]{2,1,0:T(8,128)S(1)}, f32[2,128,1536]{2,1,0:T(8,128)S(1)}, f32[2,128,512]{2,1,0:T(8,128)S(1)}, f...) custom-call(s32[6]{0:T(128)S(1)} %stack.42.where_ref, ...), custom_call_target="tpu_custom_call" | custom-call | tf_op jit(solution)/shard_map/fetch/pallas_call | solution.py:1064
  273.3 7.9 %collective-permute-done.44.refs_6_.refs_8_ = bf16[9,32,512]{2,1,0:T(8,128)(2,1)S(1)} collective-permute-done((bf16[9,32,512]{2,1,0:T(8,128)(2,1)S(1)}, bf16[9,32,512]{2,1,0:T(8,128)(2,1)S(1)}, u32[]{:S(2)}, u32[]{:S(2)}) %collective-permute-start.44) | collective-permute-done | bytes 294944 | tf_op jit(solution)/shard_map/ppermute | solution.py:75
  281.2 4.8 %collective-permute-done.46.refs_1_ = bf16[7,64,512]{2,1,0:T(8,128)(2,1)S(1)} collective-permute-done((bf16[7,64,512]{2,1,0:T(8,128)(2,1)S(1)}, bf16[7,64,512]{2,1,0:T(8,128)(2,1)S(1)}, u32[]{:S(2)}, u32[]{:S(2)}) %collective-permute-start.46) | collective-permute-done | bytes 458784 | tf_op jit(solution)/shard_map/ppermute | solution.py:75
  287.5 1.6 collective-permute-done.38.refs_3_.refs_13_
  290.2 1.5 collective-permute-start.50
  292.3 1.4 collective-permute-start.48
  295.9 11.2 %adam_step.1 = (f32[2,128,1536]{2,1,0:T(8,128)}, f32[2,128,1536]{2,1,0:T(8,128)}, f32[2,128,1536]{2,1,0:T(8,128)}, f32[2,128,512]{2,1,0:T(8,128)}, f32[2,128,512...) custom-call(s32[6]{0:T(128)S(1)} %stack.42.where_ref, ...), custom_call_target="tpu_custom_call" | custom-call | flops 943718400 | bytes 1132462080 | tf_op jit(solution)/shard_map/adam_step/pallas_call | solution.py:1160
  (182 shorter events, 25.5 us)
Async XLA Ops:
  3.1 12.7 %collective-permute-start.2 = (bf16[5,64,512]{2,1,0:T(8,128)(2,1)}, bf16[5,64,512]{2,1,0:T(8,128)(2,1)S(1)}, u32[]{:S(2)}, u32[]{:S(2)}) collective-permute-start(bf16[5,64,512]{2,1,0:T(8,128)(2,1)} %get-tuple-element.218), channel_id=1, source_target_pairs={{0,24},{8,16},{16,8},{24,0},{1,25},{9,17},{17,9},{25,1},{2,26},{10... | collective-permute-start | bytes 983048 | tf_op jit(solution)/shard_map/ppermute | solution.py:75
  7.0 14.9 %collective-permute-start.1 = (bf16[5,64,512]{2,1,0:T(8,128)(2,1)}, bf16[5,64,512]{2,1,0:T(8,128)(2,1)S(1)}, u32[]{:S(2)}, u32[]{:S(2)}) collective-permute-start(bf16[5,64,512]{2,1,0:T(8,128)(2,1)} %get-tuple-element.218), channel_id=1, source_target_pairs={{0,16},{8,24},{16,0},{24,8},{1,17},{9,25},{17,1},{25,9},{2,18},{10... | collective-permute-start | bytes 983048 | tf_op jit(solution)/shard_map/ppermute | solution.py:75
  7.5 14.7 %collective-permute-start = (bf16[5,64,512]{2,1,0:T(8,128)(2,1)}, bf16[5,64,512]{2,1,0:T(8,128)(2,1)S(1)}, u32[]{:S(2)}, u32[]{:S(2)}) collective-permute-start(bf16[5,64,512]{2,1,0:T(8,128)(2,1)} %get-tuple-element.218), channel_id=1, source_target_pairs={{0,8},{8,0},{16,24},{24,16},{1,9},{9,1},{17,25},{25,17},{2,10},{10... | collective-permute-start | bytes 983048 | tf_op jit(solution)/shard_map/ppermute | solution.py:75
  7.6 19.2 %copy-start.45 = (f32[1,1,4,256]{3,1,2,0:T(1,128)}, f32[1,1,4,256]{3,1,2,0:T(1,128)S(1)}, u32[]{:S(2)}) copy-start(f32[1,1,4,256]{3,1,2,0:T(1,128)S(1)} %copy.42) | copy-start | bytes 12292
  7.8 19.2 %copy-start.18 = (bf16[1024,64]{1,0:T(8,128)(2,1)}, bf16[1024,64]{1,0:T(8,128)(2,1)S(1)}, u32[]{:S(2)}) copy-start(bf16[1024,64]{1,0:T(8,128)(2,1)S(1)} %reshape.110.target_ref) | copy-start | bytes 393220
  15.8 14.9 %copy-start.12 = (bf16[5,64,512]{2,1,0:T(8,128)(2,1)}, bf16[5,64,512]{2,1,0:T(8,128)(2,1)S(1)}, u32[]{:S(2)}) copy-start(bf16[5,64,512]{2,1,0:T(8,128)(2,1)S(1)} %collective-permute-done.2.refs_3_) | copy-start | bytes 983044
  23.3 3.7 %collective-permute-start.3 = (bf16[3,5,64,512]{3,2,1,0:T(8,128)(2,1)}, bf16[3,5,64,512]{3,2,1,0:T(8,128)(2,1)}, u32[]{:S(2)}, u32[]{:S(2)}) collective-permute-start(bf16[3,5,64,512]{3,2,1,0:T(8,128)(2,1)} %pad_maximum_fusion), channel_id=1, source_target_pairs={{0,1},{1,0},{2,3},{3,2},{4,5},{5,4},{6,7},{7,6},{8,9},{9,8},{10,11... | collective-permute-start | bytes 2949128 | tf_op jit(solution)/shard_map/ppermute | solution.py:75
  23.3 19.1 %collective-permute-start.6 = (bf16[8,64,512]{2,1,0:T(8,128)(2,1)}, bf16[8,64,512]{2,1,0:T(8,128)(2,1)S(1)}, u32[]{:S(2)}, u32[]{:S(2)}) collective-permute-start(bf16[8,64,512]{2,1,0:T(8,128)(2,1)} %get-tuple-element.219), channel_id=1, source_target_pairs={{0,24},{8,16},{16,8},{24,0},{1,25},{9,17},{17,9},{25,1},{2,26},{10... | collective-permute-start | bytes 1572872 | tf_op jit(solution)/shard_map/ppermute | solution.py:75
  24.8 25.1 %collective-permute-start.5 = (bf16[8,64,512]{2,1,0:T(8,128)(2,1)}, bf16[8,64,512]{2,1,0:T(8,128)(2,1)S(1)}, u32[]{:S(2)}, u32[]{:S(2)}) collective-permute-start(bf16[8,64,512]{2,1,0:T(8,128)(2,1)} %get-tuple-element.219), channel_id=1, source_target_pairs={{0,16},{8,24},{16,0},{24,8},{1,17},{9,25},{17,1},{25,9},{2,18},{10... | collective-permute-start | bytes 1572872 | tf_op jit(solution)/shard_map/ppermute | solution.py:75
  26.2 23.8 %collective-permute-start.4 = (bf16[8,64,512]{2,1,0:T(8,128)(2,1)}, bf16[8,64,512]{2,1,0:T(8,128)(2,1)S(1)}, u32[]{:S(2)}, u32[]{:S(2)}) collective-permute-start(bf16[8,64,512]{2,1,0:T(8,128)(2,1)} %get-tuple-element.219), channel_id=1, source_target_pairs={{0,8},{8,0},{16,24},{24,16},{1,9},{9,1},{17,25},{25,17},{2,10},{10... | collective-permute-start | bytes 1572872 | tf_op jit(solution)/shard_map/ppermute | solution.py:75
  30.7 23.3 %copy-start.27 = (f32[4,512]{1,0:T(4,128)}, f32[4,512]{1,0:T(4,128)S(1)}, u32[]{:S(2)}) copy-start(f32[4,512]{1,0:T(4,128)S(1)} %get-tuple-element.415.norm_ref) | copy-start | bytes 24580
  42.4 21.6 %copy-start = (bf16[8,64,512]{2,1,0:T(8,128)(2,1)}, bf16[8,64,512]{2,1,0:T(8,128)(2,1)S(1)}, u32[]{:S(2)}) copy-start(bf16[8,64,512]{2,1,0:T(8,128)(2,1)S(1)} %collective-permute-done.6.refs_2_.refs_3_) | copy-start | bytes 1572868
  50.0 14.0 %copy-start.2 = (bf16[8,64,512]{2,1,0:T(8,128)(2,1)}, bf16[8,64,512]{2,1,0:T(8,128)(2,1)S(1)}, u32[]{:S(2)}) copy-start(bf16[8,64,512]{2,1,0:T(8,128)(2,1)S(1)} %collective-permute-done.5.refs_1_.refs_2_) | copy-start | bytes 1572868
  50.1 13.9 %copy-start.4 = (bf16[8,64,512]{2,1,0:T(8,128)(2,1)}, bf16[8,64,512]{2,1,0:T(8,128)(2,1)S(1)}, u32[]{:S(2)}) copy-start(bf16[8,64,512]{2,1,0:T(8,128)(2,1)S(1)} %collective-permute-done.4.refs_0_.refs_1_) | copy-start | bytes 1572868
  50.3 3.6 %collective-permute-start.7 = (bf16[3,8,64,512]{3,2,1,0:T(8,128)(2,1)S(1)}, bf16[3,8,64,512]{3,2,1,0:T(8,128)(2,1)S(1)}, u32[]{:S(2)}, u32[]{:S(2)}) collective-permute-start(bf16[3,8,64,512]{3,2,1,0:T(8,128)(2,1)S(1)} %stack.47), channel_id=1, source_target_pairs={{0,1},{1,0},{2,3},{3,2},{4,5},{5,4},{6,7},{7,6},{8,9},{9,8},{10,11... | collective-permute-start | bytes 4718600 | tf_op jit(solution)/shard_map/ppermute | solution.py:75
  50.4 13.6 %collective-permute-start.10 = (bf16[4,64,512]{2,1,0:T(8,128)(2,1)S(1)}, bf16[4,64,512]{2,1,0:T(8,128)(2,1)S(1)}, u32[]{:S(2)}, u32[]{:S(2)}) collective-permute-start(bf16[4,64,512]{2,1,0:T(8,128)(2,1)S(1)} %copy-done.49), channel_id=1, source_target_pairs={{0,24},{8,16},{16,8},{24,0},{1,25},{9,17},{17,9},{25,1},{2,26},{10... | collective-permute-start | bytes 786440 | tf_op jit(solution)/shard_map/ppermute | solution.py:75
  51.9 13.7 %collective-permute-start.9 = (bf16[4,64,512]{2,1,0:T(8,128)(2,1)S(1)}, bf16[4,64,512]{2,1,0:T(8,128)(2,1)S(1)}, u32[]{:S(2)}, u32[]{:S(2)}) collective-permute-start(bf16[4,64,512]{2,1,0:T(8,128)(2,1)S(1)} %copy-done.49), channel_id=1, source_target_pairs={{0,16},{8,24},{16,0},{24,8},{1,17},{9,25},{17,1},{25,9},{2,18},{10... | collective-permute-start | bytes 786440 | tf_op jit(solution)/shard_map/ppermute | solution.py:75
  53.3 12.3 %collective-permute-start.8 = (bf16[4,64,512]{2,1,0:T(8,128)(2,1)S(1)}, bf16[4,64,512]{2,1,0:T(8,128)(2,1)S(1)}, u32[]{:S(2)}, u32[]{:S(2)}) collective-permute-start(bf16[4,64,512]{2,1,0:T(8,128)(2,1)S(1)} %copy-done.49), channel_id=1, source_target_pairs={{0,8},{8,0},{16,24},{24,16},{1,9},{9,1},{17,25},{25,17},{2,10},{10... | collective-permute-start | bytes 786440 | tf_op jit(solution)/shard_map/ppermute | solution.py:75
  64.0 16.3 %copy-start.42 = (f32[1024,512]{1,0:T(8,128)}, f32[1024,512]{1,0:T(8,128)S(1)}, u32[]{:S(2)}) copy-start(f32[1024,512]{1,0:T(8,128)S(1)} %get-tuple-element.241.x_ref) | copy-start | bytes 6291460
  64.0 16.3 %copy-start.20 = (bf16[4,64,512]{2,1,0:T(8,128)(2,1)}, bf16[4,64,512]{2,1,0:T(8,128)(2,1)S(1)}, u32[]{:S(2)}) copy-start(bf16[4,64,512]{2,1,0:T(8,128)(2,1)S(1)} %collective-permute-done.10.refs_2_.refs_3_) | copy-start | bytes 786436
  65.6 14.7 %copy-start.22 = (bf16[4,64,512]{2,1,0:T(8,128)(2,1)}, bf16[4,64,512]{2,1,0:T(8,128)(2,1)S(1)}, u32[]{:S(2)}) copy-start(bf16[4,64,512]{2,1,0:T(8,128)(2,1)S(1)} %collective-permute-done.9.refs_1_.refs_2_) | copy-start | bytes 786436
  65.7 14.7 %copy-start.24 = (bf16[4,64,512]{2,1,0:T(8,128)(2,1)}, bf16[4,64,512]{2,1,0:T(8,128)(2,1)S(1)}, u32[]{:S(2)}) copy-start(bf16[4,64,512]{2,1,0:T(8,128)(2,1)S(1)} %collective-permute-done.8.refs_0_.refs_1_) | copy-start | bytes 786436
  65.8 3.6 %collective-permute-start.11 = (bf16[3,4,64,512]{3,2,1,0:T(8,128)(2,1)S(1)}, bf16[3,4,64,512]{3,2,1,0:T(8,128)(2,1)S(1)}, u32[]{:S(2)}, u32[]{:S(2)}) collective-permute-start(bf16[3,4,64,512]{3,2,1,0:T(8,128)(2,1)S(1)} %stack.48), channel_id=1, source_target_pairs={{0,1},{1,0},{2,3},{3,2},{4,5},{5,4},{6,7},{7,6},{8,9},{9,8},{10,11... | collective-permute-start | bytes 2359304 | tf_op jit(solution)/shard_map/ppermute | solution.py:75
  65.9 15.7 %collective-permute-start.14 = (bf16[8,64,512]{2,1,0:T(8,128)(2,1)S(1)}, bf16[8,64,512]{2,1,0:T(8,128)(2,1)S(1)}, u32[]{:S(2)}, u32[]{:S(2)}) collective-permute-start(bf16[8,64,512]{2,1,0:T(8,128)(2,1)S(1)} %copy-done.48), channel_id=1, source_target_pairs={{0,24},{8,16},{16,8},{24,0},{1,25},{9,17},{17,9},{25,1},{2,26},{10... | collective-permute-start | bytes 1572872 | tf_op jit(solution)/shard_map/ppermute | solution.py:75
  67.4 24.9 %collective-permute-start.13 = (bf16[8,64,512]{2,1,0:T(8,128)(2,1)S(1)}, bf16[8,64,512]{2,1,0:T(8,128)(2,1)S(1)}, u32[]{:S(2)}, u32[]{:S(2)}) collective-permute-start(bf16[8,64,512]{2,1,0:T(8,128)(2,1)S(1)} %copy-done.48), channel_id=1, source_target_pairs={{0,16},{8,24},{16,0},{24,8},{1,17},{9,25},{17,1},{25,9},{2,18},{10... | collective-permute-start | bytes 1572872 | tf_op jit(solution)/shard_map/ppermute | solution.py:75
  68.8 23.5 %collective-permute-start.12 = (bf16[8,64,512]{2,1,0:T(8,128)(2,1)S(1)}, bf16[8,64,512]{2,1,0:T(8,128)(2,1)S(1)}, u32[]{:S(2)}, u32[]{:S(2)}) collective-permute-start(bf16[8,64,512]{2,1,0:T(8,128)(2,1)S(1)} %copy-done.48), channel_id=1, source_target_pairs={{0,8},{8,0},{16,24},{24,16},{1,9},{9,1},{17,25},{25,17},{2,10},{10... | collective-permute-start | bytes 1572872 | tf_op jit(solution)/shard_map/ppermute | solution.py:75
  80.3 12.9 %copy-start.46 = (f32[1,1,4,256]{3,1,2,0:T(1,128)S(1)}, f32[1,1,4,256]{3,1,2,0:T(1,128)}, u32[]{:S(2)}) copy-start(f32[1,1,4,256]{3,1,2,0:T(1,128)} %copy-done.45) | copy-start | bytes 12292
  81.6 15.2 %copy-start.6 = (bf16[8,64,512]{2,1,0:T(8,128)(2,1)}, bf16[8,64,512]{2,1,0:T(8,128)(2,1)S(1)}, u32[]{:S(2)}) copy-start(bf16[8,64,512]{2,1,0:T(8,128)(2,1)S(1)} %collective-permute-done.14.refs_2_.refs_3_) | copy-start | bytes 1572868
  93.2 3.5 %collective-permute-start.15 = (bf16[3,8,64,512]{3,2,1,0:T(8,128)(2,1)S(1)}, bf16[3,8,64,512]{3,2,1,0:T(8,128)(2,1)}, u32[]{:S(2)}, u32[]{:S(2)}) collective-permute-start(bf16[3,8,64,512]{3,2,1,0:T(8,128)(2,1)S(1)} %stack.49), channel_id=1, source_target_pairs={{0,1},{1,0},{2,3},{3,2},{4,5},{5,4},{6,7},{7,6},{8,9},{9,8},{10,11... | collective-permute-start | bytes 4718600 | tf_op jit(solution)/shard_map/ppermute | solution.py:75
  132.1 11.4 %collective-permute-start.17 = (bf16[4,9,64,512]{3,2,1,0:T(8,128)(2,1)S(1)}, bf16[4,9,64,512]{3,2,1,0:T(8,128)(2,1)S(1)}, u32[]{:S(2)}, u32[]{:S(2)}) collective-permute-start(bf16[4,9,64,512]{3,2,1,0:T(8,128)(2,1)S(1)} %get-tuple-element.263), channel_id=1, source_target_pairs={{0,1},{1,0},{2,3},{3,2},{4,5},{5,4},{6,7},{7,6},{8,9},{9,8},{10,11... | collective-permute-start | bytes 7077896 | tf_op jit(solution)/shard_map/ppermute | solution.py:75
  145.0 17.1 %collective-permute-start.18 = (bf16[2,5,64,512]{3,2,1,0:T(8,128)(2,1)S(1)}, bf16[2,5,64,512]{3,2,1,0:T(8,128)(2,1)S(1)}, u32[]{:S(2)}, u32[]{:S(2)}) collective-permute-start(bf16[2,5,64,512]{3,2,1,0:T(8,128)(2,1)S(1)} %get-tuple-element.272), channel_id=1, source_target_pairs={{0,8},{8,0},{16,24},{24,16},{1,9},{9,1},{17,25},{25,17},{2,10},{10... | collective-permute-start | bytes 1966088 | tf_op jit(solution)/shard_map/ppermute | solution.py:75
  146.4 13.9 %collective-permute-start.19 = (bf16[2,4,64,512]{3,2,1,0:T(8,128)(2,1)S(1)}, bf16[2,4,64,512]{3,2,1,0:T(8,128)(2,1)S(1)}, u32[]{:S(2)}, u32[]{:S(2)}) collective-permute-start(bf16[2,4,64,512]{3,2,1,0:T(8,128)(2,1)S(1)} %get-tuple-element.274), channel_id=1, source_target_pairs={{0,16},{8,24},{16,0},{24,8},{1,17},{9,25},{17,1},{25,9},{2,18},{10... | collective-permute-start | bytes 1572872 | tf_op jit(solution)/shard_map/ppermute | solution.py:75
  163.1 11.4 %collective-permute-start.20 = (bf16[5,64,512]{2,1,0:T(8,128)(2,1)S(1)}, bf16[5,64,512]{2,1,0:T(8,128)(2,1)S(1)}, u32[]{:S(2)}, u32[]{:S(2)}) collective-permute-start(bf16[5,64,512]{2,1,0:T(8,128)(2,1)S(1)} %get-tuple-element.283), channel_id=1, source_target_pairs={{0,16},{8,24},{16,0},{24,8},{1,17},{9,25},{17,1},{25,9},{2,18},{10... | collective-permute-start | bytes 983048 | tf_op jit(solution)/shard_map/ppermute | solution.py:75
  164.5 9.9 %collective-permute-start.21 = (bf16[4,64,512]{2,1,0:T(8,128)(2,1)S(1)}, bf16[4,64,512]{2,1,0:T(8,128)(2,1)S(1)}, u32[]{:S(2)}, u32[]{:S(2)}) collective-permute-start(bf16[4,64,512]{2,1,0:T(8,128)(2,1)S(1)} %get-tuple-element.285), channel_id=1, source_target_pairs={{0,8},{8,0},{16,24},{24,16},{1,9},{9,1},{17,25},{25,17},{2,10},{10... | collective-permute-start | bytes 786440 | tf_op jit(solution)/shard_map/ppermute | solution.py:75
  174.4 7.8 %collective-permute-start.23 = (bf16[4,9,64,512]{3,2,1,0:T(8,128)(2,1)S(1)}, bf16[4,9,64,512]{3,2,1,0:T(8,128)(2,1)S(1)}, u32[]{:S(2)}, u32[]{:S(2)}) collective-permute-start(bf16[4,9,64,512]{3,2,1,0:T(8,128)(2,1)S(1)} %get-tuple-element.293), channel_id=1, source_target_pairs={{0,1},{1,0},{2,3},{3,2},{4,5},{5,4},{6,7},{7,6},{8,9},{9,8},{10,11... | collective-permute-start | bytes 7077896 | tf_op jit(solution)/shard_map/ppermute | solution.py:75
  175.9 22.3 %collective-permute-start.22 = (bf16[9,32,512]{2,1,0:T(8,128)(2,1)}, bf16[9,32,512]{2,1,0:T(8,128)(2,1)}, u32[]{:S(2)}, u32[]{:S(2)}) collective-permute-start(bf16[9,32,512]{2,1,0:T(8,128)(2,1)} %get-tuple-element.299), channel_id=1, source_target_pairs={{0,4},{1,5},{2,6},{3,7},{4,0},{5,1},{6,2},{7,3},{8,12},{9,13},{10,... | collective-permute-start | bytes 884744 | tf_op jit(solution)/shard_map/ppermute | solution.py:75
  181.9 16.2 %collective-permute-start.26 = (bf16[4,3,64,512]{3,2,1,0:T(8,128)(2,1)S(1)}, bf16[4,3,64,512]{3,2,1,0:T(8,128)(2,1)S(1)}, u32[]{:S(2)}, u32[]{:S(2)}) collective-permute-start(bf16[4,3,64,512]{3,2,1,0:T(8,128)(2,1)S(1)} %get-tuple-element.304), channel_id=1, source_target_pairs={{0,1},{1,0},{2,3},{3,2},{4,5},{5,4},{6,7},{7,6},{8,9},{9,8},{10,11... | collective-permute-start | bytes 2359304 | tf_op jit(solution)/shard_map/ppermute | solution.py:75
  183.9 17.0 %collective-permute-start.24 = (bf16[2,5,64,512]{3,2,1,0:T(8,128)(2,1)S(1)}, bf16[2,5,64,512]{3,2,1,0:T(8,128)(2,1)S(1)}, u32[]{:S(2)}, u32[]{:S(2)}) collective-permute-start(bf16[2,5,64,512]{3,2,1,0:T(8,128)(2,1)S(1)} %get-tuple-element.308), channel_id=1, source_target_pairs={{0,8},{8,0},{16,24},{24,16},{1,9},{9,1},{17,25},{25,17},{2,10},{10... | collective-permute-start | bytes 1966088 | tf_op jit(solution)/shard_map/ppermute | solution.py:75
  185.2 13.9 %collective-permute-start.25 = (bf16[2,4,64,512]{3,2,1,0:T(8,128)(2,1)S(1)}, bf16[2,4,64,512]{3,2,1,0:T(8,128)(2,1)S(1)}, u32[]{:S(2)}, u32[]{:S(2)}) collective-permute-start(bf16[2,4,64,512]{3,2,1,0:T(8,128)(2,1)S(1)} %get-tuple-element.310), channel_id=1, source_target_pairs={{0,16},{8,24},{16,0},{24,8},{1,17},{9,25},{17,1},{25,9},{2,18},{10... | collective-permute-start | bytes 1572872 | tf_op jit(solution)/shard_map/ppermute | solution.py:75
  207.1 11.0 %collective-permute-start.30 = (bf16[4,4,64,512]{3,2,1,0:T(8,128)(2,1)S(1)}, bf16[4,4,64,512]{3,2,1,0:T(8,128)(2,1)S(1)}, u32[]{:S(2)}, u32[]{:S(2)}) collective-permute-start(bf16[4,4,64,512]{3,2,1,0:T(8,128)(2,1)S(1)} %get-tuple-element.341), channel_id=1, source_target_pairs={{0,1},{1,0},{2,3},{3,2},{4,5},{5,4},{6,7},{7,6},{8,9},{9,8},{10,11... | collective-permute-start | bytes 3145736 | tf_op jit(solution)/shard_map/ppermute | solution.py:75
  207.2 10.9 %collective-permute-start.28 = (bf16[5,64,512]{2,1,0:T(8,128)(2,1)S(1)}, bf16[5,64,512]{2,1,0:T(8,128)(2,1)S(1)}, u32[]{:S(2)}, u32[]{:S(2)}) collective-permute-start(bf16[5,64,512]{2,1,0:T(8,128)(2,1)S(1)} %get-tuple-element.326), channel_id=1, source_target_pairs={{0,16},{8,24},{16,0},{24,8},{1,17},{9,25},{17,1},{25,9},{2,18},{10... | collective-permute-start | bytes 983048 | tf_op jit(solution)/shard_map/ppermute | solution.py:75
  208.5 9.7 %collective-permute-start.27 = (bf16[9,32,512]{2,1,0:T(8,128)(2,1)S(1)}, bf16[9,32,512]{2,1,0:T(8,128)(2,1)S(1)}, u32[]{:S(2)}, u32[]{:S(2)}) collective-permute-start(bf16[9,32,512]{2,1,0:T(8,128)(2,1)S(1)} %get-tuple-element.342.refs_0_), channel_id=1, source_target_pairs={{0,2},{1,3},{2,0},{3,1},{4,6},{5,7},{6,4},{7,5},{8,10},{9,11},{10,... | collective-permute-start | bytes 884744 | tf_op jit(solution)/shard_map/ppermute | solution.py:75
  210.1 8.1 %collective-permute-start.29 = (bf16[4,64,512]{2,1,0:T(8,128)(2,1)S(1)}, bf16[4,64,512]{2,1,0:T(8,128)(2,1)S(1)}, u32[]{:S(2)}, u32[]{:S(2)}) collective-permute-start(bf16[4,64,512]{2,1,0:T(8,128)(2,1)S(1)} %get-tuple-element.328), channel_id=1, source_target_pairs={{0,8},{8,0},{16,24},{24,16},{1,9},{9,1},{17,25},{25,17},{2,10},{10... | collective-permute-start | bytes 786440 | tf_op jit(solution)/shard_map/ppermute | solution.py:75
  220.1 12.8 %collective-permute-start.33 = (bf16[2,4,64,512]{3,2,1,0:T(8,128)(2,1)S(1)}, bf16[2,4,64,512]{3,2,1,0:T(8,128)(2,1)S(1)}, u32[]{:S(2)}, u32[]{:S(2)}) collective-permute-start(bf16[2,4,64,512]{3,2,1,0:T(8,128)(2,1)S(1)} %get-tuple-element.350), channel_id=1, source_target_pairs={{0,8},{8,0},{16,24},{24,16},{1,9},{9,1},{17,25},{25,17},{2,10},{10... | collective-permute-start | bytes 1572872 | tf_op jit(solution)/shard_map/ppermute | solution.py:75
  220.8 10.3 %collective-permute-start.32 = (bf16[2,3,64,512]{3,2,1,0:T(8,128)(2,1)}, bf16[2,3,64,512]{3,2,1,0:T(8,128)(2,1)S(1)}, u32[]{:S(2)}, u32[]{:S(2)}) collective-permute-start(bf16[2,3,64,512]{3,2,1,0:T(8,128)(2,1)} %get-tuple-element.330), channel_id=1, source_target_pairs={{0,16},{8,24},{16,0},{24,8},{1,17},{9,25},{17,1},{25,9},{2,18},{10... | collective-permute-start | bytes 1179656 | tf_op jit(solution)/shard_map/ppermute | solution.py:75
  222.1 9.0 %collective-permute-start.34 = (bf16[9,32,512]{2,1,0:T(8,128)(2,1)}, bf16[9,32,512]{2,1,0:T(8,128)(2,1)S(1)}, u32[]{:S(2)}, u32[]{:S(2)}) collective-permute-start(bf16[9,32,512]{2,1,0:T(8,128)(2,1)} %get-tuple-element.355), channel_id=1, source_target_pairs={{0,2},{1,3},{2,0},{3,1},{4,6},{5,7},{6,4},{7,5},{8,10},{9,11},{10,... | collective-permute-start | bytes 884744 | tf_op jit(solution)/shard_map/ppermute | solution.py:75
  224.3 1.3 collective-permute-start.16
  226.3 3.7 %collective-permute-start.31 = (f32[1,1]{1,0:T(1,128)}, f32[1,1]{1,0:T(1,128)}, u32[]{:S(2)}, u32[]{:S(2)}) collective-permute-start(f32[1,1]{1,0:T(1,128)} %add.15), channel_id=1, source_target_pairs={{0,2},{1,3},{2,0},{3,1},{4,6},{5,7},{6,4},{7,5},{8,10},{9,11},{10,... | collective-permute-start | bytes 20 | tf_op jit(solution)/shard_map/ppermute | solution.py:75
  228.7 16.3 %collective-permute-start.37 = (bf16[9,32,512]{2,1,0:T(8,128)(2,1)S(1)}, bf16[9,32,512]{2,1,0:T(8,128)(2,1)S(1)}, u32[]{:S(2)}, u32[]{:S(2)}) collective-permute-start(bf16[9,32,512]{2,1,0:T(8,128)(2,1)S(1)} %get-tuple-element.364.refs_0_.refs_10_), channel_id=1, source_target_pairs={{0,4},{1,5},{2,6},{3,7},{4,0},{5,1},{6,2},{7,3},{8,12},{9,13},{10,... | collective-permute-start | bytes 884744 | tf_op jit(solution)/shard_map/ppermute | solution.py:75
  230.0 15.0 %collective-permute-start.36 = (bf16[9,32,512]{2,1,0:T(8,128)(2,1)S(1)}, bf16[9,32,512]{2,1,0:T(8,128)(2,1)S(1)}, u32[]{:S(2)}, u32[]{:S(2)}) collective-permute-start(bf16[9,32,512]{2,1,0:T(8,128)(2,1)S(1)} %get-tuple-element.364.refs_0_.refs_10_), channel_id=1, source_target_pairs={{0,1},{1,0},{2,3},{3,2},{4,5},{5,4},{6,7},{7,6},{8,9},{9,8},{10,11... | collective-permute-start | bytes 884744 | tf_op jit(solution)/shard_map/ppermute | solution.py:75
  234.0 11.0 %collective-permute-start.40 = (bf16[4,64,512]{2,1,0:T(8,128)(2,1)S(1)}, bf16[4,64,512]{2,1,0:T(8,128)(2,1)S(1)}, u32[]{:S(2)}, u32[]{:S(2)}) collective-permute-start(bf16[4,64,512]{2,1,0:T(8,128)(2,1)S(1)} %get-tuple-element.368), channel_id=1, source_target_pairs={{0,16},{8,24},{16,0},{24,8},{1,17},{9,25},{17,1},{25,9},{2,18},{10... | collective-permute-start | bytes 786440 | tf_op jit(solution)/shard_map/ppermute | solution.py:75
  235.1 10.0 %collective-permute-start.39 = (bf16[3,64,512]{2,1,0:T(8,128)(2,1)S(1)}, bf16[3,64,512]{2,1,0:T(8,128)(2,1)S(1)}, u32[]{:S(2)}, u32[]{:S(2)}) collective-permute-start(bf16[3,64,512]{2,1,0:T(8,128)(2,1)S(1)} %get-tuple-element.366), channel_id=1, source_target_pairs={{0,8},{8,0},{16,24},{24,16},{1,9},{9,1},{17,25},{25,17},{2,10},{10... | collective-permute-start | bytes 589832 | tf_op jit(solution)/shard_map/ppermute | solution.py:75
  236.1 8.3 %collective-permute-start.35 = (f32[1,1]{1,0:T(1,128)}, f32[1,1]{1,0:T(1,128)}, u32[]{:S(2)}, u32[]{:S(2)}) collective-permute-start(f32[1,1]{1,0:T(1,128)} %add.16), channel_id=1, source_target_pairs={{0,4},{1,5},{2,6},{3,7},{4,0},{5,1},{6,2},{7,3},{8,12},{9,13},{10,... | collective-permute-start | bytes 20 | tf_op jit(solution)/shard_map/ppermute | solution.py:75
  245.8 18.2 %collective-permute-start.41 = (bf16[7,64,512]{2,1,0:T(8,128)(2,1)S(1)}, bf16[7,64,512]{2,1,0:T(8,128)(2,1)S(1)}, u32[]{:S(2)}, u32[]{:S(2)}) collective-permute-start(bf16[7,64,512]{2,1,0:T(8,128)(2,1)S(1)} %sum_round.17.refs_0_), channel_id=1, source_target_pairs={{0,2},{1,3},{2,0},{3,1},{4,6},{5,7},{6,4},{7,5},{8,10},{9,11},{10,... | collective-permute-start | bytes 1376264 | tf_op jit(solution)/shard_map/ppermute | solution.py:75
  245.9 15.9 %collective-permute-start.42 = (bf16[9,32,512]{2,1,0:T(8,128)(2,1)S(1)}, bf16[9,32,512]{2,1,0:T(8,128)(2,1)S(1)}, u32[]{:S(2)}, u32[]{:S(2)}) collective-permute-start(bf16[9,32,512]{2,1,0:T(8,128)(2,1)S(1)} %get-tuple-element.375.refs_2_), channel_id=1, source_target_pairs={{0,4},{1,5},{2,6},{3,7},{4,0},{5,1},{6,2},{7,3},{8,12},{9,13},{10,... | collective-permute-start | bytes 884744 | tf_op jit(solution)/shard_map/ppermute | solution.py:75
  264.9 21.2 %collective-permute-start.46 = (bf16[7,64,512]{2,1,0:T(8,128)(2,1)S(1)}, bf16[7,64,512]{2,1,0:T(8,128)(2,1)S(1)}, u32[]{:S(2)}, u32[]{:S(2)}) collective-permute-start(bf16[7,64,512]{2,1,0:T(8,128)(2,1)S(1)} %get-tuple-element.381.refs_0_), channel_id=1, source_target_pairs={{0,4},{1,5},{2,6},{3,7},{4,0},{5,1},{6,2},{7,3},{8,12},{9,13},{10,... | collective-permute-start | bytes 1376264 | tf_op jit(solution)/shard_map/ppermute | solution.py:75
  266.2 15.1 %collective-permute-start.44 = (bf16[9,32,512]{2,1,0:T(8,128)(2,1)S(1)}, bf16[9,32,512]{2,1,0:T(8,128)(2,1)S(1)}, u32[]{:S(2)}, u32[]{:S(2)}) collective-permute-start(bf16[9,32,512]{2,1,0:T(8,128)(2,1)S(1)} %get-tuple-element.377.refs_4_.refs_6_), channel_id=1, source_target_pairs={{0,2},{1,3},{2,0},{3,1},{4,6},{5,7},{6,4},{7,5},{8,10},{9,11},{10,... | collective-permute-start | bytes 884744 | tf_op jit(solution)/shard_map/ppermute | solution.py:75
  266.2 15.0 %collective-permute-start.43 = (bf16[9,32,512]{2,1,0:T(8,128)(2,1)S(1)}, bf16[9,32,512]{2,1,0:T(8,128)(2,1)S(1)}, u32[]{:S(2)}, u32[]{:S(2)}) collective-permute-start(bf16[9,32,512]{2,1,0:T(8,128)(2,1)S(1)} %get-tuple-element.377.refs_4_.refs_6_), channel_id=1, source_target_pairs={{0,1},{1,0},{2,3},{3,2},{4,5},{5,4},{6,7},{7,6},{8,9},{9,8},{10,11... | collective-permute-start | bytes 884744 | tf_op jit(solution)/shard_map/ppermute | solution.py:75
  286.8 2.7 collective-permute-start.47
  286.9 2.2 collective-permute-start.38
  287.4 2.1 collective-permute-start.45
  290.2 4.4 %collective-permute-start.50 = (f32[1,2]{1,0:T(1,128)S(1)}, f32[1,2]{1,0:T(1,128)S(1)}, u32[]{:S(2)}, u32[]{:S(2)}) collective-permute-start(f32[1,2]{1,0:T(1,128)S(1)} %square_sum.1.refs_0_), channel_id=1, source_target_pairs={{0,24},{8,16},{16,8},{24,0},{1,25},{9,17},{17,9},{25,1},{2,26},{10... | collective-permute-start | bytes 32 | tf_op jit(solution)/shard_map/ppermute | solution.py:75
  291.7 3.5 %collective-permute-start.49 = (f32[1,2]{1,0:T(1,128)S(1)}, f32[1,2]{1,0:T(1,128)S(1)}, u32[]{:S(2)}, u32[]{:S(2)}) collective-permute-start(f32[1,2]{1,0:T(1,128)S(1)} %square_sum.1.refs_0_), channel_id=1, source_target_pairs={{0,16},{8,24},{16,0},{24,8},{1,17},{9,25},{17,1},{25,9},{2,18},{10... | collective-permute-start | bytes 32 | tf_op jit(solution)/shard_map/ppermute | solution.py:75
  292.3 3.5 %collective-permute-start.48 = (f32[1,2]{1,0:T(1,128)S(1)}, f32[1,2]{1,0:T(1,128)S(1)}, u32[]{:S(2)}, u32[]{:S(2)}) collective-permute-start(f32[1,2]{1,0:T(1,128)S(1)} %square_sum.1.refs_0_), channel_id=1, source_target_pairs={{0,8},{8,0},{16,24},{24,16},{1,9},{9,1},{17,25},{25,17},{2,10},{10... | collective-permute-start | bytes 32 | tf_op jit(solution)/shard_map/ppermute | solution.py:75
  (37 other events, 243.9 us)

commit v4 on v3

--- a/solution.py
+++ b/solution.py
@@ -1246,7 +1246,7 @@
             held = gate(mid, mine)
         theirs = gather_cores(place, ours_mlp, mid)
         mlp_groups[index] = group_of(packs[index][1], ours_mlp, theirs)
-        pieces = mlp_groups[index] if index == 0 else [in_hbm(x) for x in mlp_groups[index]]
+        pieces = [in_hbm(x) if n < 2 * index else x for n, x in enumerate(mlp_groups[index])]
         y, act, gp = mlp_fwd(place, where, held, norms, pieces)
         if index + 1 < L:
             got = gates(ours_attn, y)

time: 308 us -> 308 us (level)
  no operation moved by 1% of the time
where the time goes in v4:
time: 308 us; the launch traced here: 307 us
  Pallas kernels  163 us (53%)
  waiting for transfers between devices  90.1 us (29%)
  starting transfers between devices  45.5 us (15%)
  between operations  4.43 us (1%)
    ppermute x51, waiting for transfers between devices, permute(): return lax.ppermute(x, axis, [(i, i ^ mask) for i in range(size)])  90.1 us
    ppermute x51, starting transfers between devices, permute(): return lax.ppermute(x, axis, [(i, i ^ mask) for i in range(size)])  45.5 us
    pallas_call x2, Pallas kernels, attn_bwd(): pl.pallas_call(kernel, grid=(seqs,), in_specs=[SMEM, row(D), row(D), row(...  23.4 us
    pallas_call x2, Pallas kernels, attn_fwd(): pl.pallas_call(kernel, grid=(seqs // SP,), in_specs=[SMEM, pl.BlockSpec((...  22.5 us
    pallas_call x2, Pallas kernels, mlp_fwd(): pl.pallas_call(kernel, grid=(n // tall,), in_specs=[SMEM, row(D), whole((...  21 us
    pallas_call x2, Pallas kernels, mlp_bwd(): pl.pallas_call(kernel, grid=(n // LEN,), in_specs=[SMEM, row(D), row(D),...  19.6 us
    pallas_call x2, Pallas kernels, grad_mlp(): pl.pallas_call(kernel, grid=(2 * steps + 1,), in_specs=[SMEM, whole((n, D...  18.7 us
    pallas_call x10, Pallas kernels, combine(): pl.pallas_call(kernel, grid=(2,), in_specs=[SMEM] + [block(a.shape) for a...  13.4 us
  transfers between devices with their start and end apart: 51, of which 27 were waited for; matrix products, arithmetic and copies ran while one was open for 1% of the time, Pallas kernels for 33%

profile of v4, /device:TPU:0, one launch (start us, length us, event | category | flops | bytes accessed | tf_op | source)
XLA Modules:
  0.0 306.8 jit_solution(9124017027089522609)
XLA Ops:
  0.8 2.3 pack.5
  3.1 3.9 %collective-permute-start.2 = (bf16[5,64,512]{2,1,0:T(8,128)(2,1)}, bf16[5,64,512]{2,1,0:T(8,128)(2,1)S(1)}, u32[]{:S(2)}, u32[]{:S(2)}) collective-permute-start(bf16[5,64,512]{2,1,0:T(8,128)(2,1)} %get-tuple-element.218), channel_id=1, source_target_pairs={{0,24},{8,16},{16,8},{24,0},{1,25},{9,17},{17,9},{25,1},{2,26},{10... | collective-permute-start | bytes 983048 | tf_op jit(solution)/shard_map/ppermute | solution.py:75
  7.9 2.2 pack.6
  10.1 2.8 pack.7
  12.9 2.8 pack.4
  15.8 6.1 %collective-permute-done.1.refs_2_ = bf16[5,64,512]{2,1,0:T(8,128)(2,1)S(1)} collective-permute-done((bf16[5,64,512]{2,1,0:T(8,128)(2,1)}, bf16[5,64,512]{2,1,0:T(8,128)(2,1)S(1)}, u32[]{:S(2)}, u32[]{:S(2)}) %collective-permute-start.1) | collective-permute-done | bytes 327712 | tf_op jit(solution)/shard_map/ppermute | solution.py:75
  23.3 1.6 collective-permute-start.6
  24.8 1.4 collective-permute-start.5
  27.0 3.6 %embed_step.1 = (f32[1024,512]{1,0:T(8,128)}, bf16[1024,64]{1,0:T(8,128)(2,1)S(1)}, bf16[64,512]{1,0:T(8,128)(2,1)S(1)}, f32[16,512]{1,0:T(8,128)S(1)}) custom-call(s32[6]{0:T(128)S(1)} %stack.42.where_ref, bf16[1024,64]{1,0:T(8,128)(2,1)S(1)} %reshape.110.target_ref, f32[1024,1]{1,0:T(8,128)S(1)} %copy.40.mask_ref, ...), custom_call_target="tpu_custom_call" | custom-call | flops 2013265920 | bytes 78643200 | tf_op jit(solution)/shard_map/embed_step/pallas_call | solution.py:479
  30.7 11.6 %attn_fwd.2 = (f32[1024,512]{1,0:T(8,128)}, bf16[1024,1536]{1,0:T(8,128)(2,1)}, bf16[4,8,256,256]{3,2,1,0:T(8,128)(2,1)}, bf16[4,512,256]{2,1,0:T(8,128)(2,1)}) custom-call(s32[6]{0:T(128)S(1)} %stack.42.where_ref, f32[1024,512]{1,0:T(8,128)} %get-tuple-element.227.x_ref, f32[4,512]{1,0:T(4,128)S(1)} %get-tuple-element.415.norm_ref, ...), custom_call_target="tpu_custom_call" | custom-call | flops 80530636800 | bytes 314572800 | tf_op jit(solution)/shard_map/attn_fwd/pallas_call | solution.py:582
  42.4 7.6 %collective-permute-done.5.refs_1_.refs_2_ = bf16[8,64,512]{2,1,0:T(8,128)(2,1)S(1)} collective-permute-done((bf16[8,64,512]{2,1,0:T(8,128)(2,1)}, bf16[8,64,512]{2,1,0:T(8,128)(2,1)S(1)}, u32[]{:S(2)}, u32[]{:S(2)}) %collective-permute-start.5) | collective-permute-done | bytes 524320 | tf_op jit(solution)/shard_map/ppermute | solution.py:75
  50.4 1.5 collective-permute-start.10
  51.9 1.4 collective-permute-start.9
  54.0 10.0 %mlp_fwd.2 = (f32[1024,512]{1,0:T(8,128)S(1)}, bf16[1024,2048]{1,0:T(8,128)(2,1)}, bf16[1024,2048]{1,0:T(8,128)(2,1)}) custom-call(s32[6]{0:T(128)S(1)} %stack.42.where_ref, f32[1024,512]{1,0:T(8,128)} %get-tuple-element.234.mid_ref, f32[4,512]{1,0:T(4,128)S(1)} %get-tuple-element.415.norm_ref, bf16[8,128,512]{2,1,0:T(8,128)(2,1)S(1)} %copy-done.28, ...), custom_call_target="tpu_custom_call" | custom-call | flops 128849018880 | bytes 377487360 | tf_op jit(solution)/shard_map/mlp_fwd/pallas_call | solution.py:657
  64.1 1.6 collective-permute-done.9.refs_1_.refs_2_
  65.9 1.5 collective-permute-start.14
  67.4 1.4 collective-permute-start.13
  69.4 10.8 %attn_fwd.3 = (f32[1024,512]{1,0:T(8,128)}, bf16[1024,1536]{1,0:T(8,128)(2,1)}, bf16[4,8,256,256]{3,2,1,0:T(8,128)(2,1)}, bf16[4,512,256]{2,1,0:T(8,128)(2,1)}) custom-call(s32[6]{0:T(128)S(1)} %stack.42.where_ref, f32[1024,512]{1,0:T(8,128)S(1)} %get-tuple-element.241.x_ref, f32[4,512]{1,0:T(4,128)S(1)} %get-tuple-element.414.norm_ref, ...), custom_call_target="tpu_custom_call" | custom-call | flops 80530636800 | bytes 314572800 | tf_op jit(solution)/shard_map/attn_fwd/pallas_call | solution.py:582
  80.4 1.3 collective-permute-done.14.refs_2_.refs_3_
  81.6 10.7 %collective-permute-done.13.refs_1_.refs_2_ = bf16[8,64,512]{2,1,0:T(8,128)(2,1)S(1)} collective-permute-done((bf16[8,64,512]{2,1,0:T(8,128)(2,1)S(1)}, bf16[8,64,512]{2,1,0:T(8,128)(2,1)S(1)}, u32[]{:S(2)}, u32[]{:S(2)}) %collective-permute-start.13) | collective-permute-done | bytes 524320 | tf_op jit(solution)/shard_map/ppermute | solution.py:75
  94.1 2.6 collective-permute-done.15.refs_4_
  96.7 11.0 %mlp_fwd.3 = (f32[1024,512]{1,0:T(8,128)S(1)}, bf16[1024,2048]{1,0:T(8,128)(2,1)}, bf16[1024,2048]{1,0:T(8,128)(2,1)}) custom-call(s32[6]{0:T(128)S(1)} %stack.42.where_ref, f32[1024,512]{1,0:T(8,128)} %get-tuple-element.246.mid_ref, f32[4,512]{1,0:T(4,128)S(1)} %get-tuple-element.414.norm_ref, bf16[8,128,512]{2,1,0:T(8,128)(2,1)} %get-tuple-element.247.refs_0_, ...), custom_call_target="tpu_custom_call" | custom-call | flops 128849018880 | bytes 377487360 | tf_op jit(solution)/shard_map/mlp_fwd/pallas_call | solution.py:657
  107.8 3.8 %head_step.1 = (f32[1024,512]{1,0:T(8,128)S(1)}, f32[1,64]{1,0:T(1,128)S(1)}, f32[64,512]{1,0:T(8,128)S(1)}, f32[8,512]{1,0:T(8,128)S(1)}) custom-call(f32[1024,512]{1,0:T(8,128)S(1)} %get-tuple-element.251.x_ref, bf16[1024,64]{1,0:T(8,128)(2,1)S(1)} %copy-done.15, f32[1024,1]{1,0:T(8,128)S(1)} %copy.41.mask_ref, ...), custom_call_target="tpu_custom_call" | custom-call | flops 6039797760 | bytes 125829120 | tf_op jit(solution)/shard_map/head_step/pallas_call | solution.py:881
  111.6 10.4 %mlp_bwd.2 = (f32[1024,512]{1,0:T(8,128)S(1)}, bf16[1024,512]{1,0:T(8,128)(2,1)S(1)}, bf16[1024,2048]{1,0:T(8,128)(2,1)}, bf16[1024,512]{1,0:T(8,128)(2,1)S(1)},...) custom-call(s32[6]{0:T(128)S(1)} %stack.42.where_ref, f32[1024,512]{1,0:T(8,128)S(1)} %get-tuple-element.254.dz_ref, ...), custom_call_target="tpu_custom_call" | custom-call | flops 128849018880 | bytes 503316480 | tf_op jit(solution)/shard_map/mlp_bwd/pallas_call | solution.py:724
  122.1 9.5 %grad_mlp.2 = (bf16[4,9,64,512]{3,2,1,0:T(8,128)(2,1)S(1)}, bf16[4,9,64,512]{3,2,1,0:T(8,128)(2,1)S(1)}) custom-call(s32[6]{0:T(128)S(1)} %stack.42.where_ref, bf16[1024,512]{1,0:T(8,128)(2,1)S(1)} %get-tuple-element.256.c_ref, bf16[1024,2048]{1,0:T(8,128)(2,1)} %get-tuple-element.257.du_ref, bf16[1024,2048]{1,0:T(8,128)(2,1)} %get-tuple-element.258.act_ref, ...), custom_call_target="tpu_custom_call" | custom-call | flops 128849018880 | bytes 440401920 | tf_op jit(solution)/shard_map/grad_mlp/pallas_call | solution.py:952
  131.9 11.1 %attn_bwd.2 = (f32[1024,512]{1,0:T(8,128)S(1)}, bf16[1024,1536]{1,0:T(8,128)(2,1)S(1)}, bf16[1024,512]{1,0:T(8,128)(2,1)S(1)}, f32[8,512]{1,0:T(8,128)S(1)}) custom-call(s32[6]{0:T(128)S(1)} %stack.42.where_ref, f32[1024,512]{1,0:T(8,128)S(1)} %get-tuple-element.265.dmid_ref, bf16[1024,512]{1,0:T(8,128)(2,1)S(1)} %get-tuple-element.261.dh_ref, ...), custom_call_target="tpu_custom_call" | custom-call | flops 104689827840 | bytes 503316480 | tf_op jit(solution)/shard_map/attn_bwd/pallas_call | solution.py:821
  143.1 1.5 sum_round.10
  144.6 1.5 collective-permute-start.18
  146.7 9.2 %mlp_bwd.3 = (f32[1024,512]{1,0:T(8,128)S(1)}, bf16[1024,512]{1,0:T(8,128)(2,1)S(1)}, bf16[1024,2048]{1,0:T(8,128)(2,1)}, bf16[1024,512]{1,0:T(8,128)(2,1)S(1)},...) custom-call(s32[6]{0:T(128)S(1)} %stack.42.where_ref, f32[1024,512]{1,0:T(8,128)S(1)} %get-tuple-element.275.dz_ref, ...), custom_call_target="tpu_custom_call" | custom-call | flops 128849018880 | bytes 503316480 | tf_op jit(solution)/shard_map/mlp_bwd/pallas_call | solution.py:724
  155.9 4.0 %collective-permute-done.19.refs_3_ = bf16[2,4,64,512]{3,2,1,0:T(8,128)(2,1)S(1)} collective-permute-done((bf16[2,4,64,512]{3,2,1,0:T(8,128)(2,1)S(1)}, bf16[2,4,64,512]{3,2,1,0:T(8,128)(2,1)S(1)}, u32[]{:S(2)}, u32[]{:S(2)}) %collective-permute-start.19) | collective-permute-done | bytes 524320 | tf_op jit(solution)/shard_map/ppermute | solution.py:75
  159.9 1.7 collective-permute-done.18.refs_1_
  162.6 1.5 collective-permute-start.20
  164.8 9.2 %grad_mlp.3 = (bf16[4,9,64,512]{3,2,1,0:T(8,128)(2,1)S(1)}, bf16[4,9,64,512]{3,2,1,0:T(8,128)(2,1)S(1)}) custom-call(s32[6]{0:T(128)S(1)} %stack.42.where_ref, bf16[1024,512]{1,0:T(8,128)(2,1)S(1)} %get-tuple-element.287.c_ref, bf16[1024,2048]{1,0:T(8,128)(2,1)} %get-tuple-element.288.du_ref, bf16[1024,2048]{1,0:T(8,128)(2,1)} %get-tuple-element.289.act_ref, ...), custom_call_target="tpu_custom_call" | custom-call | flops 128849018880 | bytes 440401920 | tf_op jit(solution)/shard_map/grad_mlp/pallas_call | solution.py:952
  174.1 1.4 sum_round.12
  175.5 2.7 collective-permute-start.22
  178.2 3.2 %grad_qkv.2 = (bf16[4,3,64,512]{3,2,1,0:T(8,128)(2,1)S(1)}, bf16[4,3,64,512]{3,2,1,0:T(8,128)(2,1)S(1)}) custom-call(s32[6]{0:T(128)S(1)} %stack.42.where_ref, bf16[1024,512]{1,0:T(8,128)(2,1)S(1)} %get-tuple-element.302.a_ref, bf16[1024,1536]{1,0:T(8,128)(2,1)S(1)} %get-tuple-element.303.dqkv_ref), custom_call_target="tpu_custom_call" | custom-call | flops 48318382080 | bytes 173015040 | tf_op jit(solution)/shard_map/grad_qkv/pallas_call | solution.py:1029
  181.8 1.7 sum_round.13
  183.5 1.3 collective-permute-start.24
  185.5 12.3 %attn_bwd.3 = (f32[1024,512]{1,0:T(8,128)S(1)}, bf16[1024,1536]{1,0:T(8,128)(2,1)S(1)}, bf16[1024,512]{1,0:T(8,128)(2,1)S(1)}, f32[8,512]{1,0:T(8,128)S(1)}) custom-call(s32[6]{0:T(128)S(1)} %stack.42.where_ref, f32[1024,512]{1,0:T(8,128)S(1)} %get-tuple-element.312.dmid_ref, bf16[1024,512]{1,0:T(8,128)(2,1)S(1)} %get-tuple-element.292.dh_ref, ...), custom_call_target="tpu_custom_call" | custom-call | flops 104689827840 | bytes 503316480 | tf_op jit(solution)/shard_map/attn_bwd/pallas_call | solution.py:821
  198.7 1.8 collective-permute-done.24.refs_3_
  200.5 2.3 sum_round.14
  202.8 3.8 %grad_qkv.3 = (bf16[4,4,64,512]{3,2,1,0:T(8,128)(2,1)S(1)}, bf16[4,4,64,512]{3,2,1,0:T(8,128)(2,1)S(1)}) custom-call(s32[6]{0:T(128)S(1)} %stack.42.where_ref, bf16[1024,512]{1,0:T(8,128)(2,1)S(1)} %get-tuple-element.331.a_ref, bf16[1024,1536]{1,0:T(8,128)(2,1)S(1)} %get-tuple-element.332.dqkv_ref, bf16[1024,64]{1,0:T(8,128)(2,1)S(1)} %copy-done.37, ...), custom_call_target="tpu_custom_call" | custom-call | flops 48318382080 | bytes 173015040 | tf_op jit(solution)/shard_map/grad_qkv/pallas_call | solution.py:1029
  206.8 1.3 collective-permute-start.28
  208.1 1.6 collective-permute-start.27
  210.3 7.5 %collective-permute-done.29.refs_5_ = bf16[4,64,512]{2,1,0:T(8,128)(2,1)S(1)} collective-permute-done((bf16[4,64,512]{2,1,0:T(8,128)(2,1)S(1)}, bf16[4,64,512]{2,1,0:T(8,128)(2,1)S(1)}, u32[]{:S(2)}, u32[]{:S(2)}) %collective-permute-start.29) | collective-permute-done | bytes 262176 | tf_op jit(solution)/shard_map/ppermute | solution.py:75
  217.7 1.9 sum_round.15
  220.3 1.4 collective-permute-start.32
  225.8 2.5 collective-permute-start.31
  230.7 1.9 collective-permute-done.33.refs_3_
  233.6 1.1 collective-permute-start.40
  234.7 1.1 collective-permute-start.39
  235.7 1.6 collective-permute-start.35
  237.4 6.4 %collective-permute-done.35 = f32[1,1]{1,0:T(1,128)} collective-permute-done((f32[1,1]{1,0:T(1,128)}, f32[1,1]{1,0:T(1,128)}, u32[]{:S(2)}, u32[]{:S(2)}) %collective-permute-start.35) | collective-permute-done | bytes 36 | tf_op jit(solution)/shard_map/ppermute | solution.py:75
  245.3 1.3 collective-permute-start.42
  246.6 14.8 %collective-permute-done.42.refs_3_ = bf16[9,32,512]{2,1,0:T(8,128)(2,1)S(1)} collective-permute-done((bf16[9,32,512]{2,1,0:T(8,128)(2,1)S(1)}, bf16[9,32,512]{2,1,0:T(8,128)(2,1)S(1)}, u32[]{:S(2)}, u32[]{:S(2)}) %collective-permute-start.42) | collective-permute-done | bytes 294944 | tf_op jit(solution)/shard_map/ppermute | solution.py:75
  261.4 2.2 collective-permute-done.41.refs_1_
  264.5 1.3 collective-permute-start.46
  265.7 7.1 %fetch.1 = (f32[2,128,1536]{2,1,0:T(8,128)S(1)}, f32[2,128,1536]{2,1,0:T(8,128)S(1)}, f32[2,128,1536]{2,1,0:T(8,128)S(1)}, f32[2,128,512]{2,1,0:T(8,128)S(1)}, f...) custom-call(s32[6]{0:T(128)S(1)} %stack.42.where_ref, ...), custom_call_target="tpu_custom_call" | custom-call | tf_op jit(solution)/shard_map/fetch/pallas_call | solution.py:1064
  272.9 8.1 %collective-permute-done.44.refs_6_.refs_8_ = bf16[9,32,512]{2,1,0:T(8,128)(2,1)S(1)} collective-permute-done((bf16[9,32,512]{2,1,0:T(8,128)(2,1)S(1)}, bf16[9,32,512]{2,1,0:T(8,128)(2,1)S(1)}, u32[]{:S(2)}, u32[]{:S(2)}) %collective-permute-start.44) | collective-permute-done | bytes 294944 | tf_op jit(solution)/shard_map/ppermute | solution.py:75
  281.0 4.7 %collective-permute-done.46.refs_1_ = bf16[7,64,512]{2,1,0:T(8,128)(2,1)S(1)} collective-permute-done((bf16[7,64,512]{2,1,0:T(8,128)(2,1)S(1)}, bf16[7,64,512]{2,1,0:T(8,128)(2,1)S(1)}, u32[]{:S(2)}, u32[]{:S(2)}) %collective-permute-start.46) | collective-permute-done | bytes 458784 | tf_op jit(solution)/shard_map/ppermute | solution.py:75
  287.1 1.6 collective-permute-done.38.refs_3_.refs_13_
  289.8 1.4 collective-permute-start.50
  291.9 1.4 collective-permute-start.48
  295.4 11.2 %adam_step.1 = (f32[2,128,1536]{2,1,0:T(8,128)}, f32[2,128,1536]{2,1,0:T(8,128)}, f32[2,128,1536]{2,1,0:T(8,128)}, f32[2,128,512]{2,1,0:T(8,128)}, f32[2,128,512...) custom-call(s32[6]{0:T(128)S(1)} %stack.42.where_ref, ...), custom_call_target="tpu_custom_call" | custom-call | flops 943718400 | bytes 1132462080 | tf_op jit(solution)/shard_map/adam_step/pallas_call | solution.py:1160
  (174 shorter events, 25.2 us)
Async XLA Ops:
  3.1 12.7 %collective-permute-start.2 = (bf16[5,64,512]{2,1,0:T(8,128)(2,1)}, bf16[5,64,512]{2,1,0:T(8,128)(2,1)S(1)}, u32[]{:S(2)}, u32[]{:S(2)}) collective-permute-start(bf16[5,64,512]{2,1,0:T(8,128)(2,1)} %get-tuple-element.218), channel_id=1, source_target_pairs={{0,24},{8,16},{16,8},{24,0},{1,25},{9,17},{17,9},{25,1},{2,26},{10... | collective-permute-start | bytes 983048 | tf_op jit(solution)/shard_map/ppermute | solution.py:75
  7.0 14.9 %collective-permute-start.1 = (bf16[5,64,512]{2,1,0:T(8,128)(2,1)}, bf16[5,64,512]{2,1,0:T(8,128)(2,1)S(1)}, u32[]{:S(2)}, u32[]{:S(2)}) collective-permute-start(bf16[5,64,512]{2,1,0:T(8,128)(2,1)} %get-tuple-element.218), channel_id=1, source_target_pairs={{0,16},{8,24},{16,0},{24,8},{1,17},{9,25},{17,1},{25,9},{2,18},{10... | collective-permute-start | bytes 983048 | tf_op jit(solution)/shard_map/ppermute | solution.py:75
  7.5 14.7 %collective-permute-start = (bf16[5,64,512]{2,1,0:T(8,128)(2,1)}, bf16[5,64,512]{2,1,0:T(8,128)(2,1)S(1)}, u32[]{:S(2)}, u32[]{:S(2)}) collective-permute-start(bf16[5,64,512]{2,1,0:T(8,128)(2,1)} %get-tuple-element.218), channel_id=1, source_target_pairs={{0,8},{8,0},{16,24},{24,16},{1,9},{9,1},{17,25},{25,17},{2,10},{10... | collective-permute-start | bytes 983048 | tf_op jit(solution)/shard_map/ppermute | solution.py:75
  7.6 19.2 %copy-start.41 = (f32[1,1,4,256]{3,1,2,0:T(1,128)}, f32[1,1,4,256]{3,1,2,0:T(1,128)S(1)}, u32[]{:S(2)}) copy-start(f32[1,1,4,256]{3,1,2,0:T(1,128)S(1)} %copy.42) | copy-start | bytes 12292
  7.8 19.2 %copy-start.14 = (bf16[1024,64]{1,0:T(8,128)(2,1)}, bf16[1024,64]{1,0:T(8,128)(2,1)S(1)}, u32[]{:S(2)}) copy-start(bf16[1024,64]{1,0:T(8,128)(2,1)S(1)} %reshape.110.target_ref) | copy-start | bytes 393220
  15.8 14.9 %copy-start.8 = (bf16[5,64,512]{2,1,0:T(8,128)(2,1)}, bf16[5,64,512]{2,1,0:T(8,128)(2,1)S(1)}, u32[]{:S(2)}) copy-start(bf16[5,64,512]{2,1,0:T(8,128)(2,1)S(1)} %collective-permute-done.2.refs_3_) | copy-start | bytes 983044
  23.3 3.7 %collective-permute-start.3 = (bf16[3,5,64,512]{3,2,1,0:T(8,128)(2,1)}, bf16[3,5,64,512]{3,2,1,0:T(8,128)(2,1)}, u32[]{:S(2)}, u32[]{:S(2)}) collective-permute-start(bf16[3,5,64,512]{3,2,1,0:T(8,128)(2,1)} %pad_maximum_fusion), channel_id=1, source_target_pairs={{0,1},{1,0},{2,3},{3,2},{4,5},{5,4},{6,7},{7,6},{8,9},{9,8},{10,11... | collective-permute-start | bytes 2949128 | tf_op jit(solution)/shard_map/ppermute | solution.py:75
  23.3 19.1 %collective-permute-start.6 = (bf16[8,64,512]{2,1,0:T(8,128)(2,1)}, bf16[8,64,512]{2,1,0:T(8,128)(2,1)S(1)}, u32[]{:S(2)}, u32[]{:S(2)}) collective-permute-start(bf16[8,64,512]{2,1,0:T(8,128)(2,1)} %get-tuple-element.219), channel_id=1, source_target_pairs={{0,24},{8,16},{16,8},{24,0},{1,25},{9,17},{17,9},{25,1},{2,26},{10... | collective-permute-start | bytes 1572872 | tf_op jit(solution)/shard_map/ppermute | solution.py:75
  24.8 25.1 %collective-permute-start.5 = (bf16[8,64,512]{2,1,0:T(8,128)(2,1)}, bf16[8,64,512]{2,1,0:T(8,128)(2,1)S(1)}, u32[]{:S(2)}, u32[]{:S(2)}) collective-permute-start(bf16[8,64,512]{2,1,0:T(8,128)(2,1)} %get-tuple-element.219), channel_id=1, source_target_pairs={{0,16},{8,24},{16,0},{24,8},{1,17},{9,25},{17,1},{25,9},{2,18},{10... | collective-permute-start | bytes 1572872 | tf_op jit(solution)/shard_map/ppermute | solution.py:75
  26.2 23.8 %collective-permute-start.4 = (bf16[8,64,512]{2,1,0:T(8,128)(2,1)}, bf16[8,64,512]{2,1,0:T(8,128)(2,1)S(1)}, u32[]{:S(2)}, u32[]{:S(2)}) collective-permute-start(bf16[8,64,512]{2,1,0:T(8,128)(2,1)} %get-tuple-element.219), channel_id=1, source_target_pairs={{0,8},{8,0},{16,24},{24,16},{1,9},{9,1},{17,25},{25,17},{2,10},{10... | collective-permute-start | bytes 1572872 | tf_op jit(solution)/shard_map/ppermute | solution.py:75
  30.7 23.3 %copy-start.23 = (f32[4,512]{1,0:T(4,128)}, f32[4,512]{1,0:T(4,128)S(1)}, u32[]{:S(2)}) copy-start(f32[4,512]{1,0:T(4,128)S(1)} %get-tuple-element.415.norm_ref) | copy-start | bytes 24580
  42.4 21.6 %copy-start = (bf16[8,64,512]{2,1,0:T(8,128)(2,1)}, bf16[8,64,512]{2,1,0:T(8,128)(2,1)S(1)}, u32[]{:S(2)}) copy-start(bf16[8,64,512]{2,1,0:T(8,128)(2,1)S(1)} %collective-permute-done.6.refs_2_.refs_3_) | copy-start | bytes 1572868
  50.0 14.0 %copy-start.2 = (bf16[8,64,512]{2,1,0:T(8,128)(2,1)}, bf16[8,64,512]{2,1,0:T(8,128)(2,1)S(1)}, u32[]{:S(2)}) copy-start(bf16[8,64,512]{2,1,0:T(8,128)(2,1)S(1)} %collective-permute-done.5.refs_1_.refs_2_) | copy-start | bytes 1572868
  50.1 13.9 %copy-start.4 = (bf16[8,64,512]{2,1,0:T(8,128)(2,1)}, bf16[8,64,512]{2,1,0:T(8,128)(2,1)S(1)}, u32[]{:S(2)}) copy-start(bf16[8,64,512]{2,1,0:T(8,128)(2,1)S(1)} %collective-permute-done.4.refs_0_.refs_1_) | copy-start | bytes 1572868
  50.3 3.6 %collective-permute-start.7 = (bf16[3,8,64,512]{3,2,1,0:T(8,128)(2,1)S(1)}, bf16[3,8,64,512]{3,2,1,0:T(8,128)(2,1)S(1)}, u32[]{:S(2)}, u32[]{:S(2)}) collective-permute-start(bf16[3,8,64,512]{3,2,1,0:T(8,128)(2,1)S(1)} %stack.47), channel_id=1, source_target_pairs={{0,1},{1,0},{2,3},{3,2},{4,5},{5,4},{6,7},{7,6},{8,9},{9,8},{10,11... | collective-permute-start | bytes 4718600 | tf_op jit(solution)/shard_map/ppermute | solution.py:75
  50.4 13.6 %collective-permute-start.10 = (bf16[4,64,512]{2,1,0:T(8,128)(2,1)S(1)}, bf16[4,64,512]{2,1,0:T(8,128)(2,1)S(1)}, u32[]{:S(2)}, u32[]{:S(2)}) collective-permute-start(bf16[4,64,512]{2,1,0:T(8,128)(2,1)S(1)} %copy-done.45), channel_id=1, source_target_pairs={{0,24},{8,16},{16,8},{24,0},{1,25},{9,17},{17,9},{25,1},{2,26},{10... | collective-permute-start | bytes 786440 | tf_op jit(solution)/shard_map/ppermute | solution.py:75
  51.9 13.7 %collective-permute-start.9 = (bf16[4,64,512]{2,1,0:T(8,128)(2,1)S(1)}, bf16[4,64,512]{2,1,0:T(8,128)(2,1)S(1)}, u32[]{:S(2)}, u32[]{:S(2)}) collective-permute-start(bf16[4,64,512]{2,1,0:T(8,128)(2,1)S(1)} %copy-done.45), channel_id=1, source_target_pairs={{0,16},{8,24},{16,0},{24,8},{1,17},{9,25},{17,1},{25,9},{2,18},{10... | collective-permute-start | bytes 786440 | tf_op jit(solution)/shard_map/ppermute | solution.py:75
  53.3 12.3 %collective-permute-start.8 = (bf16[4,64,512]{2,1,0:T(8,128)(2,1)S(1)}, bf16[4,64,512]{2,1,0:T(8,128)(2,1)S(1)}, u32[]{:S(2)}, u32[]{:S(2)}) collective-permute-start(bf16[4,64,512]{2,1,0:T(8,128)(2,1)S(1)} %copy-done.45), channel_id=1, source_target_pairs={{0,8},{8,0},{16,24},{24,16},{1,9},{9,1},{17,25},{25,17},{2,10},{10... | collective-permute-start | bytes 786440 | tf_op jit(solution)/shard_map/ppermute | solution.py:75
  54.0 11.9 %copy-start.44 = (bf16[8,64,512]{2,1,0:T(8,128)(2,1)S(1)}, bf16[8,64,512]{2,1,0:T(8,128)(2,1)}, u32[]{:S(2)}) copy-start(bf16[8,64,512]{2,1,0:T(8,128)(2,1)} %get-tuple-element.240) | copy-start | bytes 1572868
  64.0 16.3 %copy-start.38 = (f32[1024,512]{1,0:T(8,128)}, f32[1024,512]{1,0:T(8,128)S(1)}, u32[]{:S(2)}) copy-start(f32[1024,512]{1,0:T(8,128)S(1)} %get-tuple-element.241.x_ref) | copy-start | bytes 6291460
  64.0 16.3 %copy-start.16 = (bf16[4,64,512]{2,1,0:T(8,128)(2,1)}, bf16[4,64,512]{2,1,0:T(8,128)(2,1)S(1)}, u32[]{:S(2)}) copy-start(bf16[4,64,512]{2,1,0:T(8,128)(2,1)S(1)} %collective-permute-done.10.refs_2_.refs_3_) | copy-start | bytes 786436
  65.6 14.7 %copy-start.18 = (bf16[4,64,512]{2,1,0:T(8,128)(2,1)}, bf16[4,64,512]{2,1,0:T(8,128)(2,1)S(1)}, u32[]{:S(2)}) copy-start(bf16[4,64,512]{2,1,0:T(8,128)(2,1)S(1)} %collective-permute-done.9.refs_1_.refs_2_) | copy-start | bytes 786436
  65.7 14.7 %copy-start.20 = (bf16[4,64,512]{2,1,0:T(8,128)(2,1)}, bf16[4,64,512]{2,1,0:T(8,128)(2,1)S(1)}, u32[]{:S(2)}) copy-start(bf16[4,64,512]{2,1,0:T(8,128)(2,1)S(1)} %collective-permute-done.8.refs_0_.refs_1_) | copy-start | bytes 786436
  65.8 3.6 %collective-permute-start.11 = (bf16[3,4,64,512]{3,2,1,0:T(8,128)(2,1)S(1)}, bf16[3,4,64,512]{3,2,1,0:T(8,128)(2,1)S(1)}, u32[]{:S(2)}, u32[]{:S(2)}) collective-permute-start(bf16[3,4,64,512]{3,2,1,0:T(8,128)(2,1)S(1)} %stack.48), channel_id=1, source_target_pairs={{0,1},{1,0},{2,3},{3,2},{4,5},{5,4},{6,7},{7,6},{8,9},{9,8},{10,11... | collective-permute-start | bytes 2359304 | tf_op jit(solution)/shard_map/ppermute | solution.py:75
  65.9 15.7 %collective-permute-start.14 = (bf16[8,64,512]{2,1,0:T(8,128)(2,1)S(1)}, bf16[8,64,512]{2,1,0:T(8,128)(2,1)S(1)}, u32[]{:S(2)}, u32[]{:S(2)}) collective-permute-start(bf16[8,64,512]{2,1,0:T(8,128)(2,1)S(1)} %copy-done.44), channel_id=1, source_target_pairs={{0,24},{8,16},{16,8},{24,0},{1,25},{9,17},{17,9},{25,1},{2,26},{10... | collective-permute-start | bytes 1572872 | tf_op jit(solution)/shard_map/ppermute | solution.py:75
  67.4 24.9 %collective-permute-start.13 = (bf16[8,64,512]{2,1,0:T(8,128)(2,1)S(1)}, bf16[8,64,512]{2,1,0:T(8,128)(2,1)S(1)}, u32[]{:S(2)}, u32[]{:S(2)}) collective-permute-start(bf16[8,64,512]{2,1,0:T(8,128)(2,1)S(1)} %copy-done.44), channel_id=1, source_target_pairs={{0,16},{8,24},{16,0},{24,8},{1,17},{9,25},{17,1},{25,9},{2,18},{10... | collective-permute-start | bytes 1572872 | tf_op jit(solution)/shard_map/ppermute | solution.py:75
  68.8 23.5 %collective-permute-start.12 = (bf16[8,64,512]{2,1,0:T(8,128)(2,1)S(1)}, bf16[8,64,512]{2,1,0:T(8,128)(2,1)S(1)}, u32[]{:S(2)}, u32[]{:S(2)}) collective-permute-start(bf16[8,64,512]{2,1,0:T(8,128)(2,1)S(1)} %copy-done.44), channel_id=1, source_target_pairs={{0,8},{8,0},{16,24},{24,16},{1,9},{9,1},{17,25},{25,17},{2,10},{10... | collective-permute-start | bytes 1572872 | tf_op jit(solution)/shard_map/ppermute | solution.py:75
  80.3 12.8 %copy-start.42 = (f32[1,1,4,256]{3,1,2,0:T(1,128)S(1)}, f32[1,1,4,256]{3,1,2,0:T(1,128)}, u32[]{:S(2)}) copy-start(f32[1,1,4,256]{3,1,2,0:T(1,128)} %copy-done.41) | copy-start | bytes 12292
  93.2 3.5 %collective-permute-start.15 = (bf16[3,8,64,512]{3,2,1,0:T(8,128)(2,1)S(1)}, bf16[3,8,64,512]{3,2,1,0:T(8,128)(2,1)}, u32[]{:S(2)}, u32[]{:S(2)}) collective-permute-start(bf16[3,8,64,512]{3,2,1,0:T(8,128)(2,1)S(1)} %stack.49), channel_id=1, source_target_pairs={{0,1},{1,0},{2,3},{3,2},{4,5},{5,4},{6,7},{7,6},{8,9},{9,8},{10,11... | collective-permute-start | bytes 4718600 | tf_op jit(solution)/shard_map/ppermute | solution.py:75
  131.6 11.4 %collective-permute-start.17 = (bf16[4,9,64,512]{3,2,1,0:T(8,128)(2,1)S(1)}, bf16[4,9,64,512]{3,2,1,0:T(8,128)(2,1)S(1)}, u32[]{:S(2)}, u32[]{:S(2)}) collective-permute-start(bf16[4,9,64,512]{3,2,1,0:T(8,128)(2,1)S(1)} %get-tuple-element.263), channel_id=1, source_target_pairs={{0,1},{1,0},{2,3},{3,2},{4,5},{5,4},{6,7},{7,6},{8,9},{9,8},{10,11... | collective-permute-start | bytes 7077896 | tf_op jit(solution)/shard_map/ppermute | solution.py:75
  144.6 17.0 %collective-permute-start.18 = (bf16[2,5,64,512]{3,2,1,0:T(8,128)(2,1)S(1)}, bf16[2,5,64,512]{3,2,1,0:T(8,128)(2,1)S(1)}, u32[]{:S(2)}, u32[]{:S(2)}) collective-permute-start(bf16[2,5,64,512]{3,2,1,0:T(8,128)(2,1)S(1)} %get-tuple-element.272), channel_id=1, source_target_pairs={{0,8},{8,0},{16,24},{24,16},{1,9},{9,1},{17,25},{25,17},{2,10},{10... | collective-permute-start | bytes 1966088 | tf_op jit(solution)/shard_map/ppermute | solution.py:75
  146.0 13.9 %collective-permute-start.19 = (bf16[2,4,64,512]{3,2,1,0:T(8,128)(2,1)S(1)}, bf16[2,4,64,512]{3,2,1,0:T(8,128)(2,1)S(1)}, u32[]{:S(2)}, u32[]{:S(2)}) collective-permute-start(bf16[2,4,64,512]{3,2,1,0:T(8,128)(2,1)S(1)} %get-tuple-element.274), channel_id=1, source_target_pairs={{0,16},{8,24},{16,0},{24,8},{1,17},{9,25},{17,1},{25,9},{2,18},{10... | collective-permute-start | bytes 1572872 | tf_op jit(solution)/shard_map/ppermute | solution.py:75
  162.6 11.4 %collective-permute-start.20 = (bf16[5,64,512]{2,1,0:T(8,128)(2,1)S(1)}, bf16[5,64,512]{2,1,0:T(8,128)(2,1)S(1)}, u32[]{:S(2)}, u32[]{:S(2)}) collective-permute-start(bf16[5,64,512]{2,1,0:T(8,128)(2,1)S(1)} %get-tuple-element.283), channel_id=1, source_target_pairs={{0,16},{8,24},{16,0},{24,8},{1,17},{9,25},{17,1},{25,9},{2,18},{10... | collective-permute-start | bytes 983048 | tf_op jit(solution)/shard_map/ppermute | solution.py:75
  164.1 9.9 %collective-permute-start.21 = (bf16[4,64,512]{2,1,0:T(8,128)(2,1)S(1)}, bf16[4,64,512]{2,1,0:T(8,128)(2,1)S(1)}, u32[]{:S(2)}, u32[]{:S(2)}) collective-permute-start(bf16[4,64,512]{2,1,0:T(8,128)(2,1)S(1)} %get-tuple-element.285), channel_id=1, source_target_pairs={{0,8},{8,0},{16,24},{24,16},{1,9},{9,1},{17,25},{25,17},{2,10},{10... | collective-permute-start | bytes 786440 | tf_op jit(solution)/shard_map/ppermute | solution.py:75
  174.0 7.8 %collective-permute-start.23 = (bf16[4,9,64,512]{3,2,1,0:T(8,128)(2,1)S(1)}, bf16[4,9,64,512]{3,2,1,0:T(8,128)(2,1)S(1)}, u32[]{:S(2)}, u32[]{:S(2)}) collective-permute-start(bf16[4,9,64,512]{3,2,1,0:T(8,128)(2,1)S(1)} %get-tuple-element.293), channel_id=1, source_target_pairs={{0,1},{1,0},{2,3},{3,2},{4,5},{5,4},{6,7},{7,6},{8,9},{9,8},{10,11... | collective-permute-start | bytes 7077896 | tf_op jit(solution)/shard_map/ppermute | solution.py:75
  175.5 22.2 %collective-permute-start.22 = (bf16[9,32,512]{2,1,0:T(8,128)(2,1)}, bf16[9,32,512]{2,1,0:T(8,128)(2,1)}, u32[]{:S(2)}, u32[]{:S(2)}) collective-permute-start(bf16[9,32,512]{2,1,0:T(8,128)(2,1)} %get-tuple-element.299), channel_id=1, source_target_pairs={{0,4},{1,5},{2,6},{3,7},{4,0},{5,1},{6,2},{7,3},{8,12},{9,13},{10,... | collective-permute-start | bytes 884744 | tf_op jit(solution)/shard_map/ppermute | solution.py:75
  181.5 16.3 %collective-permute-start.26 = (bf16[4,3,64,512]{3,2,1,0:T(8,128)(2,1)S(1)}, bf16[4,3,64,512]{3,2,1,0:T(8,128)(2,1)S(1)}, u32[]{:S(2)}, u32[]{:S(2)}) collective-permute-start(bf16[4,3,64,512]{3,2,1,0:T(8,128)(2,1)S(1)} %get-tuple-element.304), channel_id=1, source_target_pairs={{0,1},{1,0},{2,3},{3,2},{4,5},{5,4},{6,7},{7,6},{8,9},{9,8},{10,11... | collective-permute-start | bytes 2359304 | tf_op jit(solution)/shard_map/ppermute | solution.py:75
  183.5 17.0 %collective-permute-start.24 = (bf16[2,5,64,512]{3,2,1,0:T(8,128)(2,1)S(1)}, bf16[2,5,64,512]{3,2,1,0:T(8,128)(2,1)S(1)}, u32[]{:S(2)}, u32[]{:S(2)}) collective-permute-start(bf16[2,5,64,512]{3,2,1,0:T(8,128)(2,1)S(1)} %get-tuple-element.308), channel_id=1, source_target_pairs={{0,8},{8,0},{16,24},{24,16},{1,9},{9,1},{17,25},{25,17},{2,10},{10... | collective-permute-start | bytes 1966088 | tf_op jit(solution)/shard_map/ppermute | solution.py:75
  184.8 13.9 %collective-permute-start.25 = (bf16[2,4,64,512]{3,2,1,0:T(8,128)(2,1)S(1)}, bf16[2,4,64,512]{3,2,1,0:T(8,128)(2,1)S(1)}, u32[]{:S(2)}, u32[]{:S(2)}) collective-permute-start(bf16[2,4,64,512]{3,2,1,0:T(8,128)(2,1)S(1)} %get-tuple-element.310), channel_id=1, source_target_pairs={{0,16},{8,24},{16,0},{24,8},{1,17},{9,25},{17,1},{25,9},{2,18},{10... | collective-permute-start | bytes 1572872 | tf_op jit(solution)/shard_map/ppermute | solution.py:75
  206.7 11.1 %collective-permute-start.30 = (bf16[4,4,64,512]{3,2,1,0:T(8,128)(2,1)S(1)}, bf16[4,4,64,512]{3,2,1,0:T(8,128)(2,1)S(1)}, u32[]{:S(2)}, u32[]{:S(2)}) collective-permute-start(bf16[4,4,64,512]{3,2,1,0:T(8,128)(2,1)S(1)} %get-tuple-element.341), channel_id=1, source_target_pairs={{0,1},{1,0},{2,3},{3,2},{4,5},{5,4},{6,7},{7,6},{8,9},{9,8},{10,11... | collective-permute-start | bytes 3145736 | tf_op jit(solution)/shard_map/ppermute | solution.py:75
  206.8 11.0 %collective-permute-start.28 = (bf16[5,64,512]{2,1,0:T(8,128)(2,1)S(1)}, bf16[5,64,512]{2,1,0:T(8,128)(2,1)S(1)}, u32[]{:S(2)}, u32[]{:S(2)}) collective-permute-start(bf16[5,64,512]{2,1,0:T(8,128)(2,1)S(1)} %get-tuple-element.326), channel_id=1, source_target_pairs={{0,16},{8,24},{16,0},{24,8},{1,17},{9,25},{17,1},{25,9},{2,18},{10... | collective-permute-start | bytes 983048 | tf_op jit(solution)/shard_map/ppermute | solution.py:75
  208.1 9.7 %collective-permute-start.27 = (bf16[9,32,512]{2,1,0:T(8,128)(2,1)S(1)}, bf16[9,32,512]{2,1,0:T(8,128)(2,1)S(1)}, u32[]{:S(2)}, u32[]{:S(2)}) collective-permute-start(bf16[9,32,512]{2,1,0:T(8,128)(2,1)S(1)} %get-tuple-element.342.refs_0_), channel_id=1, source_target_pairs={{0,2},{1,3},{2,0},{3,1},{4,6},{5,7},{6,4},{7,5},{8,10},{9,11},{10,... | collective-permute-start | bytes 884744 | tf_op jit(solution)/shard_map/ppermute | solution.py:75
  209.6 8.1 %collective-permute-start.29 = (bf16[4,64,512]{2,1,0:T(8,128)(2,1)S(1)}, bf16[4,64,512]{2,1,0:T(8,128)(2,1)S(1)}, u32[]{:S(2)}, u32[]{:S(2)}) collective-permute-start(bf16[4,64,512]{2,1,0:T(8,128)(2,1)S(1)} %get-tuple-element.328), channel_id=1, source_target_pairs={{0,8},{8,0},{16,24},{24,16},{1,9},{9,1},{17,25},{25,17},{2,10},{10... | collective-permute-start | bytes 786440 | tf_op jit(solution)/shard_map/ppermute | solution.py:75
  219.7 12.8 %collective-permute-start.33 = (bf16[2,4,64,512]{3,2,1,0:T(8,128)(2,1)S(1)}, bf16[2,4,64,512]{3,2,1,0:T(8,128)(2,1)S(1)}, u32[]{:S(2)}, u32[]{:S(2)}) collective-permute-start(bf16[2,4,64,512]{3,2,1,0:T(8,128)(2,1)S(1)} %get-tuple-element.350), channel_id=1, source_target_pairs={{0,8},{8,0},{16,24},{24,16},{1,9},{9,1},{17,25},{25,17},{2,10},{10... | collective-permute-start | bytes 1572872 | tf_op jit(solution)/shard_map/ppermute | solution.py:75
  220.3 10.4 %collective-permute-start.32 = (bf16[2,3,64,512]{3,2,1,0:T(8,128)(2,1)}, bf16[2,3,64,512]{3,2,1,0:T(8,128)(2,1)S(1)}, u32[]{:S(2)}, u32[]{:S(2)}) collective-permute-start(bf16[2,3,64,512]{3,2,1,0:T(8,128)(2,1)} %get-tuple-element.330), channel_id=1, source_target_pairs={{0,16},{8,24},{16,0},{24,8},{1,17},{9,25},{17,1},{25,9},{2,18},{10... | collective-permute-start | bytes 1179656 | tf_op jit(solution)/shard_map/ppermute | solution.py:75
  221.7 8.9 %collective-permute-start.34 = (bf16[9,32,512]{2,1,0:T(8,128)(2,1)}, bf16[9,32,512]{2,1,0:T(8,128)(2,1)S(1)}, u32[]{:S(2)}, u32[]{:S(2)}) collective-permute-start(bf16[9,32,512]{2,1,0:T(8,128)(2,1)} %get-tuple-element.355), channel_id=1, source_target_pairs={{0,2},{1,3},{2,0},{3,1},{4,6},{5,7},{6,4},{7,5},{8,10},{9,11},{10,... | collective-permute-start | bytes 884744 | tf_op jit(solution)/shard_map/ppermute | solution.py:75
  224.0 1.2 collective-permute-start.16
  225.8 3.6 %collective-permute-start.31 = (f32[1,1]{1,0:T(1,128)}, f32[1,1]{1,0:T(1,128)}, u32[]{:S(2)}, u32[]{:S(2)}) collective-permute-start(f32[1,1]{1,0:T(1,128)} %add.15), channel_id=1, source_target_pairs={{0,2},{1,3},{2,0},{3,1},{4,6},{5,7},{6,4},{7,5},{8,10},{9,11},{10,... | collective-permute-start | bytes 20 | tf_op jit(solution)/shard_map/ppermute | solution.py:75
  228.3 16.2 %collective-permute-start.37 = (bf16[9,32,512]{2,1,0:T(8,128)(2,1)S(1)}, bf16[9,32,512]{2,1,0:T(8,128)(2,1)S(1)}, u32[]{:S(2)}, u32[]{:S(2)}) collective-permute-start(bf16[9,32,512]{2,1,0:T(8,128)(2,1)S(1)} %get-tuple-element.364.refs_0_.refs_10_), channel_id=1, source_target_pairs={{0,4},{1,5},{2,6},{3,7},{4,0},{5,1},{6,2},{7,3},{8,12},{9,13},{10,... | collective-permute-start | bytes 884744 | tf_op jit(solution)/shard_map/ppermute | solution.py:75
  229.4 15.0 %collective-permute-start.36 = (bf16[9,32,512]{2,1,0:T(8,128)(2,1)S(1)}, bf16[9,32,512]{2,1,0:T(8,128)(2,1)S(1)}, u32[]{:S(2)}, u32[]{:S(2)}) collective-permute-start(bf16[9,32,512]{2,1,0:T(8,128)(2,1)S(1)} %get-tuple-element.364.refs_0_.refs_10_), channel_id=1, source_target_pairs={{0,1},{1,0},{2,3},{3,2},{4,5},{5,4},{6,7},{7,6},{8,9},{9,8},{10,11... | collective-permute-start | bytes 884744 | tf_op jit(solution)/shard_map/ppermute | solution.py:75
  233.6 10.9 %collective-permute-start.40 = (bf16[4,64,512]{2,1,0:T(8,128)(2,1)S(1)}, bf16[4,64,512]{2,1,0:T(8,128)(2,1)S(1)}, u32[]{:S(2)}, u32[]{:S(2)}) collective-permute-start(bf16[4,64,512]{2,1,0:T(8,128)(2,1)S(1)} %get-tuple-element.368), channel_id=1, source_target_pairs={{0,16},{8,24},{16,0},{24,8},{1,17},{9,25},{17,1},{25,9},{2,18},{10... | collective-permute-start | bytes 786440 | tf_op jit(solution)/shard_map/ppermute | solution.py:75
  234.7 9.8 %collective-permute-start.39 = (bf16[3,64,512]{2,1,0:T(8,128)(2,1)S(1)}, bf16[3,64,512]{2,1,0:T(8,128)(2,1)S(1)}, u32[]{:S(2)}, u32[]{:S(2)}) collective-permute-start(bf16[3,64,512]{2,1,0:T(8,128)(2,1)S(1)} %get-tuple-element.366), channel_id=1, source_target_pairs={{0,8},{8,0},{16,24},{24,16},{1,9},{9,1},{17,25},{25,17},{2,10},{10... | collective-permute-start | bytes 589832 | tf_op jit(solution)/shard_map/ppermute | solution.py:75
  235.7 8.0 %collective-permute-start.35 = (f32[1,1]{1,0:T(1,128)}, f32[1,1]{1,0:T(1,128)}, u32[]{:S(2)}, u32[]{:S(2)}) collective-permute-start(f32[1,1]{1,0:T(1,128)} %add.16), channel_id=1, source_target_pairs={{0,4},{1,5},{2,6},{3,7},{4,0},{5,1},{6,2},{7,3},{8,12},{9,13},{10,... | collective-permute-start | bytes 20 | tf_op jit(solution)/shard_map/ppermute | solution.py:75
  245.3 18.3 %collective-permute-start.41 = (bf16[7,64,512]{2,1,0:T(8,128)(2,1)S(1)}, bf16[7,64,512]{2,1,0:T(8,128)(2,1)S(1)}, u32[]{:S(2)}, u32[]{:S(2)}) collective-permute-start(bf16[7,64,512]{2,1,0:T(8,128)(2,1)S(1)} %sum_round.17.refs_0_), channel_id=1, source_target_pairs={{0,2},{1,3},{2,0},{3,1},{4,6},{5,7},{6,4},{7,5},{8,10},{9,11},{10,... | collective-permute-start | bytes 1376264 | tf_op jit(solution)/shard_map/ppermute | solution.py:75
  245.3 16.1 %collective-permute-start.42 = (bf16[9,32,512]{2,1,0:T(8,128)(2,1)S(1)}, bf16[9,32,512]{2,1,0:T(8,128)(2,1)S(1)}, u32[]{:S(2)}, u32[]{:S(2)}) collective-permute-start(bf16[9,32,512]{2,1,0:T(8,128)(2,1)S(1)} %get-tuple-element.375.refs_2_), channel_id=1, source_target_pairs={{0,4},{1,5},{2,6},{3,7},{4,0},{5,1},{6,2},{7,3},{8,12},{9,13},{10,... | collective-permute-start | bytes 884744 | tf_op jit(solution)/shard_map/ppermute | solution.py:75
  264.5 21.2 %collective-permute-start.46 = (bf16[7,64,512]{2,1,0:T(8,128)(2,1)S(1)}, bf16[7,64,512]{2,1,0:T(8,128)(2,1)S(1)}, u32[]{:S(2)}, u32[]{:S(2)}) collective-permute-start(bf16[7,64,512]{2,1,0:T(8,128)(2,1)S(1)} %get-tuple-element.381.refs_0_), channel_id=1, source_target_pairs={{0,4},{1,5},{2,6},{3,7},{4,0},{5,1},{6,2},{7,3},{8,12},{9,13},{10,... | collective-permute-start | bytes 1376264 | tf_op jit(solution)/shard_map/ppermute | solution.py:75
  265.7 15.2 %collective-permute-start.44 = (bf16[9,32,512]{2,1,0:T(8,128)(2,1)S(1)}, bf16[9,32,512]{2,1,0:T(8,128)(2,1)S(1)}, u32[]{:S(2)}, u32[]{:S(2)}) collective-permute-start(bf16[9,32,512]{2,1,0:T(8,128)(2,1)S(1)} %get-tuple-element.377.refs_4_.refs_6_), channel_id=1, source_target_pairs={{0,2},{1,3},{2,0},{3,1},{4,6},{5,7},{6,4},{7,5},{8,10},{9,11},{10,... | collective-permute-start | bytes 884744 | tf_op jit(solution)/shard_map/ppermute | solution.py:75
  265.7 15.2 %collective-permute-start.43 = (bf16[9,32,512]{2,1,0:T(8,128)(2,1)S(1)}, bf16[9,32,512]{2,1,0:T(8,128)(2,1)S(1)}, u32[]{:S(2)}, u32[]{:S(2)}) collective-permute-start(bf16[9,32,512]{2,1,0:T(8,128)(2,1)S(1)} %get-tuple-element.377.refs_4_.refs_6_), channel_id=1, source_target_pairs={{0,1},{1,0},{2,3},{3,2},{4,5},{5,4},{6,7},{7,6},{8,9},{9,8},{10,11... | collective-permute-start | bytes 884744 | tf_op jit(solution)/shard_map/ppermute | solution.py:75
  286.4 2.7 collective-permute-start.47
  286.5 2.2 collective-permute-start.38
  287.0 2.1 collective-permute-start.45
  289.8 4.4 %collective-permute-start.50 = (f32[1,2]{1,0:T(1,128)S(1)}, f32[1,2]{1,0:T(1,128)S(1)}, u32[]{:S(2)}, u32[]{:S(2)}) collective-permute-start(f32[1,2]{1,0:T(1,128)S(1)} %square_sum.1.refs_0_), channel_id=1, source_target_pairs={{0,24},{8,16},{16,8},{24,0},{1,25},{9,17},{17,9},{25,1},{2,26},{10... | collective-permute-start | bytes 32 | tf_op jit(solution)/shard_map/ppermute | solution.py:75
  291.2 3.5 %collective-permute-start.49 = (f32[1,2]{1,0:T(1,128)S(1)}, f32[1,2]{1,0:T(1,128)S(1)}, u32[]{:S(2)}, u32[]{:S(2)}) collective-permute-start(f32[1,2]{1,0:T(1,128)S(1)} %square_sum.1.refs_0_), channel_id=1, source_target_pairs={{0,16},{8,24},{16,0},{24,8},{1,17},{9,25},{17,1},{25,9},{2,18},{10... | collective-permute-start | bytes 32 | tf_op jit(solution)/shard_map/ppermute | solution.py:75
  291.9 3.5 %collective-permute-start.48 = (f32[1,2]{1,0:T(1,128)S(1)}, f32[1,2]{1,0:T(1,128)S(1)}, u32[]{:S(2)}, u32[]{:S(2)}) collective-permute-start(f32[1,2]{1,0:T(1,128)S(1)} %square_sum.1.refs_0_), channel_id=1, source_target_pairs={{0,8},{8,0},{16,24},{24,16},{1,9},{9,1},{17,25},{25,17},{2,10},{10... | collective-permute-start | bytes 32 | tf_op jit(solution)/shard_map/ppermute | solution.py:75
  (33 other events, 219.8 us)
